TPU v7x, 32 devices: a whole 2x2x4 slice. The times are simulated.
32 devices in a mesh: gx: 8 (over z, x), gy: 4 (over y, core).
Axes of the slice: x: 2, y: 2, z: 4, core: 2. Of those that a mesh axis runs over, the one named last changes fastest.
Arguments:
- control: float32 [75, 128, 1024], P(None, 'gy', 'gx'), may hold values from -6 to 6
- east_coeff: float32 [75, 128, 1024], P(None, 'gy', 'gx'), may hold values from 0.12 to 0.245
- north_coeff: float32 [75, 128, 1024], P(None, 'gy', 'gx'), may hold values from 0.12 to 0.245
- ocean_mask: int32 [75, 128, 1024], P(None, 'gy', 'gx'), may hold values 0 or 1
- corner_cells: int32 [4, 131072], P(None, ('gx', 'gy')), may hold values from 0 to 4095, as said below
- corner_weights: float32 [4, 131072], P(None, ('gx', 'gy')), may hold values from 0 to 1, as said below
- obs_value: float32 [75, 131072], P(None, ('gx', 'gy')), may hold values from -6 to 6
- obs_precision: float32 [75, 131072], P(None, ('gx', 'gy')), may hold values from 0.3 to 3
- slot_counts: int32 [32, 32], P(('gx', 'gy')), may hold values from 1 to 128, as said below
Outputs:
- gradient: float32 [75, 128, 1024], P(None, 'gy', 'gx')
- departures: float32 [75, 131072], P(None, ('gx', 'gy'))
Inputs may be any that keep to these rules, and one draw needn't show every extreme that they name: For each slot, corner_cells lists the cells (r, s), (r, s + 1), (r + 1, s), (r + 1, s + 1) of one grid cell with r < 31 and s < 127, numbered r * 128 + s in the holding device's tile, in that order. `corner_weights`: the four weights of a slot are the bilinear weights (1 - a)(1 - b), a(1 - b), (1 - a)b, ab of two fractions a, b in [0, 1]; they sum to 1. slot_counts[d, p] counts the live slots that device p holds for owner d; for every owner some device sends exactly 128 live slots.
All inputs are finite; a program needn't handle non-finite values. No bound on the sum of `ocean_mask` on one device may be relied on, other than what follows from the above.
Results may differ from a plain program's by a relative error of at most 0.00002.
Values sent between devices are 32-bit elements; how exact they have to be, the bound alone decides.
No kernel may reach another device: no remote copies, remote signals or barrier semaphores. Data moves between devices by JAX's collectives and lax.ppermute only.
A program may use at most 128 MiB of HBM per device.

v0:
```python
import functools

import jax
import jax.numpy as jnp
from jax import lax
from jax.experimental import pallas as pl
from jax.experimental.pallas import tpu as pltpu
from jax.sharding import PartitionSpec as P

F32, BF16 = jnp.float32, jnp.bfloat16
VMEM = pltpu.VMEM
STEPS = 4
LANES8 = 8
WHOLE = pl.BlockSpec(memory_space=pltpu.VMEM)


def split2(x):
    hi = x.astype(BF16)
    lo = (x - hi.astype(F32)).astype(BF16)
    return hi, lo

def hats(cells_ref, weights_ref, j0, n, rows, cols):
    c = cells_ref[0:1, pl.ds(j0, n)]
    w = weights_ref[:, pl.ds(j0, n)]
    r = c // cols
    s = c - r * cols
    east, west = w[1:2] + w[3:4], w[0:1] + w[2:3]
    north, south = w[2:3] + w[3:4], w[0:1] + w[1:2]
    return r, s, east, west, north, south

def hat(index, low, high, size):
    at = lax.broadcasted_iota(jnp.int32, (size, index.shape[1]), 0) - index
    return jnp.where(at == 0, low, jnp.where(at == 1, high, 0.0))

def gather_kernel(rows, lev, cols, nb, cells_ref, weights_ref, bg_ref, out_ref, bb, t0, t1, rr0, rr1):
    for r in range(rows):
        hi, lo = split2(bg_ref[r])
        bb[r * lev:(r + 1) * lev, 0:cols] = hi
        bb[r * lev:(r + 1) * lev, cols:2 * cols] = lo
    blk = 256
    def multiply(jb, t, rr):
        r, s, east, west, north, south = hats(cells_ref, weights_ref, pl.multiple_of(jb * blk, blk), blk, rows, cols)
        rr[...] = hat(r, south, north, rows)
        hi, lo = split2(hat(s, west, east, cols))
        left = bb[...]
        t[...] = (jnp.dot(left, jnp.concatenate([hi, hi], 0), preferred_element_type=F32)
                  + jnp.dot(left, jnp.concatenate([lo, lo], 0), preferred_element_type=F32))
    def reduce(jb, t, rr):
        acc = jnp.zeros((lev, blk), F32)
        for r in range(rows):
            acc = acc + t[r * lev:(r + 1) * lev, :] * rr[r:r + 1, :]
        out_ref[2 * jb] = acc[:, 0:128]
        out_ref[2 * jb + 1] = acc[:, 128:256]
    def step(i, _):
        multiply(2 * i, t0, rr0)
        multiply(2 * i + 1, t1, rr1)
        reduce(2 * i, t0, rr0)
        reduce(2 * i + 1, t1, rr1)
        return 0
    lax.fori_loop(0, nb // 2, step, 0)

def gather(cells, weights, bg, slots):
    rows, lev, cols = bg.shape
    nb = slots // 256
    return pl.pallas_call(functools.partial(gather_kernel, rows, lev, cols, nb),
        out_shape=jax.ShapeDtypeStruct((2 * nb, lev, 128), F32),
        in_specs=[pl.BlockSpec(memory_space=VMEM)] * 3,
        out_specs=pl.BlockSpec(memory_space=VMEM),
        scratch_shapes=[VMEM((rows * lev, 2 * cols), BF16), VMEM((rows * lev, 256), F32), VMEM((rows * lev, 256), F32), VMEM((rows, 256), F32), VMEM((rows, 256), F32)],
        compiler_params=params(20),
    )(cells, weights, bg)

def scatter_kernel(rows, lev, cols, nb, cells_ref, weights_ref, back_ref, out_ref, x, acc):
    blk = 256
    acc[...] = jnp.zeros_like(acc)
    def step(jb, _):
        r, s, east, west, north, south = hats(cells_ref, weights_ref, pl.multiple_of(jb * blk, blk), blk, rows, cols)
        hi, lo = split2(hat(s, west, east, cols))
        right = jnp.concatenate([hi, lo], 0)
        back = jnp.concatenate([back_ref[2 * jb], back_ref[2 * jb + 1]], 1)
        u_hi, u_lo = split2(back * south)
        v_hi, v_lo = split2(back * north)
        one = hat(r, 1.0, 0.0, rows + 1).astype(BF16)
        for q in range(rows):
            at = jnp.broadcast_to(one[q:q + 1, :], (lev, blk))
            if q:
                below = jnp.broadcast_to(one[q - 1:q, :], (lev, blk))
                x[q * lev:(q + 1) * lev, 0:blk] = u_hi * at + v_hi * below
                x[q * lev:(q + 1) * lev, blk:] = u_lo * at + v_lo * below
            else:
                x[0:lev, 0:blk] = u_hi * at
                x[0:lev, blk:] = u_lo * at
        acc[...] += lax.dot_general(x[...], jnp.concatenate([right, right], 1), (((1,), (1,)), ((), ())), preferred_element_type=F32)
        return 0
    lax.fori_loop(0, nb, step, 0)
    for r in range(rows):
        a = acc[r * lev:(r + 1) * lev, :]
        out_ref[r] = a[:, 0:cols] + a[:, cols:]

def scatter(cells, weights, back, rows, cols):
    n2, lev, _ = back.shape
    nb = n2 // 2
    return pl.pallas_call(functools.partial(scatter_kernel, rows, lev, cols, nb),
        out_shape=jax.ShapeDtypeStruct((rows, lev, cols), F32),
        in_specs=[pl.BlockSpec(memory_space=VMEM)] * 3,
        out_specs=pl.BlockSpec(memory_space=VMEM),
        scratch_shapes=[VMEM((rows * lev, 512), BF16), VMEM((rows * lev, 256), F32)],
        compiler_params=params(20),
    )(cells, weights, back)


def group_start(g, levels):
    start, last = LANES8 * g, levels - LANES8
    return min(start, last) if isinstance(g, int) else jnp.minimum(start, last)


def params(megabytes):
    return pltpu.CompilerParams(vmem_limit_bytes=megabytes * 2**20)


def lanes_of(g):
    return pl.ds(pl.multiple_of(LANES8 * g, LANES8), LANES8)


def stage_kernel(groups, levels, margin, control_ref, east_ref, north_ref, mask_ref, *outs):
    cols = control_ref.shape[2]
    refs = [ref.reshape(levels * LANES8, cols) for ref in (control_ref, east_ref, north_ref, mask_ref)]
    block, last = pl.program_id(0), pl.num_programs(0) - 1
    field_refs, top_ref, bottom_ref = outs[:4], outs[4], outs[5]
    def step(g, _):
        start = group_start(g, levels)
        for r in range(LANES8):
            where = pl.ds(start * LANES8 + r, LANES8, stride=LANES8)
            control, east, north, mask = (ref[where, :] for ref in refs)
            mask = mask.astype(F32)
            for ref, value in zip(field_refs, (mask * control, mask, east, north)):
                ref[r, lanes_of(g), :] = value
        return 0
    lax.fori_loop(0, groups, step, 0)
    @pl.when(block == 0)
    def _():
        for f in range(4):
            bottom_ref[f * margin:(f + 1) * margin] = field_refs[f][0:margin]
    @pl.when(block == last)
    def _():
        for f in range(4):
            top_ref[f * margin:(f + 1) * margin] = field_refs[f][LANES8 - margin:LANES8]


def stage(groups, margin, natural):
    levels, rows, cols = natural[0].shape
    depth = LANES8 * groups
    return pl.pallas_call(functools.partial(stage_kernel, groups, levels, margin),
        grid=(rows // LANES8,), name="stage",
        out_shape=[jax.ShapeDtypeStruct((rows, depth, cols), F32)] * 4 + [jax.ShapeDtypeStruct((4 * margin, depth, cols), F32)] * 2,
        in_specs=[pl.BlockSpec((levels, LANES8, cols), lambda i: (0, i, 0))] * 4,
        out_specs=[pl.BlockSpec((LANES8, depth, cols), lambda i: (i, 0, 0))] * 4 + [pl.BlockSpec((4 * margin, depth, cols), lambda i: (0, 0, 0))] * 2,
        compiler_params=params(16))(*natural)


def obs_kernel(levels, value_ref, precision_ref, live_ref, out_ref):
    def step(p, _):
        here = pl.ds(pl.multiple_of(p * 128, 128), 128)
        live = live_ref[0:1, here] > 0
        out_ref[p, 0:levels, :] = value_ref[:, here]
        out_ref[p, levels:2 * levels, :] = jnp.where(live, precision_ref[:, here], 0.0)
        return 0
    lax.fori_loop(0, out_ref.shape[0], step, 0)


def obs_blocks(value, precision, live):
    levels, slots = value.shape
    return pl.pallas_call(functools.partial(obs_kernel, levels), name="obs_blocks",
        out_shape=jax.ShapeDtypeStruct((slots // 128, -(-2 * levels // LANES8) * LANES8, 128), F32),
        in_specs=[WHOLE] * 3, out_specs=WHOLE, compiler_params=params(12))(value, precision, live)


def turn(x, shift):
    shift = shift % 128
    return pltpu.roll(x, shift, x.ndim - 1) if shift else x


def place(rows):
    lane = lax.broadcasted_iota(jnp.int32, (rows, LANES8, 128), 2)
    return lane, lane % (4 * STEPS)


def slabs_of(groups):
    slabs = -(-groups // 8)
    return slabs, -(-groups // slabs)


def pack_strip(load, groups, rows, margin):
    lane, _ = place(rows)
    width = 4 * margin
    west = east = jnp.zeros((rows, LANES8, 128), F32)
    for g in range(groups):
        x = load(g)
        here = (lane >= width * g) & (lane < width * (g + 1))
        west = jnp.where(here, turn(x, width * g + margin), west)
        east = jnp.where(here, turn(x, width * g + 2 * margin), east)
    return west, east


def pack_sends(strips, rows, margin):
    _, at = place(rows)
    to_east = to_west = jnp.zeros((rows, LANES8, 128), F32)
    for f, (west, east) in enumerate(strips):
        here = (at >= margin * f) & (at < margin * (f + 1))
        to_east = jnp.where(here, turn(east, margin * f - margin), to_east)
        to_west = jnp.where(here, turn(west, margin * f - margin), to_west)
    return to_east, to_west


def complete(f, west, east, from_west, from_east, rows, margin):
    _, at = place(rows)
    west = jnp.where(at < margin, turn(from_west, -margin * f), west)
    east = jnp.where(at >= 2 * margin, turn(from_east, 2 * margin - margin * f), east)
    return west, east


def slab_load(ref, at, count, slab, per, groups):
    return lambda g: ref[pl.ds(at, count), LANES8 * (slab * per + g):LANES8 * (slab * per + g + 1), :]


def strip_kernel(groups, rows, margin, *refs):
    fields, (south_in, north_in, strip_ref, to_east, to_west) = refs[:4], refs[4:]
    slabs, per = slabs_of(groups)
    def build(at, count, sources):
        for slab in range(slabs):
            strips = []
            for f in range(4):
                ref, start = sources[f]
                west, east = pack_strip(slab_load(ref, start, count, slab, per, groups), min(per, groups - slab * per), count, margin)
                strip_ref[f, 0, slab, pl.ds(at, count)] = west
                strip_ref[f, 1, slab, pl.ds(at, count)] = east
                strips.append((west, east))
            to_east[slab, pl.ds(at, count)], to_west[slab, pl.ds(at, count)] = pack_sends(strips, count, margin)
    def inside(i, _):
        build(2 * i + margin, 2, [(fields[f], 2 * i) for f in range(4)])
        return 0
    lax.fori_loop(0, rows // 2, inside, 0)
    def outside(i, _):
        build(2 * i, 2, [(south_in, f * margin + 2 * i) for f in range(4)])
        build(2 * i + margin + rows, 2, [(north_in, f * margin + 2 * i) for f in range(4)])
        return 0
    lax.fori_loop(0, margin // 2, outside, 0)


def strip_fields(groups, rows, margin, fields, south_in, north_in):
    tall = rows + 2 * margin
    slabs, _ = slabs_of(groups)
    return pl.pallas_call(functools.partial(strip_kernel, groups, rows, margin),
        out_shape=[jax.ShapeDtypeStruct((4, 2, slabs, tall, LANES8, 128), F32)] + [jax.ShapeDtypeStruct((slabs, tall, LANES8, 128), F32)] * 2,
        in_specs=[WHOLE] * 6, out_specs=[WHOLE] * 3, name="strip_fields", compiler_params=params(16))(*fields, south_in, north_in)


def faces_kernel(groups, rows, margin, mask_ref, east_ref, north_ref, south_in, north_in, e_out, n_out, mask):
    tall = rows + 2 * margin
    def step(g, _):
        put = lanes_of(g)
        mask[0:margin] = south_in[margin:2 * margin, put, :]
        mask[margin:margin + rows] = mask_ref[:, put, :]
        mask[margin + rows:tall] = north_in[margin:2 * margin, put, :]
        pieces = [(0, margin, south_in, 0), (margin + rows, margin, north_in, 0)] + [(margin + i, LANES8, None, i) for i in range(0, rows, LANES8)]
        for at, count, halo, i in pieces:
            if halo is None:
                east, north = east_ref[i:i + count, put, :], north_ref[i:i + count, put, :]
            else:
                east, north = halo[2 * margin:3 * margin, put, :], halo[3 * margin:4 * margin, put, :]
            own = mask[at:at + count]
            e_out[at:at + count, put, :] = east * own * turn(own, -1)
            n_out[at:at + count, put, :] = north * own * mask[at + 1:at + count + 1]
        return 0
    mask[tall] = jnp.zeros((LANES8, 128), F32)
    lax.fori_loop(0, groups, step, 0)


def faces(groups, rows, margin, fields, south_in, north_in):
    tall = rows + 2 * margin
    return pl.pallas_call(functools.partial(faces_kernel, groups, rows, margin),
        out_shape=[jax.ShapeDtypeStruct((tall, LANES8 * groups, 128), F32)] * 2,
        in_specs=[WHOLE] * 5, out_specs=[WHOLE] * 2, name="faces", scratch_shapes=[VMEM((tall + 1, LANES8, 128), F32)],
        compiler_params=params(12))(*fields[1:], south_in, north_in)


def sweep(source, east, north, write, low, high):
    for at in range(low, high, LANES8):
        end = min(at + LANES8, high)
        u = source(at - 1, end + 1)
        rise = north(at - 1, end) * (u[1:] - u[:-1])
        u = u[1:-1]
        run = east(at, end) * (turn(u, -1) - u)
        write(at, end, u + ((run - turn(run, 1)) + (rise[1:] - rise[:-1])))


def reader(ref, *lead):
    return lambda at, end: ref[(*lead, slice(at, end))]


def writer(ref, *lead):
    def write(at, end, value):
        ref[(*lead, slice(at, end))] = value
    return write


def all_sweeps(tall, margin, states, east, north, write):
    for k in range(margin):
        now, later = states[k % 2], states[(k + 1) % 2]
        sweep(reader(now), east, north, writer(later) if k + 1 < margin else write, k + 1, tall - 1 - k)


def strip_sweeps(rows, margin, strip_refs, faces_ref, rim):
    tall = rows + 2 * margin
    last = strip_refs[margin % 2]
    def step(slab, _):
        for side in range(2):
            states = [ref.at[side, slab] for ref in strip_refs]
            all_sweeps(tall, margin, states, reader(faces_ref, side, 0, slab), reader(faces_ref, side, 1, slab), writer(states[margin % 2]))
        for i in range(0, rows, LANES8):
            _, at = place(LANES8)
            here = slice(i + margin, i + margin + LANES8)
            rim[slab, i:i + LANES8] = jnp.where(at < margin, turn(last[1, slab, here], -margin), last[0, slab, here])
        return 0
    lax.fori_loop(0, rim.shape[0], step, 0)


def tile_sweeps(g, groups, rows, margin, states, e_ref, n_ref, rim, write):
    tall = rows + 2 * margin
    put = lanes_of(g)
    _, per = slabs_of(groups)
    slab = g // per
    shift = 128 - margin - 4 * margin * (g - slab * per)
    def finish(at, end, value):
        lane, _ = place(end - at)
        edge = pltpu.roll(rim[slab, at - margin:end - margin], shift, 2)
        write(at - margin, end - margin, jnp.where((lane < margin) | (lane >= 128 - margin), edge, value))
    all_sweeps(tall, margin, states, lambda a, b: e_ref[a:b, put, :], lambda a, b: n_ref[a:b, put, :], finish)


def fill(state, put, low, middle, high, margin, offset):
    rows = middle.shape[0]
    state[0:margin] = low[offset:offset + margin, put, :]
    state[margin:margin + rows] = middle[:, put, :]
    state[margin + rows:2 * margin + rows] = high[offset:offset + margin, put, :]


def forward_kernel(groups, rows, margin, u_ref, south_in, north_in, e_ref, n_ref, strip_ref, from_west, from_east, out_ref, faces_ref, strip_a, strip_b, mask, state_a, state_b, rim):
    tall = rows + 2 * margin
    def join(slab, _):
        for side in range(2):
            mask[side, tall] = jnp.zeros((LANES8, 128), F32)
        for at in range(0, tall, LANES8):
            here = slice(at, at + LANES8)
            for f in range(4):
                pair = complete(f, strip_ref[f, 0, slab, here], strip_ref[f, 1, slab, here], from_west[slab, here], from_east[slab, here], LANES8, margin)
                for side, value in enumerate(pair):
                    if f == 0:
                        strip_a[side, slab, here] = value
                    elif f == 1:
                        mask[side, here] = value
                    else:
                        faces_ref[side, f - 2, slab, here] = value
        for at in range(0, tall, LANES8):
            here = slice(at, at + LANES8)
            for side in range(2):
                own = mask[side, here]
                faces_ref[side, 0, slab, here] = faces_ref[side, 0, slab, here] * own * turn(own, -1)
                faces_ref[side, 1, slab, here] = faces_ref[side, 1, slab, here] * own * mask[side, at + 1:at + 1 + LANES8]
        return 0
    lax.fori_loop(0, rim.shape[0], join, 0)
    strip_sweeps(rows, margin, (strip_a, strip_b), faces_ref, rim)
    def step(g, _):
        put = lanes_of(g)
        fill(state_a, put, south_in, u_ref, north_in, margin, 0)
        def write(at, end, value):
            out_ref[at:end, put, :] = value
        tile_sweeps(g, groups, rows, margin, (state_a, state_b), e_ref, n_ref, rim, write)
        return 0
    lax.fori_loop(0, groups, step, 0)


def sweep_scratch(groups, rows, margin):
    tall = rows + 2 * margin
    slabs, _ = slabs_of(groups)
    return [VMEM((2, slabs, tall, LANES8, 128), F32)] * 2, [VMEM((tall, LANES8, 128), F32)] * 2 + [VMEM((slabs, rows, LANES8, 128), F32)]


def forward(groups, rows, margin, u, south_in, north_in, e, n, strip, from_west, from_east):
    tall = rows + 2 * margin
    slabs, _ = slabs_of(groups)
    strips, tiles = sweep_scratch(groups, rows, margin)
    return pl.pallas_call(functools.partial(forward_kernel, groups, rows, margin),
        out_shape=[jax.ShapeDtypeStruct((rows, LANES8 * groups, 128), F32), jax.ShapeDtypeStruct((2, 2, slabs, tall, LANES8, 128), F32)],
        in_specs=[WHOLE] * 8, out_specs=[WHOLE] * 2, name="forward",
        scratch_shapes=strips + [VMEM((2, tall + 1, LANES8, 128), F32)] + tiles,
        compiler_params=params(24))(u, south_in, north_in, e, n, strip, from_west, from_east)


def strip_adjoint_kernel(groups, rows, margin, adjoint_ref, south_in, north_in, strip_ref, to_east, to_west):
    quarter = (rows + 2 * margin) // 4
    slabs, per = slabs_of(groups)
    def build(ref, i, at):
        for slab in range(slabs):
            west, east = pack_strip(slab_load(ref, i, 2, slab, per, groups), min(per, groups - slab * per), 2, margin)
            strip_ref[0, slab, pl.ds(at, 2)] = west
            strip_ref[1, slab, pl.ds(at, 2)] = east
    for i in range(0, margin, 2):
        build(south_in, i, i)
        build(north_in, i, i + margin + rows)
    def inside(i, _):
        build(adjoint_ref, 2 * i, 2 * i + margin)
        return 0
    lax.fori_loop(0, rows // 2, inside, 0)
    for slab in range(slabs):
        for at in range(0, quarter, 2):
            here = [slice(at + q * quarter, at + q * quarter + 2) for q in range(4)]
            sends = pack_sends([(strip_ref[0, slab, s], strip_ref[1, slab, s]) for s in here], 2, margin)
            to_east[slab, at:at + 2], to_west[slab, at:at + 2] = sends


def strip_adjoint(groups, rows, margin, adjoint, south_in, north_in):
    tall = rows + 2 * margin
    slabs, _ = slabs_of(groups)
    return pl.pallas_call(functools.partial(strip_adjoint_kernel, groups, rows, margin),
        out_shape=[jax.ShapeDtypeStruct((2, slabs, tall, LANES8, 128), F32)] + [jax.ShapeDtypeStruct((slabs, tall // 4, LANES8, 128), F32)] * 2,
        in_specs=[WHOLE] * 3, out_specs=[WHOLE] * 3, name="strip_adjoint", compiler_params=params(12))(adjoint, south_in, north_in)


def backward_kernel(groups, levels, rows, margin, adjoint_ref, south_in, north_in, strip_ref, from_west, from_east, e_ref, n_ref, faces_ref, u_ref, mask_ref,
                    out_ref, strip_a, strip_b, state_a, state_b, rim):
    quarter = (rows + 2 * margin) // 4
    for slab in range(rim.shape[0]):
        for at in range(0, quarter, 2):
            for q in range(4):
                here = slice(at + q * quarter, at + q * quarter + 2)
                pair = complete(q, strip_ref[0, slab, here], strip_ref[1, slab, here], from_west[slab, at:at + 2], from_east[slab, at:at + 2], 2, margin)
                for side in range(2):
                    strip_a[side, slab, here] = pair[side]
    strip_sweeps(rows, margin, (strip_a, strip_b), faces_ref, rim)
    def step(g, _):
        put = lanes_of(g)
        start = group_start(g, levels)
        fill(state_a, put, south_in, adjoint_ref, north_in, margin, 0)
        def write(at, end, value):
            value = u_ref[at:end, put, :] + mask_ref[at:end, put, :] * value
            for r in range(at, end):
                out_ref[pl.ds(start * rows + r, LANES8, stride=rows), :] = value[r - at]
        tile_sweeps(g, groups, rows, margin, (state_a, state_b), e_ref, n_ref, rim, write)
        return 0
    lax.fori_loop(0, groups, step, 0)


def backward(groups, levels, rows, margin, *args):
    strips, tiles = sweep_scratch(groups, rows, margin)
    return pl.pallas_call(functools.partial(backward_kernel, groups, levels, rows, margin),
        out_shape=jax.ShapeDtypeStruct((levels * rows, 128), F32),
        in_specs=[WHOLE] * 11, out_specs=WHOLE, name="backward",
        scratch_shapes=strips + tiles, compiler_params=params(24))(*args)


def departures_kernel(groups, levels, equivalent_ref, obs_ref, out_ref, back_ref):
    def step(p, _):
        for g in range(groups):
            start = group_start(g, levels)
            here = slice(LANES8 * g, LANES8 * (g + 1))
            gap = obs_ref[p, levels + start:levels + start + LANES8, :] * (equivalent_ref[p, here, :] - obs_ref[p, start:start + LANES8, :])
            back_ref[p, here, :] = gap
            out_ref[p, start:start + LANES8, :] = gap
        return 0
    lax.fori_loop(0, out_ref.shape[0], step, 0, unroll=2)


def departures_of(groups, levels, equivalent, obs):
    return pl.pallas_call(functools.partial(departures_kernel, groups, levels),
        out_shape=[jax.ShapeDtypeStruct((equivalent.shape[0], levels, 128), F32), jax.ShapeDtypeStruct(equivalent.shape, F32)],
        in_specs=[WHOLE] * 2, out_specs=[WHOLE] * 2, name="departures", compiler_params=params(16))(equivalent, obs)


def exchange(values, share):
    blocks, levels, width = values.shape
    if share > 1:
        values = values.reshape(blocks, levels, share, -1).transpose(0, 2, 1, 3)
    values = values.reshape(blocks * share, levels, width // share)
    values = lax.all_to_all(values, ("gx", "gy"), 0, 0, tiled=True)
    if share > 1:
        values = values.reshape(blocks, share, levels, -1).transpose(0, 2, 1, 3)
    return values.reshape(blocks, levels, width)


def pass_along(axis, forth, back, cyclic):
    size = lax.axis_size(axis)
    up = [(i, (i + 1) % size) for i in range(size if cyclic else size - 1)]
    down = [(j, i) for i, j in up]
    return lax.ppermute(forth, axis, up), lax.ppermute(back, axis, down)


def body(
    control,
    east_coeff,
    north_coeff,
    ocean_mask,
    corner_cells,
    corner_weights,
    obs_value,
    obs_precision,
    slot_counts,
):
    levels, rows, cols = control.shape
    slots = corner_cells.shape[1]
    capacity = slots // lax.axis_size(("gx", "gy"))
    share = 128 // capacity
    margin = STEPS
    live = (slot_counts[0][:, None] > jnp.arange(capacity)[None, :]).astype(jnp.int32).reshape(1, slots)
    groups = -(-levels // 16) * 2
    obs = exchange(obs_blocks(obs_value, obs_precision, live), share)
    *fields, top, bottom = stage(groups, margin, (control, east_coeff, north_coeff, ocean_mask))
    south_in, north_in = pass_along("gy", top, bottom, False)
    strip, to_east, to_west = strip_fields(groups, rows, margin, fields, south_in, north_in)
    from_west, from_east = pass_along("gx", to_east, to_west, True)
    e, n = faces(groups, rows, margin, fields, south_in, north_in)
    background, strip_faces = forward(groups, rows, margin, fields[0], south_in, north_in, e, n, strip, from_west, from_east)
    equivalent = gather(corner_cells, corner_weights, background, slots)
    out, back = departures_of(groups, levels, equivalent, obs)
    departures = exchange(out, share).transpose(1, 0, 2).reshape(levels, slots)
    adjoint = scatter(corner_cells, corner_weights, back, rows, cols)
    south_in, north_in = pass_along("gy", adjoint[rows - margin:], adjoint[:margin], False)
    strip, to_east, to_west = strip_adjoint(groups, rows, margin, adjoint, south_in, north_in)
    from_west, from_east = pass_along("gx", to_east, to_west, True)
    gradient = backward(groups, levels, rows, margin, adjoint, south_in, north_in, strip, from_west, from_east, e, n, strip_faces, fields[0], fields[1])
    return gradient.reshape(levels, rows, cols), departures


def solution(mesh):
    return jax.shard_map(
        body,
        mesh=mesh,
        in_specs=(
            P(None, "gy", "gx"),
            P(None, "gy", "gx"),
            P(None, "gy", "gx"),
            P(None, "gy", "gx"),
            P(None, ("gx", "gy")),
            P(None, ("gx", "gy")),
            P(None, ("gx", "gy")),
            P(None, ("gx", "gy")),
            P(("gx", "gy"), None),
        ),
        out_specs=(P(None, "gy", "gx"), P(None, ("gx", "gy"))),
        check_vma=False,
    )
```

profile of v0, /device:TPU:1, one launch (start us, length us, event | category | flops | bytes accessed | tf_op | source)
XLA Modules:
  0.0 161.0 jit_solution(13787036417066669602)
XLA Ops:
  1.4 1.3 copy-done.6
  2.7 1.3 copy-done.7
  4.0 1.9 %obs_blocks.1 = f32[32,152,128]{2,1,0:T(8,128)} custom-call(f32[75,4096]{1,0:T(8,128)S(1)} %copy-done.6, f32[75,4096]{1,0:T(8,128)S(1)} %copy-done.7, s32[1,4096]{1,0:T(1,128)S(1)} %bitcast.7), custom_call_target="tpu_custom_call" | custom-call | tf_op jit(solution)/shard_map/obs_blocks/pallas_call | solution.py:173
  5.9 7.1 %all-to-all-start = ((f32[32,152,128]{2,1,0:T(8,128)}), f32[32,152,128]{2,1,0:T(8,128)}, u32[]{:S(2)}, u32[]{:S(2)}) async-start(f32[32,152,128]{2,1,0:T(8,128)} %obs_blocks.1), calls=%async_computation | async-start | bytes 4980736 | tf_op jit(solution)/shard_map/all_to_all | solution.py:485
  14.4 1.3 copy-done.14
  15.7 1.3 copy-done.15
  18.2 1.9 %stage.1 = (f32[32,80,128]{2,1,0:T(8,128)S(1)}, f32[32,80,128]{2,1,0:T(8,128)S(1)}, f32[32,80,128]{2,1,0:T(8,128)S(1)}, f32[32,80,128]{2,1,0:T(8,128)S(1)}, f32[...) custom-call(f32[75,32,128]{2,1,0:T(8,128)S(1)} %copy-done.13, f32[75,32,128]{2,1,0:T(8,128)S(1)} %copy-done.14, ...), custom_call_target="tpu_custom_call" | custom-call | tf_op jit(solution)/shard_map/stage/pallas_call | solution.py:153
  20.1 3.5 %collective-permute-start = (f32[16,80,128]{2,1,0:T(8,128)S(1)}, f32[16,80,128]{2,1,0:T(8,128)S(1)}, u32[]{:S(2)}, u32[]{:S(2)}) collective-permute-start(f32[16,80,128]{2,1,0:T(8,128)S(1)} %get-tuple-element.21), channel_id=1, source_target_pairs={{0,1},{1,2},{2,3},{4,5},{5,6},{6,7},{8,9},{9,10},{10,11},{12,13},{... | collective-permute-start | bytes 1966088 | tf_op jit(solution)/shard_map/ppermute | solution.py:495
  23.7 1.9 %collective-permute-start.1 = (f32[16,80,128]{2,1,0:T(8,128)S(1)}, f32[16,80,128]{2,1,0:T(8,128)S(1)}, u32[]{:S(2)}, u32[]{:S(2)}) collective-permute-start(f32[16,80,128]{2,1,0:T(8,128)S(1)} %get-tuple-element.22), channel_id=1, source_target_pairs={{1,0},{2,1},{3,2},{5,4},{6,5},{7,6},{9,8},{10,9},{11,10},{13,12},{... | collective-permute-start | bytes 1966088 | tf_op jit(solution)/shard_map/ppermute | solution.py:495
  25.6 16.6 %collective-permute-done.south_in.refs_4_ = f32[16,80,128]{2,1,0:T(8,128)S(1)} collective-permute-done((f32[16,80,128]{2,1,0:T(8,128)S(1)}, f32[16,80,128]{2,1,0:T(8,128)S(1)}, u32[]{:S(2)}, u32[]{:S(2)}) %collective-permute-start) | collective-permute-done | bytes 655392 | tf_op jit(solution)/shard_map/ppermute | solution.py:495
  42.2 2.8 %collective-permute-done.1.north_in.refs_5_ = f32[16,80,128]{2,1,0:T(8,128)S(1)} collective-permute-done((f32[16,80,128]{2,1,0:T(8,128)S(1)}, f32[16,80,128]{2,1,0:T(8,128)S(1)}, u32[]{:S(2)}, u32[]{:S(2)}) %collective-permute-start.1) | collective-permute-done | bytes 655392 | tf_op jit(solution)/shard_map/ppermute | solution.py:495
  45.0 7.1 %strip_fields.1 = (f32[4,2,2,40,8,128]{5,4,3,2,1,0:T(8,128)S(1)}, f32[2,40,8,128]{3,2,1,0:T(8,128)S(1)}, f32[2,40,8,128]{3,2,1,0:T(8,128)S(1)}) custom-call(f32[32,80,128]{2,1,0:T(8,128)S(1)} %get-tuple-element.20.refs_0_.u_ref, f32[32,80,128]{2,1,0:T(8,128)S(1)} %get-tuple-element.23.mask_ref.refs_1_, ...), custom_call_target="tpu_custom_call" | custom-call | tf_op jit(solution)/shard_map/strip_fields/pallas_call | solution.py:253
  52.1 1.6 %collective-permute-start.2 = (f32[2,40,8,128]{3,2,1,0:T(8,128)S(1)}, f32[2,40,8,128]{3,2,1,0:T(8,128)S(1)}, u32[]{:S(2)}, u32[]{:S(2)}) collective-permute-start(f32[2,40,8,128]{3,2,1,0:T(8,128)S(1)} %get-tuple-element.29), channel_id=1, source_target_pairs={{0,4},{4,8},{8,12},{12,16},{16,20},{20,24},{24,28},{28,0},{1,5},{5... | collective-permute-start | bytes 983048 | tf_op jit(solution)/shard_map/ppermute | solution.py:495
  53.7 2.6 %collective-permute-start.3 = (f32[2,40,8,128]{3,2,1,0:T(8,128)S(1)}, f32[2,40,8,128]{3,2,1,0:T(8,128)S(1)}, u32[]{:S(2)}, u32[]{:S(2)}) collective-permute-start(f32[2,40,8,128]{3,2,1,0:T(8,128)S(1)} %get-tuple-element.30), channel_id=1, source_target_pairs={{4,0},{8,4},{12,8},{16,12},{20,16},{24,20},{28,24},{0,28},{5,1},{9... | collective-permute-start | bytes 983048 | tf_op jit(solution)/shard_map/ppermute | solution.py:495
  57.4 7.7 %collective-permute-done.2.from_west = f32[2,40,8,128]{3,2,1,0:T(8,128)S(1)} collective-permute-done((f32[2,40,8,128]{3,2,1,0:T(8,128)S(1)}, f32[2,40,8,128]{3,2,1,0:T(8,128)S(1)}, u32[]{:S(2)}, u32[]{:S(2)}) %collective-permute-start.2) | collective-permute-done | bytes 327712 | tf_op jit(solution)/shard_map/ppermute | solution.py:495
  65.1 1.6 collective-permute-done.3.from_east
  66.7 9.3 %forward.1 = (f32[32,80,128]{2,1,0:T(8,128)S(1)}, f32[2,2,2,40,8,128]{5,4,3,2,1,0:T(8,128)S(1)}) custom-call(f32[32,80,128]{2,1,0:T(8,128)S(1)} %get-tuple-element.20.refs_0_.u_ref, f32[16,80,128]{2,1,0:T(8,128)S(1)} %collective-permute-done.south_in.refs_4_, f32[16,80,128]{2,1,0:T(8,128)S(1)} %collective-permute-done.1.north_in.refs_5_, ...), custom_call_target="tpu_custom_call" | custom-call | tf_op jit(solution)/shard_map/forward/pallas_call | solution.py:393
  77.2 13.1 %shard_map.104.equivalent_ref = f32[32,80,128]{2,1,0:T(8,128)S(1)} custom-call(s32[4,4096]{1,0:T(4,128)S(1)} %copy-done.17, f32[4,4096]{1,0:T(4,128)S(1)} %copy-done.18, f32[32,80,128]{2,1,0:T(8,128)S(1)} %get-tuple-element.31.bg_ref), custom_call_target="tpu_custom_call" | custom-call | tf_op jit(solution)/shard_map/pallas_call | solution.py:65
  91.3 1.3 copy-done.5
  92.6 2.0 %departures.1 = (f32[32,75,128]{2,1,0:T(8,128)S(1)}, f32[32,80,128]{2,1,0:T(8,128)S(1)}) custom-call(f32[32,80,128]{2,1,0:T(8,128)S(1)} %copy-done.5, f32[32,152,128]{2,1,0:T(8,128)} %all-to-all-done.obs_ref), custom_call_target="tpu_custom_call" | custom-call | tf_op jit(solution)/shard_map/departures/pallas_call | solution.py:475
  96.8 14.1 %all-to-all-start.1 = ((f32[32,75,128]{2,1,0:T(8,128)}), f32[32,75,128]{2,1,0:T(8,128)}, u32[]{:S(2)}, u32[]{:S(2)}) async-start(f32[32,75,128]{2,1,0:T(8,128)} %copy-done.8), calls=%async_computation.1 | async-start | bytes 2621440 | tf_op jit(solution)/shard_map/all_to_all | solution.py:485
  110.9 1.3 copy-done.10
  112.2 15.0 %shard_map.105.adjoint_ref = f32[32,80,128]{2,1,0:T(8,128)S(1)} custom-call(s32[4,4096]{1,0:T(4,128)S(1)} %copy-done.17, f32[4,4096]{1,0:T(4,128)S(1)} %copy-done.18, f32[32,80,128]{2,1,0:T(8,128)S(1)} %copy-done.10), custom_call_target="tpu_custom_call" | custom-call | tf_op jit(solution)/shard_map/pallas_call | solution.py:103
  127.2 3.7 %collective-permute-start.4 = (f32[4,80,128]{2,1,0:T(8,128)S(1)}, f32[4,80,128]{2,1,0:T(8,128)S(1)}, u32[]{:S(2)}, u32[]{:S(2)}) collective-permute-start(f32[4,80,128]{2,1,0:T(8,128)S(1)} %get-tuple-element.39), channel_id=1, source_target_pairs={{0,1},{1,2},{2,3},{4,5},{5,6},{6,7},{8,9},{9,10},{10,11},{12,13},{... | collective-permute-start | bytes 491528 | tf_op jit(solution)/shard_map/ppermute | solution.py:495
  130.9 1.9 %collective-permute-start.5 = (f32[4,80,128]{2,1,0:T(8,128)S(1)}, f32[4,80,128]{2,1,0:T(8,128)S(1)}, u32[]{:S(2)}, u32[]{:S(2)}) collective-permute-start(f32[4,80,128]{2,1,0:T(8,128)S(1)} %get-tuple-element.38), channel_id=1, source_target_pairs={{1,0},{2,1},{3,2},{5,4},{6,5},{7,6},{9,8},{10,9},{11,10},{13,12},{... | collective-permute-start | bytes 491528 | tf_op jit(solution)/shard_map/ppermute | solution.py:495
  133.2 5.5 %collective-permute-done.5.north_in = f32[4,80,128]{2,1,0:T(8,128)S(1)} collective-permute-done((f32[4,80,128]{2,1,0:T(8,128)S(1)}, f32[4,80,128]{2,1,0:T(8,128)S(1)}, u32[]{:S(2)}, u32[]{:S(2)}) %collective-permute-start.5) | collective-permute-done | bytes 163872 | tf_op jit(solution)/shard_map/ppermute | solution.py:495
  138.7 2.2 %strip_adjoint.1 = (f32[2,2,40,8,128]{4,3,2,1,0:T(8,128)S(1)}, f32[2,10,8,128]{3,2,1,0:T(8,128)S(1)}, f32[2,10,8,128]{3,2,1,0:T(8,128)S(1)}) custom-call(f32[32,80,128]{2,1,0:T(8,128)S(1)} %shard_map.105.adjoint_ref, f32[4,80,128]{2,1,0:T(8,128)S(1)} %collective-permute-done.4.south_in, f32[4,80,128]{2,1,0:T(8,128)S(1)} %collective-permute-done.5.north_in), custom_call_target="tpu_custom_call" | custom-call | tf_op jit(solution)/shard_map/strip_adjoint/pallas_call | solution.py:425
  141.0 4.3 %collective-permute-start.7 = (f32[2,10,8,128]{3,2,1,0:T(8,128)S(1)}, f32[2,10,8,128]{3,2,1,0:T(8,128)S(1)}, u32[]{:S(2)}, u32[]{:S(2)}) collective-permute-start(f32[2,10,8,128]{3,2,1,0:T(8,128)S(1)} %get-tuple-element.35), channel_id=1, source_target_pairs={{4,0},{8,4},{12,8},{16,12},{20,16},{24,20},{28,24},{0,28},{5,1},{9... | collective-permute-start | bytes 245768 | tf_op jit(solution)/shard_map/ppermute | solution.py:495
  145.2 1.8 %collective-permute-done.6.from_west = f32[2,10,8,128]{3,2,1,0:T(8,128)S(1)} collective-permute-done((f32[2,10,8,128]{3,2,1,0:T(8,128)S(1)}, f32[2,10,8,128]{3,2,1,0:T(8,128)S(1)}, u32[]{:S(2)}, u32[]{:S(2)}) %collective-permute-start.6) | collective-permute-done | bytes 81952 | tf_op jit(solution)/shard_map/ppermute | solution.py:495
  147.0 10.3 %backward.1 = f32[2400,128]{1,0:T(8,128)} custom-call(f32[32,80,128]{2,1,0:T(8,128)S(1)} %shard_map.105.adjoint_ref, f32[4,80,128]{2,1,0:T(8,128)S(1)} %collective-permute-done.4.south_in, f32[4,80,128]{2,1,0:T(8,128)S(1)} %collective-permute-done.5.north_in, f32[2,2,40,8,128]{4,3,2,1,0:T(8,128)S(1)} %get-tuple-element.33.strip_ref, ...), custom_call_target="tpu_custom_call" | custom-call | tf_op jit(solution)/shard_map/backward/pallas_call | solution.py:456
  157.3 1.7 %copy.11 = f32[75,32,128]{2,1,0:T(8,128)S(1)} copy(f32[75,32,128]{2,0,1:T(8,128)} %bitcast.3) | data formatting | bytes 2457600 | tf_op jit(solution)/shard_map/transpose | solution.py:525
  159.1 1.9 %copy.12 = f32[10,8,32,128]{3,1,2,0:T(8,128)} copy(f32[10,8,32,128]{3,2,1,0:T(8,128)S(1)} %bitcast.8) | data formatting | bytes 2621440
  (41 shorter events, 9.3 us)
Async XLA Ops:
  1.4 1.3 copy-start.6
  2.7 1.3 copy-start.7
  5.9 85.4 %all-to-all-start = ((f32[32,152,128]{2,1,0:T(8,128)}), f32[32,152,128]{2,1,0:T(8,128)}, u32[]{:S(2)}, u32[]{:S(2)}) async-start(f32[32,152,128]{2,1,0:T(8,128)} %obs_blocks.1), calls=%async_computation | async-start | bytes 4980736 | tf_op jit(solution)/shard_map/all_to_all | solution.py:485
  13.1 1.3 copy-start.13
  14.4 1.3 copy-start.14
  15.6 1.3 copy-start.15
  16.9 1.3 copy-start.16
  20.1 22.1 %collective-permute-start = (f32[16,80,128]{2,1,0:T(8,128)S(1)}, f32[16,80,128]{2,1,0:T(8,128)S(1)}, u32[]{:S(2)}, u32[]{:S(2)}) collective-permute-start(f32[16,80,128]{2,1,0:T(8,128)S(1)} %get-tuple-element.21), channel_id=1, source_target_pairs={{0,1},{1,2},{2,3},{4,5},{5,6},{6,7},{8,9},{9,10},{10,11},{12,13},{... | collective-permute-start | bytes 1966088 | tf_op jit(solution)/shard_map/ppermute | solution.py:495
  23.7 21.4 %collective-permute-start.1 = (f32[16,80,128]{2,1,0:T(8,128)S(1)}, f32[16,80,128]{2,1,0:T(8,128)S(1)}, u32[]{:S(2)}, u32[]{:S(2)}) collective-permute-start(f32[16,80,128]{2,1,0:T(8,128)S(1)} %get-tuple-element.22), channel_id=1, source_target_pairs={{1,0},{2,1},{3,2},{5,4},{6,5},{7,6},{9,8},{10,9},{11,10},{13,12},{... | collective-permute-start | bytes 1966088 | tf_op jit(solution)/shard_map/ppermute | solution.py:495
  52.1 13.0 %collective-permute-start.2 = (f32[2,40,8,128]{3,2,1,0:T(8,128)S(1)}, f32[2,40,8,128]{3,2,1,0:T(8,128)S(1)}, u32[]{:S(2)}, u32[]{:S(2)}) collective-permute-start(f32[2,40,8,128]{3,2,1,0:T(8,128)S(1)} %get-tuple-element.29), channel_id=1, source_target_pairs={{0,4},{4,8},{8,12},{12,16},{16,20},{20,24},{24,28},{28,0},{1,5},{5... | collective-permute-start | bytes 983048 | tf_op jit(solution)/shard_map/ppermute | solution.py:495
  53.7 13.0 %collective-permute-start.3 = (f32[2,40,8,128]{3,2,1,0:T(8,128)S(1)}, f32[2,40,8,128]{3,2,1,0:T(8,128)S(1)}, u32[]{:S(2)}, u32[]{:S(2)}) collective-permute-start(f32[2,40,8,128]{3,2,1,0:T(8,128)S(1)} %get-tuple-element.30), channel_id=1, source_target_pairs={{4,0},{8,4},{12,8},{16,12},{20,16},{24,20},{28,24},{0,28},{5,1},{9... | collective-permute-start | bytes 983048 | tf_op jit(solution)/shard_map/ppermute | solution.py:495
  57.4 18.6 %copy-start = (f32[40,80,128]{2,1,0:T(8,128)}, f32[40,80,128]{2,1,0:T(8,128)S(1)}, u32[]{:S(2)}) copy-start(f32[40,80,128]{2,1,0:T(8,128)S(1)} %get-tuple-element.26.e_ref) | copy-start | bytes 4915204
  57.4 18.6 %copy-start.2 = (f32[40,80,128]{2,1,0:T(8,128)}, f32[40,80,128]{2,1,0:T(8,128)S(1)}, u32[]{:S(2)}) copy-start(f32[40,80,128]{2,1,0:T(8,128)S(1)} %get-tuple-element.27.n_ref) | copy-start | bytes 4915204
  66.7 10.4 %copy-start.17 = (s32[4,4096]{1,0:T(4,128)S(1)}, s32[4,4096]{1,0:T(4,128)}, u32[]{:S(2)}) copy-start(s32[4,4096]{1,0:T(4,128)} %cells_ref.3) | copy-start | bytes 196612
  66.7 10.4 %copy-start.18 = (f32[4,4096]{1,0:T(4,128)S(1)}, f32[4,4096]{1,0:T(4,128)}, u32[]{:S(2)}) copy-start(f32[4,4096]{1,0:T(4,128)} %weights_ref.3) | copy-start | bytes 196612
  76.0 1.1 copy-start.11
  90.3 1.1 copy-start.4
  91.3 1.3 copy-start.5
  94.6 1.1 copy-start.8
  95.7 1.1 copy-start.9
  96.8 60.5 %all-to-all-start.1 = ((f32[32,75,128]{2,1,0:T(8,128)}), f32[32,75,128]{2,1,0:T(8,128)}, u32[]{:S(2)}, u32[]{:S(2)}) async-start(f32[32,75,128]{2,1,0:T(8,128)} %copy-done.8), calls=%async_computation.1 | async-start | bytes 2621440 | tf_op jit(solution)/shard_map/all_to_all | solution.py:485
  110.9 1.3 copy-start.10
  112.2 34.8 %copy-start.3 = (f32[40,80,128]{2,1,0:T(8,128)S(1)}, f32[40,80,128]{2,1,0:T(8,128)}, u32[]{:S(2)}) copy-start(f32[40,80,128]{2,1,0:T(8,128)} %copy-done.2) | copy-start | bytes 4915204
  112.2 34.8 %copy-start.12 = (f32[2,2,2,40,8,128]{5,4,3,2,1,0:T(8,128)S(1)}, f32[2,2,2,40,8,128]{5,4,3,2,1,0:T(8,128)}, u32[]{:S(2)}) copy-start(f32[2,2,2,40,8,128]{5,4,3,2,1,0:T(8,128)} %copy-done.11) | copy-start | bytes 3932164
  127.2 19.8 %copy-start.1 = (f32[40,80,128]{2,1,0:T(8,128)S(1)}, f32[40,80,128]{2,1,0:T(8,128)}, u32[]{:S(2)}) copy-start(f32[40,80,128]{2,1,0:T(8,128)} %copy-done) | copy-start | bytes 4915204
  127.2 5.9 %collective-permute-start.4 = (f32[4,80,128]{2,1,0:T(8,128)S(1)}, f32[4,80,128]{2,1,0:T(8,128)S(1)}, u32[]{:S(2)}, u32[]{:S(2)}) collective-permute-start(f32[4,80,128]{2,1,0:T(8,128)S(1)} %get-tuple-element.39), channel_id=1, source_target_pairs={{0,1},{1,2},{2,3},{4,5},{5,6},{6,7},{8,9},{9,10},{10,11},{12,13},{... | collective-permute-start | bytes 491528 | tf_op jit(solution)/shard_map/ppermute | solution.py:495
  130.9 7.7 %collective-permute-start.5 = (f32[4,80,128]{2,1,0:T(8,128)S(1)}, f32[4,80,128]{2,1,0:T(8,128)S(1)}, u32[]{:S(2)}, u32[]{:S(2)}) collective-permute-start(f32[4,80,128]{2,1,0:T(8,128)S(1)} %get-tuple-element.38), channel_id=1, source_target_pairs={{1,0},{2,1},{3,2},{5,4},{6,5},{7,6},{9,8},{10,9},{11,10},{13,12},{... | collective-permute-start | bytes 491528 | tf_op jit(solution)/shard_map/ppermute | solution.py:495
  140.9 6.2 %collective-permute-start.6 = (f32[2,10,8,128]{3,2,1,0:T(8,128)S(1)}, f32[2,10,8,128]{3,2,1,0:T(8,128)S(1)}, u32[]{:S(2)}, u32[]{:S(2)}) collective-permute-start(f32[2,10,8,128]{3,2,1,0:T(8,128)S(1)} %get-tuple-element.34), channel_id=1, source_target_pairs={{0,4},{4,8},{8,12},{12,16},{16,20},{20,24},{24,28},{28,0},{1,5},{5... | collective-permute-start | bytes 245768 | tf_op jit(solution)/shard_map/ppermute | solution.py:495
  141.0 6.0 %collective-permute-start.7 = (f32[2,10,8,128]{3,2,1,0:T(8,128)S(1)}, f32[2,10,8,128]{3,2,1,0:T(8,128)S(1)}, u32[]{:S(2)}, u32[]{:S(2)}) collective-permute-start(f32[2,10,8,128]{3,2,1,0:T(8,128)S(1)} %get-tuple-element.35), channel_id=1, source_target_pairs={{4,0},{8,4},{12,8},{16,12},{20,16},{24,20},{28,24},{0,28},{5,1},{9... | collective-permute-start | bytes 245768 | tf_op jit(solution)/shard_map/ppermute | solution.py:495
where the time goes:
time: 162 us; the launch traced here: 161 us
  Pallas kernels  63.9 us (39%)
  starting transfers between devices  40.9 us (25%)
  waiting for transfers between devices  36.3 us (22%)
  local copies, waits for them, and re-layouts  18.4 us (11%)
    ppermute x8, waiting for transfers between devices, pass_along(): return (lax.ppermute(forth, axis, up), lax.ppermute(back, axis, down))  36.3 us
    all_to_all x2, starting transfers between devices, exchange(): values = lax.all_to_all(values, ('gx', 'gy'), 0, 0, tiled=True)  21.2 us
    ppermute x8, starting transfers between devices, pass_along(): return (lax.ppermute(forth, axis, up), lax.ppermute(back, axis, down))  19.6 us
    unnamed x40, local copies, waits for them, and re-layouts  16.7 us
    pallas_call x1, Pallas kernels, scatter(): pl.pallas_call(functools.partial(scatter_kernel, rows, lev, cols, nb), ou...  15 us
    pallas_call x1, Pallas kernels, gather(): pl.pallas_call(functools.partial(gather_kernel, rows, lev, cols, nb), out...  13.1 us
    pallas_call x1, Pallas kernels, backward(): pl.pallas_call(functools.partial(backward_kernel, groups, levels, rows, m...  10.3 us
    pallas_call x1, Pallas kernels, forward(): pl.pallas_call(functools.partial(forward_kernel, groups, rows, margin), o...  9.31 us
  transfers between devices with their start and end apart: 10, of which 7 were waited for; matrix products, arithmetic and copies ran while one was open for 0% of the time, Pallas kernels for 37%

commit v1 on v0

--- a/solution.py
+++ b/solution.py
@@ -7,6 +7,7 @@
 from jax.experimental.pallas import tpu as pltpu
 from jax.sharding import PartitionSpec as P
 
+
 F32, BF16 = jnp.float32, jnp.bfloat16
 VMEM = pltpu.VMEM
 STEPS = 4
@@ -19,7 +20,8 @@
     lo = (x - hi.astype(F32)).astype(BF16)
     return hi, lo
 
-def hats(cells_ref, weights_ref, j0, n, rows, cols):
+
+def hats(cells_ref, weights_ref, j0, n, cols):
     c = cells_ref[0:1, pl.ds(j0, n)]
     w = weights_ref[:, pl.ds(j0, n)]
     r = c // cols
@@ -28,9 +30,11 @@
     north, south = w[2:3] + w[3:4], w[0:1] + w[1:2]
     return r, s, east, west, north, south
 
+
 def hat(index, low, high, size):
     at = lax.broadcasted_iota(jnp.int32, (size, index.shape[1]), 0) - index
     return jnp.where(at == 0, low, jnp.where(at == 1, high, 0.0))
+
 
 def gather_kernel(rows, lev, cols, nb, cells_ref, weights_ref, bg_ref, out_ref, bb, t0, t1, rr0, rr1):
     for r in range(rows):
@@ -39,7 +43,7 @@
         bb[r * lev:(r + 1) * lev, cols:2 * cols] = lo
     blk = 256
     def multiply(jb, t, rr):
-        r, s, east, west, north, south = hats(cells_ref, weights_ref, pl.multiple_of(jb * blk, blk), blk, rows, cols)
+        r, s, east, west, north, south = hats(cells_ref, weights_ref, pl.multiple_of(jb * blk, blk), blk, cols)
         rr[...] = hat(r, south, north, rows)
         hi, lo = split2(hat(s, west, east, cols))
         left = bb[...]
@@ -59,22 +63,24 @@
         return 0
     lax.fori_loop(0, nb // 2, step, 0)
 
+
 def gather(cells, weights, bg, slots):
     rows, lev, cols = bg.shape
     nb = slots // 256
     return pl.pallas_call(functools.partial(gather_kernel, rows, lev, cols, nb),
         out_shape=jax.ShapeDtypeStruct((2 * nb, lev, 128), F32),
         in_specs=[pl.BlockSpec(memory_space=VMEM)] * 3,
-        out_specs=pl.BlockSpec(memory_space=VMEM),
+        out_specs=pl.BlockSpec(memory_space=VMEM), name="gather",
         scratch_shapes=[VMEM((rows * lev, 2 * cols), BF16), VMEM((rows * lev, 256), F32), VMEM((rows * lev, 256), F32), VMEM((rows, 256), F32), VMEM((rows, 256), F32)],
         compiler_params=params(20),
     )(cells, weights, bg)
+
 
 def scatter_kernel(rows, lev, cols, nb, cells_ref, weights_ref, back_ref, out_ref, x, acc):
     blk = 256
     acc[...] = jnp.zeros_like(acc)
     def step(jb, _):
-        r, s, east, west, north, south = hats(cells_ref, weights_ref, pl.multiple_of(jb * blk, blk), blk, rows, cols)
+        r, s, east, west, north, south = hats(cells_ref, weights_ref, pl.multiple_of(jb * blk, blk), blk, cols)
         hi, lo = split2(hat(s, west, east, cols))
         right = jnp.concatenate([hi, lo], 0)
         back = jnp.concatenate([back_ref[2 * jb], back_ref[2 * jb + 1]], 1)
@@ -97,13 +103,14 @@
         a = acc[r * lev:(r + 1) * lev, :]
         out_ref[r] = a[:, 0:cols] + a[:, cols:]
 
+
 def scatter(cells, weights, back, rows, cols):
     n2, lev, _ = back.shape
     nb = n2 // 2
     return pl.pallas_call(functools.partial(scatter_kernel, rows, lev, cols, nb),
         out_shape=jax.ShapeDtypeStruct((rows, lev, cols), F32),
         in_specs=[pl.BlockSpec(memory_space=VMEM)] * 3,
-        out_specs=pl.BlockSpec(memory_space=VMEM),
+        out_specs=pl.BlockSpec(memory_space=VMEM), name="scatter",
         scratch_shapes=[VMEM((rows * lev, 512), BF16), VMEM((rows * lev, 256), F32)],
         compiler_params=params(20),
     )(cells, weights, back)
@@ -120,42 +127,6 @@
 
 def lanes_of(g):
     return pl.ds(pl.multiple_of(LANES8 * g, LANES8), LANES8)
-
-
-def stage_kernel(groups, levels, margin, control_ref, east_ref, north_ref, mask_ref, *outs):
-    cols = control_ref.shape[2]
-    refs = [ref.reshape(levels * LANES8, cols) for ref in (control_ref, east_ref, north_ref, mask_ref)]
-    block, last = pl.program_id(0), pl.num_programs(0) - 1
-    field_refs, top_ref, bottom_ref = outs[:4], outs[4], outs[5]
-    def step(g, _):
-        start = group_start(g, levels)
-        for r in range(LANES8):
-            where = pl.ds(start * LANES8 + r, LANES8, stride=LANES8)
-            control, east, north, mask = (ref[where, :] for ref in refs)
-            mask = mask.astype(F32)
-            for ref, value in zip(field_refs, (mask * control, mask, east, north)):
-                ref[r, lanes_of(g), :] = value
-        return 0
-    lax.fori_loop(0, groups, step, 0)
-    @pl.when(block == 0)
-    def _():
-        for f in range(4):
-            bottom_ref[f * margin:(f + 1) * margin] = field_refs[f][0:margin]
-    @pl.when(block == last)
-    def _():
-        for f in range(4):
-            top_ref[f * margin:(f + 1) * margin] = field_refs[f][LANES8 - margin:LANES8]
-
-
-def stage(groups, margin, natural):
-    levels, rows, cols = natural[0].shape
-    depth = LANES8 * groups
-    return pl.pallas_call(functools.partial(stage_kernel, groups, levels, margin),
-        grid=(rows // LANES8,), name="stage",
-        out_shape=[jax.ShapeDtypeStruct((rows, depth, cols), F32)] * 4 + [jax.ShapeDtypeStruct((4 * margin, depth, cols), F32)] * 2,
-        in_specs=[pl.BlockSpec((levels, LANES8, cols), lambda i: (0, i, 0))] * 4,
-        out_specs=[pl.BlockSpec((LANES8, depth, cols), lambda i: (i, 0, 0))] * 4 + [pl.BlockSpec((4 * margin, depth, cols), lambda i: (0, 0, 0))] * 2,
-        compiler_params=params(16))(*natural)
 
 
 def obs_kernel(levels, value_ref, precision_ref, live_ref, out_ref):
@@ -219,40 +190,107 @@
     return west, east
 
 
-def slab_load(ref, at, count, slab, per, groups):
+def slab_load(ref, at, count, slab, per):
     return lambda g: ref[pl.ds(at, count), LANES8 * (slab * per + g):LANES8 * (slab * per + g + 1), :]
 
 
-def strip_kernel(groups, rows, margin, *refs):
-    fields, (south_in, north_in, strip_ref, to_east, to_west) = refs[:4], refs[4:]
+def stage_kernel(groups, levels, margin, control_ref, east_ref, north_ref, mask_ref, *outs):
+    cols = control_ref.shape[2]
+    refs = [ref.reshape(levels * LANES8, cols) for ref in (control_ref, east_ref, north_ref, mask_ref)]
+    block, last = pl.program_id(0), pl.num_programs(0) - 1
+    field_refs, (top_ref, bottom_ref, strip_ref) = outs[:4], outs[4:]
+    def step(g, _):
+        start = group_start(g, levels)
+        for r in range(LANES8):
+            where = pl.ds(start * LANES8 + r, LANES8, stride=LANES8)
+            control, east, north, mask = (ref[where, :] for ref in refs)
+            mask = mask.astype(F32)
+            for ref, value in zip(field_refs, (mask * control, mask, east, north)):
+                ref[r, lanes_of(g), :] = value
+        return 0
+    lax.fori_loop(0, groups, step, 0)
     slabs, per = slabs_of(groups)
-    def build(at, count, sources):
+    count = 2
+    def pack(i, _):
+        at = count * i
         for slab in range(slabs):
-            strips = []
             for f in range(4):
-                ref, start = sources[f]
-                west, east = pack_strip(slab_load(ref, start, count, slab, per, groups), min(per, groups - slab * per), count, margin)
+                west, east = pack_strip(slab_load(field_refs[f], at, count, slab, per), min(per, groups - slab * per), count, margin)
                 strip_ref[f, 0, slab, pl.ds(at, count)] = west
                 strip_ref[f, 1, slab, pl.ds(at, count)] = east
-                strips.append((west, east))
-            to_east[slab, pl.ds(at, count)], to_west[slab, pl.ds(at, count)] = pack_sends(strips, count, margin)
-    def inside(i, _):
-        build(2 * i + margin, 2, [(fields[f], 2 * i) for f in range(4)])
-        return 0
-    lax.fori_loop(0, rows // 2, inside, 0)
-    def outside(i, _):
-        build(2 * i, 2, [(south_in, f * margin + 2 * i) for f in range(4)])
-        build(2 * i + margin + rows, 2, [(north_in, f * margin + 2 * i) for f in range(4)])
-        return 0
-    lax.fori_loop(0, margin // 2, outside, 0)
-
-
-def strip_fields(groups, rows, margin, fields, south_in, north_in):
-    tall = rows + 2 * margin
+        return 0
+    lax.fori_loop(0, LANES8 // count, pack, 0)
+    @pl.when(block == 0)
+    def _():
+        for f in range(4):
+            bottom_ref[f * margin:(f + 1) * margin] = field_refs[f][0:margin]
+    @pl.when(block == last)
+    def _():
+        for f in range(4):
+            top_ref[f * margin:(f + 1) * margin] = field_refs[f][LANES8 - margin:LANES8]
+
+
+def stage(groups, margin, natural):
+    levels, rows, cols = natural[0].shape
+    depth = LANES8 * groups
     slabs, _ = slabs_of(groups)
-    return pl.pallas_call(functools.partial(strip_kernel, groups, rows, margin),
-        out_shape=[jax.ShapeDtypeStruct((4, 2, slabs, tall, LANES8, 128), F32)] + [jax.ShapeDtypeStruct((slabs, tall, LANES8, 128), F32)] * 2,
-        in_specs=[WHOLE] * 6, out_specs=[WHOLE] * 3, name="strip_fields", compiler_params=params(16))(*fields, south_in, north_in)
+    natural = [pltpu.with_memory_space_constraint(x, pltpu.HBM) for x in natural]
+    return pl.pallas_call(functools.partial(stage_kernel, groups, levels, margin),
+        grid=(rows // LANES8,), name="stage",
+        out_shape=[jax.ShapeDtypeStruct((rows, depth, cols), F32)] * 4 + [jax.ShapeDtypeStruct((4 * margin, depth, cols), F32)] * 2
+        + [jax.ShapeDtypeStruct((4, 2, slabs, rows, LANES8, 128), F32)],
+        in_specs=[pl.BlockSpec((levels, LANES8, cols), lambda i: (0, i, 0))] * 4,
+        out_specs=[pl.BlockSpec((LANES8, depth, cols), lambda i: (i, 0, 0))] * 4 + [pl.BlockSpec((4 * margin, depth, cols), lambda i: (0, 0, 0))] * 2
+        + [pl.BlockSpec((4, 2, slabs, LANES8, LANES8, 128), lambda i: (0, 0, 0, i, 0, 0))],
+        compiler_params=params(16))(*natural)
+
+
+def sends_kernel(groups, levels, margin, control_ref, east_ref, north_ref, mask_ref, to_east, to_west):
+    cols = control_ref.shape[2]
+    refs = [ref.reshape(levels * LANES8, cols) for ref in (control_ref, east_ref, north_ref, mask_ref)]
+    slabs, per = slabs_of(groups)
+    quad = lax.broadcasted_iota(jnp.int32, (LANES8, 128), 1) // margin
+    for r in range(LANES8):
+        for slab in range(slabs):
+            east_out = west_out = jnp.zeros((LANES8, 128), F32)
+            for g in range(min(per, groups - slab * per)):
+                where = pl.ds(group_start(slab * per + g, levels) * LANES8 + r, LANES8, stride=LANES8)
+                control, east, north, mask = (ref[where, :] for ref in refs)
+                mask = mask.astype(F32)
+                for f, x in enumerate((mask * control, mask, east, north)):
+                    here = quad == 4 * g + f
+                    east_out = jnp.where(here, turn(x, margin * (4 * g + f + 1) - cols), east_out)
+                    west_out = jnp.where(here, turn(x, margin * (4 * g + f)), west_out)
+            to_east[slab, r] = east_out
+            to_west[slab, r] = west_out
+
+
+def lon_sends(groups, margin, natural):
+    levels, rows, cols = natural[0].shape
+    slabs, _ = slabs_of(groups)
+    natural = [pltpu.with_memory_space_constraint(x, pltpu.HBM) for x in natural]
+    return pl.pallas_call(functools.partial(sends_kernel, groups, levels, margin), grid=(rows // LANES8,), name="lon_sends",
+        out_shape=[jax.ShapeDtypeStruct((slabs, rows, LANES8, 128), F32)] * 2,
+        in_specs=[pl.BlockSpec((levels, LANES8, cols), lambda i: (0, i, 0))] * 4,
+        out_specs=[pl.BlockSpec((slabs, LANES8, LANES8, 128), lambda i: (0, i, 0, 0))] * 2,
+        compiler_params=params(16))(*natural)
+
+
+def rim_kernel(groups, margin, south_in, north_in, strip_ref):
+    slabs, per = slabs_of(groups)
+    for slab in range(slabs):
+        for f in range(4):
+            for end, ref in enumerate((south_in, north_in)):
+                west, east = pack_strip(slab_load(ref, f * margin, margin, slab, per), min(per, groups - slab * per), margin, margin)
+                strip_ref[f, 0, slab, end * margin:(end + 1) * margin] = west
+                strip_ref[f, 1, slab, end * margin:(end + 1) * margin] = east
+
+
+def strip_rims(groups, margin, south_in, north_in):
+    slabs, _ = slabs_of(groups)
+    return pl.pallas_call(functools.partial(rim_kernel, groups, margin),
+        out_shape=jax.ShapeDtypeStruct((4, 2, slabs, 2 * margin, LANES8, 128), F32),
+        in_specs=[WHOLE] * 2, out_specs=WHOLE, name="strip_rims", compiler_params=params(12))(south_in, north_in)
 
 
 def faces_kernel(groups, rows, margin, mask_ref, east_ref, north_ref, south_in, north_in, e_out, n_out, mask):
@@ -345,15 +383,18 @@
     state[margin + rows:2 * margin + rows] = high[offset:offset + margin, put, :]
 
 
-def forward_kernel(groups, rows, margin, u_ref, south_in, north_in, e_ref, n_ref, strip_ref, from_west, from_east, out_ref, faces_ref, strip_a, strip_b, mask, state_a, state_b, rim):
+def forward_kernel(groups, rows, margin, u_ref, south_in, north_in, e_ref, n_ref, strip_ref, from_west, from_east, rims_ref, south_corners, north_corners, out_ref, faces_ref, strip_a, strip_b, mask, state_a, state_b, rim):
     tall = rows + 2 * margin
     def join(slab, _):
         for side in range(2):
             mask[side, tall] = jnp.zeros((LANES8, 128), F32)
-        for at in range(0, tall, LANES8):
-            here = slice(at, at + LANES8)
+        pieces = [(0, margin, rims_ref, 0, south_corners.at[0, slab], south_corners.at[1, slab], 0),
+                  (margin + rows, margin, rims_ref, margin, north_corners.at[0, slab], north_corners.at[1, slab], 0)]
+        pieces += [(margin + i, LANES8, strip_ref, i, from_west.at[slab], from_east.at[slab], i) for i in range(0, rows, LANES8)]
+        for at, count, own_ref, own_at, west_ref, east_ref, in_at in pieces:
+            here, there, source = slice(at, at + count), slice(own_at, own_at + count), slice(in_at, in_at + count)
             for f in range(4):
-                pair = complete(f, strip_ref[f, 0, slab, here], strip_ref[f, 1, slab, here], from_west[slab, here], from_east[slab, here], LANES8, margin)
+                pair = complete(f, own_ref[f, 0, slab, there], own_ref[f, 1, slab, there], west_ref[source], east_ref[source], count, margin)
                 for side, value in enumerate(pair):
                     if f == 0:
                         strip_a[side, slab, here] = value
@@ -386,15 +427,15 @@
     return [VMEM((2, slabs, tall, LANES8, 128), F32)] * 2, [VMEM((tall, LANES8, 128), F32)] * 2 + [VMEM((slabs, rows, LANES8, 128), F32)]
 
 
-def forward(groups, rows, margin, u, south_in, north_in, e, n, strip, from_west, from_east):
+def forward(groups, rows, margin, *args):
     tall = rows + 2 * margin
     slabs, _ = slabs_of(groups)
     strips, tiles = sweep_scratch(groups, rows, margin)
     return pl.pallas_call(functools.partial(forward_kernel, groups, rows, margin),
         out_shape=[jax.ShapeDtypeStruct((rows, LANES8 * groups, 128), F32), jax.ShapeDtypeStruct((2, 2, slabs, tall, LANES8, 128), F32)],
-        in_specs=[WHOLE] * 8, out_specs=[WHOLE] * 2, name="forward",
+        in_specs=[WHOLE] * 11, out_specs=[WHOLE] * 2, name="forward",
         scratch_shapes=strips + [VMEM((2, tall + 1, LANES8, 128), F32)] + tiles,
-        compiler_params=params(24))(u, south_in, north_in, e, n, strip, from_west, from_east)
+        compiler_params=params(24))(*args)
 
 
 def strip_adjoint_kernel(groups, rows, margin, adjoint_ref, south_in, north_in, strip_ref, to_east, to_west):
@@ -402,7 +443,7 @@
     slabs, per = slabs_of(groups)
     def build(ref, i, at):
         for slab in range(slabs):
-            west, east = pack_strip(slab_load(ref, i, 2, slab, per, groups), min(per, groups - slab * per), 2, margin)
+            west, east = pack_strip(slab_load(ref, i, 2, slab, per), min(per, groups - slab * per), 2, margin)
             strip_ref[0, slab, pl.ds(at, 2)] = west
             strip_ref[1, slab, pl.ds(at, 2)] = east
     for i in range(0, margin, 2):
@@ -477,6 +518,20 @@
         in_specs=[WHOLE] * 2, out_specs=[WHOLE] * 2, name="departures", compiler_params=params(16))(equivalent, obs)
 
 
+def place_kernel(part_ref, out_ref):
+    def step(p, _):
+        out_ref[:, pl.ds(pl.multiple_of(p * 128, 128), 128)] = part_ref[p]
+        return 0
+    lax.fori_loop(0, part_ref.shape[0], step, 0, unroll=2)
+
+
+def place_departures(part):
+    blocks, levels, width = part.shape
+    return pl.pallas_call(place_kernel, name="place_departures",
+        out_shape=jax.ShapeDtypeStruct((levels, blocks * width), F32),
+        in_specs=[WHOLE], out_specs=WHOLE, compiler_params=params(12))(part)
+
+
 def exchange(values, share):
     blocks, levels, width = values.shape
     if share > 1:
@@ -488,11 +543,18 @@
     return values.reshape(blocks, levels, width)
 
 
-def pass_along(axis, forth, back, cyclic):
+def pass_around(axis, forth, back):
     size = lax.axis_size(axis)
-    up = [(i, (i + 1) % size) for i in range(size if cyclic else size - 1)]
-    down = [(j, i) for i, j in up]
-    return lax.ppermute(forth, axis, up), lax.ppermute(back, axis, down)
+    up = [(i, (i + 1) % size) for i in range(size)]
+    return lax.ppermute(forth, axis, up), lax.ppermute(back, axis, [(j, i) for i, j in up])
+
+
+def swap_edges(axis, forth, back):
+    size, odd = lax.axis_size(axis), lax.axis_index(axis) % 2 == 1
+    rounds = [[pair for i in range(first, size - 1, 2) for pair in ((i, i + 1), (i + 1, i))] for first in range(2)]
+    inner = lax.ppermute(jnp.where(odd, back, forth), axis, rounds[0])
+    outer = lax.ppermute(jnp.where(odd, forth, back), axis, rounds[1])
+    return jnp.where(odd, inner, outer), jnp.where(odd, outer, inner)
 
 
 def body(
@@ -513,20 +575,27 @@
     margin = STEPS
     live = (slot_counts[0][:, None] > jnp.arange(capacity)[None, :]).astype(jnp.int32).reshape(1, slots)
     groups = -(-levels // 16) * 2
-    obs = exchange(obs_blocks(obs_value, obs_precision, live), share)
-    *fields, top, bottom = stage(groups, margin, (control, east_coeff, north_coeff, ocean_mask))
-    south_in, north_in = pass_along("gy", top, bottom, False)
-    strip, to_east, to_west = strip_fields(groups, rows, margin, fields, south_in, north_in)
-    from_west, from_east = pass_along("gx", to_east, to_west, True)
+    natural = (control, east_coeff, north_coeff, ocean_mask)
+    to_east, to_west = lon_sends(groups, margin, natural)
+    from_west, from_east = pass_around("gx", to_east, to_west)
+    obs = obs_blocks(obs_value, obs_precision, live)
+    obs, *_ = lax.optimization_barrier((obs, to_east, to_west))
+    obs = exchange(obs, share)
+    *fields, top, bottom, strip = stage(groups, margin, natural)
+    south_in, north_in = swap_edges("gy", top, bottom)
+    corners = jnp.stack([from_west, from_east])
+    south_corners, north_corners = swap_edges("gy", corners[:, :, rows - margin:], corners[:, :, :margin])
+    rims = strip_rims(groups, margin, south_in, north_in)
     e, n = faces(groups, rows, margin, fields, south_in, north_in)
-    background, strip_faces = forward(groups, rows, margin, fields[0], south_in, north_in, e, n, strip, from_west, from_east)
+    background, strip_faces = forward(groups, rows, margin, fields[0], south_in, north_in, e, n, strip, from_west, from_east, rims, south_corners, north_corners)
     equivalent = gather(corner_cells, corner_weights, background, slots)
     out, back = departures_of(groups, levels, equivalent, obs)
-    departures = exchange(out, share).transpose(1, 0, 2).reshape(levels, slots)
+    sent = exchange(out, share)
     adjoint = scatter(corner_cells, corner_weights, back, rows, cols)
-    south_in, north_in = pass_along("gy", adjoint[rows - margin:], adjoint[:margin], False)
+    south_in, north_in = swap_edges("gy", adjoint[rows - margin:], adjoint[:margin])
     strip, to_east, to_west = strip_adjoint(groups, rows, margin, adjoint, south_in, north_in)
-    from_west, from_east = pass_along("gx", to_east, to_west, True)
+    from_west, from_east = pass_around("gx", to_east, to_west)
+    departures = place_departures(sent)
     gradient = backward(groups, levels, rows, margin, adjoint, south_in, north_in, strip, from_west, from_east, e, n, strip_faces, fields[0], fields[1])
     return gradient.reshape(levels, rows, cols), departures
 

time: 162 us -> 168 us (1.037)
  Pallas kernels: 63.9 us -> 66.4 us
  starting transfers between devices: 40.9 us -> 43 us
  local copies, waits for them, and re-layouts: 18.4 us -> 20.4 us
  waiting for transfers between devices: 36.3 us -> 34.4 us
    pallas_call x1, Pallas kernels: 1.9 us -> 6.49 us  [stage(): pl.pallas_call(functools.partial(stage_kernel, groups, levels, margin), g...]
    unnamed x40 -> x58, local copies, waits for them, and re-layouts: 16.7 us -> 20.4 us
    ppermute x8 -> x10, waiting for transfers between devices: 36.3 us -> 34.4 us  [the longest x2 28.8 us: pass_around(): lax.ppermute(forth, axis, up)]
    ppermute x8 -> x10, starting transfers between devices: 19.6 us -> 21.4 us  [the longest x3 10.6 us: swap_edges(): outer = lax.ppermute(jnp.where(odd, forth, back), axis, rounds[1])]
    transpose x1 -> x0, local copies, waits for them, and re-layouts: 1.71 us -> none  [body(): departures = exchange(out, share).transpose(1, 0, 2).reshape(levels, slots)]
    pallas_call x1, Pallas kernels: 2 us -> 0.3 us  [departures_of(): pl.pallas_call(functools.partial(departures_kernel, groups, levels), out_...]
    pallas_call x1 -> x3, Pallas kernels: 7.09 us -> 6.79 us  [the longest x1 4.87 us: lon_sends(): pl.pallas_call(functools.partial(sends_kernel, groups, levels, margin), g...]
  transfers between devices with their start and end apart: 10 -> 12, of which waited for: 7 -> 4; matrix products, arithmetic and copies ran while one was open for 0% -> 1% of each run, Pallas kernels for 37% -> 35%
where the time goes in v1:
time: 168 us
  Pallas kernels  66.4 us (40%)
  starting transfers between devices  43 us (26%)
  waiting for transfers between devices  34.4 us (20%)
  local copies, waits for them, and re-layouts  20.4 us (12%)
  other arithmetic  2.27 us (1%)
    ppermute x2, waiting for transfers between devices, pass_around(): lax.ppermute(forth, axis, up)  28.8 us
    all_to_all x2, starting transfers between devices, exchange(): values = lax.all_to_all(values, ('gx', 'gy'), 0, 0, tiled=True)  21.6 us
    unnamed x58, local copies, waits for them, and re-layouts  20.4 us
    pallas_call x1, Pallas kernels, scatter(): pl.pallas_call(functools.partial(scatter_kernel, rows, lev, cols, nb), ou...  15 us
    pallas_call x1, Pallas kernels, gather(): pl.pallas_call(functools.partial(gather_kernel, rows, lev, cols, nb), out...  13.1 us
    ppermute x3, starting transfers between devices, swap_edges(): outer = lax.ppermute(jnp.where(odd, forth, back), axis, rounds[1])  10.6 us
    pallas_call x1, Pallas kernels, backward(): pl.pallas_call(functools.partial(backward_kernel, groups, levels, rows, m...  10.3 us
    pallas_call x1, Pallas kernels, forward(): pl.pallas_call(functools.partial(forward_kernel, groups, rows, margin), o...  9.31 us
  transfers between devices with their start and end apart: 12, of which 4 were waited for; matrix products, arithmetic and copies ran while one was open for 1% of the time, Pallas kernels for 35%

profile of v1, /device:TPU:1, one launch (start us, length us, event | category | flops | bytes accessed | tf_op | source)
XLA Modules:
  0.0 167.6 jit_solution(17360719460575350926)
XLA Ops:
  1.4 1.3 copy-done.14
  2.7 1.3 copy-done.15
  4.0 1.9 %obs_blocks.1 = f32[32,152,128]{2,1,0:T(8,128)} custom-call(f32[75,4096]{1,0:T(8,128)S(1)} %copy-done.14, f32[75,4096]{1,0:T(8,128)S(1)} %copy-done.15, s32[1,4096]{1,0:T(1,128)S(1)} %bitcast.7), custom_call_target="tpu_custom_call" | custom-call | tf_op jit(solution)/shard_map/obs_blocks/pallas_call | solution.py:144
  5.9 4.9 %lon_sends.1 = (f32[2,32,8,128]{3,2,1,0:T(8,128)S(1)}, f32[2,32,8,128]{3,2,1,0:T(8,128)S(1)}) custom-call(f32[75,32,128]{2,1,0:T(8,128)} %control_ref.3, f32[75,32,128]{2,1,0:T(8,128)} %east_ref.3, f32[75,32,128]{2,1,0:T(8,128)} %north_ref.3, s32[75,32,128]{2,1,0:T(8,128)} %mask_ref.3), custom_call_target="tpu_custom_call" | custom-call | tf_op jit(solution)/shard_map/lon_sends/pallas_call | solution.py:272
  10.7 7.1 %all-to-all-start = ((f32[32,152,128]{2,1,0:T(8,128)}), f32[32,152,128]{2,1,0:T(8,128)S(1)}, u32[]{:S(2)}, u32[]{:S(2)}) async-start(f32[32,152,128]{2,1,0:T(8,128)} %obs_blocks.1), calls=%async_computation | async-start | bytes 4980736 | tf_op jit(solution)/shard_map/all_to_all | solution.py:540
  17.8 1.4 collective-permute-start.2
  19.2 2.8 %collective-permute-start.3 = (f32[2,32,8,128]{3,2,1,0:T(8,128)S(1)}, f32[2,32,8,128]{3,2,1,0:T(8,128)S(1)}, u32[]{:S(2)}, u32[]{:S(2)}) collective-permute-start(f32[2,32,8,128]{3,2,1,0:T(8,128)S(1)} %get-tuple-element.31), channel_id=1, source_target_pairs={{4,0},{8,4},{12,8},{16,12},{20,16},{24,20},{28,24},{0,28},{5,1},{9... | collective-permute-start | bytes 786440 | tf_op jit(solution)/shard_map/ppermute | solution.py:549
  22.1 6.5 %stage.1 = (f32[32,80,128]{2,1,0:T(8,128)S(1)}, f32[32,80,128]{2,1,0:T(8,128)S(1)}, f32[32,80,128]{2,1,0:T(8,128)S(1)}, f32[32,80,128]{2,1,0:T(8,128)S(1)}, f32[...) custom-call(f32[75,32,128]{2,1,0:T(8,128)} %control_ref.3, ...), custom_call_target="tpu_custom_call" | custom-call | tf_op jit(solution)/shard_map/stage/pallas_call | solution.py:238
  29.6 1.1 copy-done.9
  30.8 1.4 copy-done.12
  36.0 1.4 broadcast_select_fusion.2
  38.3 3.3 %collective-permute-start.1 = (f32[16,80,128]{2,1,0:T(8,128)S(1)}, f32[16,80,128]{2,1,0:T(8,128)S(1)}, u32[]{:S(2)}, u32[]{:S(2)}) collective-permute-start(f32[16,80,128]{2,1,0:T(8,128)S(1)} %get-tuple-element.47), channel_id=1, source_target_pairs={{1,2},{2,1},{5,6},{6,5},{9,10},{10,9},{13,14},{14,13},{17,18},{18,... | collective-permute-start | bytes 1966088 | tf_op jit(solution)/shard_map/ppermute | solution.py:556
  41.6 26.9 %collective-permute-done.2.from_west = f32[2,32,8,128]{3,2,1,0:T(8,128)S(1)} collective-permute-done((f32[2,32,8,128]{3,2,1,0:T(8,128)S(1)}, f32[2,32,8,128]{3,2,1,0:T(8,128)S(1)}, u32[]{:S(2)}, u32[]{:S(2)}) %collective-permute-start.2) | collective-permute-done | bytes 262176 | tf_op jit(solution)/shard_map/ppermute | solution.py:549
  69.6 3.8 %collective-permute-start.5 = (f32[2,2,4,8,128]{4,3,2,1,0:T(8,128)S(1)}, f32[2,2,4,8,128]{4,3,2,1,0:T(8,128)S(1)}, u32[]{:S(2)}, u32[]{:S(2)}) collective-permute-start(f32[2,2,4,8,128]{4,3,2,1,0:T(8,128)S(1)} %get-tuple-element.40), channel_id=1, source_target_pairs={{1,2},{2,1},{5,6},{6,5},{9,10},{10,9},{13,14},{14,13},{17,18},{18,... | collective-permute-start | bytes 196616 | tf_op jit(solution)/shard_map/ppermute | solution.py:556
  73.4 2.1 %collective-permute-done.5 = f32[2,2,4,8,128]{4,3,2,1,0:T(8,128)S(1)} collective-permute-done((f32[2,2,4,8,128]{4,3,2,1,0:T(8,128)S(1)}, f32[2,2,4,8,128]{4,3,2,1,0:T(8,128)S(1)}, u32[]{:S(2)}, u32[]{:S(2)}) %collective-permute-start.5) | collective-permute-done | bytes 65568 | tf_op jit(solution)/shard_map/ppermute | solution.py:556
  77.6 1.1 faces.1
  79.6 9.3 %forward.1 = (f32[32,80,128]{2,1,0:T(8,128)S(1)}, f32[2,2,2,40,8,128]{5,4,3,2,1,0:T(8,128)S(1)}) custom-call(f32[32,80,128]{2,1,0:T(8,128)S(1)} %copy-done.7, f32[16,80,128]{2,1,0:T(8,128)S(1)} %get-tuple-element.46.south_in, f32[16,80,128]{2,1,0:T(8,128)S(1)} %get-tuple-element.45.north_in, f32[40,80,128]{2,1,0:T(8,128)S(1)} %get-tuple-element.27.e_ref, ...), custom_call_target="tpu_custom_call" | custom-call | tf_op jit(solution)/shard_map/forward/pallas_call | solution.py:434
  88.9 1.1 copy-done.23
  90.1 13.1 %gather.1.equivalent_ref = f32[32,80,128]{2,1,0:T(8,128)S(1)} custom-call(s32[4,4096]{1,0:T(4,128)S(1)} %copy-done.27, f32[4,4096]{1,0:T(4,128)S(1)} %copy-done.28, f32[32,80,128]{2,1,0:T(8,128)S(1)} %get-tuple-element.32.bg_ref), custom_call_target="tpu_custom_call" | custom-call | tf_op jit(solution)/shard_map/gather/pallas_call | solution.py:70
  104.2 1.3 copy-done.5
  108.0 14.5 %all-to-all-start.1 = ((f32[32,75,128]{2,1,0:T(8,128)}), f32[32,75,128]{2,1,0:T(8,128)S(1)}, u32[]{:S(2)}, u32[]{:S(2)}) async-start(f32[32,75,128]{2,1,0:T(8,128)} %copy-done.20), calls=%async_computation.1 | async-start | bytes 2621440 | tf_op jit(solution)/shard_map/all_to_all | solution.py:540
  122.5 1.3 copy-done.22
  123.8 15.0 %scatter.1.adjoint_ref = f32[32,80,128]{2,1,0:T(8,128)S(1)} custom-call(s32[4,4096]{1,0:T(4,128)S(1)} %copy-done.27, f32[4,4096]{1,0:T(4,128)S(1)} %copy-done.28, f32[32,80,128]{2,1,0:T(8,128)S(1)} %copy-done.22), custom_call_target="tpu_custom_call" | custom-call | tf_op jit(solution)/shard_map/scatter/pallas_call | solution.py:110
  139.2 3.5 %collective-permute-start.7 = (f32[4,80,128]{2,1,0:T(8,128)S(1)}, f32[4,80,128]{2,1,0:T(8,128)S(1)}, u32[]{:S(2)}, u32[]{:S(2)}) collective-permute-start(f32[4,80,128]{2,1,0:T(8,128)S(1)} %get-tuple-element.43), channel_id=1, source_target_pairs={{1,2},{2,1},{5,6},{6,5},{9,10},{10,9},{13,14},{14,13},{17,18},{18,... | collective-permute-start | bytes 491528 | tf_op jit(solution)/shard_map/ppermute | solution.py:556
  142.8 3.5 %collective-permute-done.7 = f32[4,80,128]{2,1,0:T(8,128)S(1)} collective-permute-done((f32[4,80,128]{2,1,0:T(8,128)S(1)}, f32[4,80,128]{2,1,0:T(8,128)S(1)}, u32[]{:S(2)}, u32[]{:S(2)}) %collective-permute-start.7) | collective-permute-done | bytes 163872 | tf_op jit(solution)/shard_map/ppermute | solution.py:556
  146.3 2.2 %strip_adjoint.1 = (f32[2,2,40,8,128]{4,3,2,1,0:T(8,128)S(1)}, f32[2,10,8,128]{3,2,1,0:T(8,128)S(1)}, f32[2,10,8,128]{3,2,1,0:T(8,128)S(1)}) custom-call(f32[32,80,128]{2,1,0:T(8,128)S(1)} %scatter.1.adjoint_ref, f32[4,80,128]{2,1,0:T(8,128)S(1)} %get-tuple-element.50.south_in, f32[4,80,128]{2,1,0:T(8,128)S(1)} %get-tuple-element.49.north_in), custom_call_target="tpu_custom_call" | custom-call | tf_op jit(solution)/shard_map/strip_adjoint/pallas_call | solution.py:466
  148.5 1.5 collective-permute-start.8
  150.0 2.9 %collective-permute-start.9 = (f32[2,10,8,128]{3,2,1,0:T(8,128)S(1)}, f32[2,10,8,128]{3,2,1,0:T(8,128)S(1)}, u32[]{:S(2)}, u32[]{:S(2)}) collective-permute-start(f32[2,10,8,128]{3,2,1,0:T(8,128)S(1)} %get-tuple-element.37), channel_id=1, source_target_pairs={{4,0},{8,4},{12,8},{16,12},{20,16},{24,20},{28,24},{0,28},{5,1},{9... | collective-permute-start | bytes 245768 | tf_op jit(solution)/shard_map/ppermute | solution.py:549
  152.9 1.9 %collective-permute-done.8.from_west = f32[2,10,8,128]{3,2,1,0:T(8,128)S(1)} collective-permute-done((f32[2,10,8,128]{3,2,1,0:T(8,128)S(1)}, f32[2,10,8,128]{3,2,1,0:T(8,128)S(1)}, u32[]{:S(2)}, u32[]{:S(2)}) %collective-permute-start.8) | collective-permute-done | bytes 81952 | tf_op jit(solution)/shard_map/ppermute | solution.py:549
  154.8 1.3 copy-done.24
  156.1 10.3 %backward.1 = f32[2400,128]{1,0:T(8,128)} custom-call(f32[32,80,128]{2,1,0:T(8,128)S(1)} %scatter.1.adjoint_ref, f32[4,80,128]{2,1,0:T(8,128)S(1)} %get-tuple-element.50.south_in, f32[4,80,128]{2,1,0:T(8,128)S(1)} %get-tuple-element.49.north_in, f32[2,2,40,8,128]{4,3,2,1,0:T(8,128)S(1)} %get-tuple-element.35.strip_ref, ...), custom_call_target="tpu_custom_call" | custom-call | tf_op jit(solution)/shard_map/backward/pallas_call | solution.py:497
  166.4 1.2 place_departures.1
  (70 shorter events, 14.4 us)
Async XLA Ops:
  1.4 1.3 copy-start.14
  2.7 1.3 copy-start.15
  10.7 93.5 %all-to-all-start = ((f32[32,152,128]{2,1,0:T(8,128)}), f32[32,152,128]{2,1,0:T(8,128)S(1)}, u32[]{:S(2)}, u32[]{:S(2)}) async-start(f32[32,152,128]{2,1,0:T(8,128)} %obs_blocks.1), calls=%async_computation | async-start | bytes 4980736 | tf_op jit(solution)/shard_map/all_to_all | solution.py:540
  17.8 50.7 %collective-permute-start.2 = (f32[2,32,8,128]{3,2,1,0:T(8,128)S(1)}, f32[2,32,8,128]{3,2,1,0:T(8,128)S(1)}, u32[]{:S(2)}, u32[]{:S(2)}) collective-permute-start(f32[2,32,8,128]{3,2,1,0:T(8,128)S(1)} %get-tuple-element.30), channel_id=1, source_target_pairs={{0,4},{4,8},{8,12},{12,16},{16,20},{20,24},{24,28},{28,0},{1,5},{5... | collective-permute-start | bytes 786440 | tf_op jit(solution)/shard_map/ppermute | solution.py:549
  19.2 49.3 %collective-permute-start.3 = (f32[2,32,8,128]{3,2,1,0:T(8,128)S(1)}, f32[2,32,8,128]{3,2,1,0:T(8,128)S(1)}, u32[]{:S(2)}, u32[]{:S(2)}) collective-permute-start(f32[2,32,8,128]{3,2,1,0:T(8,128)S(1)} %get-tuple-element.31), channel_id=1, source_target_pairs={{4,0},{8,4},{12,8},{16,12},{20,16},{24,20},{28,24},{0,28},{5,1},{9... | collective-permute-start | bytes 786440 | tf_op jit(solution)/shard_map/ppermute | solution.py:549
  30.8 1.4 copy-start.12
  37.4 38.0 %collective-permute-start = (f32[16,80,128]{2,1,0:T(8,128)S(1)}, f32[16,80,128]{2,1,0:T(8,128)S(1)}, u32[]{:S(2)}, u32[]{:S(2)}) collective-permute-start(f32[16,80,128]{2,1,0:T(8,128)S(1)} %get-tuple-element.48), channel_id=1, source_target_pairs={{0,1},{1,0},{2,3},{3,2},{4,5},{5,4},{6,7},{7,6},{8,9},{9,8},{10,11... | collective-permute-start | bytes 1966088 | tf_op jit(solution)/shard_map/ppermute | solution.py:555
  38.3 37.2 %collective-permute-start.1 = (f32[16,80,128]{2,1,0:T(8,128)S(1)}, f32[16,80,128]{2,1,0:T(8,128)S(1)}, u32[]{:S(2)}, u32[]{:S(2)}) collective-permute-start(f32[16,80,128]{2,1,0:T(8,128)S(1)} %get-tuple-element.47), channel_id=1, source_target_pairs={{1,2},{2,1},{5,6},{6,5},{9,10},{10,9},{13,14},{14,13},{17,18},{18,... | collective-permute-start | bytes 1966088 | tf_op jit(solution)/shard_map/ppermute | solution.py:556
  68.6 4.8 %collective-permute-start.4 = (f32[2,2,4,8,128]{4,3,2,1,0:T(8,128)S(1)}, f32[2,2,4,8,128]{4,3,2,1,0:T(8,128)S(1)}, u32[]{:S(2)}, u32[]{:S(2)}) collective-permute-start(f32[2,2,4,8,128]{4,3,2,1,0:T(8,128)S(1)} %broadcast_select_fusion.9), channel_id=1, source_target_pairs={{0,1},{1,0},{2,3},{3,2},{4,5},{5,4},{6,7},{7,6},{8,9},{9,8},{10,11... | collective-permute-start | bytes 196616 | tf_op jit(solution)/shard_map/ppermute | solution.py:555
  69.6 5.8 %collective-permute-start.5 = (f32[2,2,4,8,128]{4,3,2,1,0:T(8,128)S(1)}, f32[2,2,4,8,128]{4,3,2,1,0:T(8,128)S(1)}, u32[]{:S(2)}, u32[]{:S(2)}) collective-permute-start(f32[2,2,4,8,128]{4,3,2,1,0:T(8,128)S(1)} %get-tuple-element.40), channel_id=1, source_target_pairs={{1,2},{2,1},{5,6},{6,5},{9,10},{10,9},{13,14},{14,13},{17,18},{18,... | collective-permute-start | bytes 196616 | tf_op jit(solution)/shard_map/ppermute | solution.py:556
  75.5 1.3 copy-start.17
  75.5 1.7 %copy-start.19 = (f32[32,80,128]{2,1,0:T(8,128)S(1)}, f32[32,80,128]{2,1,0:T(8,128)}, u32[]{:S(2)}) copy-start(f32[32,80,128]{2,1,0:T(8,128)} %copy-done.18) | copy-start | bytes 3932164
  75.6 2.0 %copy-start.10 = (f32[32,80,128]{2,1,0:T(8,128)S(1)}, f32[32,80,128]{2,1,0:T(8,128)}, u32[]{:S(2)}) copy-start(f32[32,80,128]{2,1,0:T(8,128)} %copy-done.9) | copy-start | bytes 3932164
  77.6 1.3 copy-start.7
  77.6 2.0 %copy-start.13 = (f32[4,2,2,32,8,128]{5,4,3,2,1,0:T(8,128)S(1)}, f32[4,2,2,32,8,128]{5,4,3,2,1,0:T(8,128)}, u32[]{:S(2)}) copy-start(f32[4,2,2,32,8,128]{5,4,3,2,1,0:T(8,128)} %copy-done.12) | copy-start | bytes 6291460
  78.7 10.2 %copy-start = (f32[40,80,128]{2,1,0:T(8,128)}, f32[40,80,128]{2,1,0:T(8,128)S(1)}, u32[]{:S(2)}) copy-start(f32[40,80,128]{2,1,0:T(8,128)S(1)} %get-tuple-element.27.e_ref) | copy-start | bytes 4915204
  78.7 10.2 %copy-start.2 = (f32[40,80,128]{2,1,0:T(8,128)}, f32[40,80,128]{2,1,0:T(8,128)S(1)}, u32[]{:S(2)}) copy-start(f32[40,80,128]{2,1,0:T(8,128)S(1)} %get-tuple-element.28.n_ref) | copy-start | bytes 4915204
  79.6 10.5 %copy-start.27 = (s32[4,4096]{1,0:T(4,128)S(1)}, s32[4,4096]{1,0:T(4,128)}, u32[]{:S(2)}) copy-start(s32[4,4096]{1,0:T(4,128)} %cells_ref.3) | copy-start | bytes 196612
  79.6 10.5 %copy-start.28 = (f32[4,4096]{1,0:T(4,128)S(1)}, f32[4,4096]{1,0:T(4,128)}, u32[]{:S(2)}) copy-start(f32[4,4096]{1,0:T(4,128)} %weights_ref.3) | copy-start | bytes 196612
  88.9 1.1 copy-start.23
  104.2 1.3 copy-start.5
  108.0 46.8 %copy-start.11 = (f32[32,80,128]{2,1,0:T(8,128)S(1)}, f32[32,80,128]{2,1,0:T(8,128)}, u32[]{:S(2)}) copy-start(f32[32,80,128]{2,1,0:T(8,128)} %copy-done.9) | copy-start | bytes 3932164
  108.0 58.4 %all-to-all-start.1 = ((f32[32,75,128]{2,1,0:T(8,128)}), f32[32,75,128]{2,1,0:T(8,128)S(1)}, u32[]{:S(2)}, u32[]{:S(2)}) async-start(f32[32,75,128]{2,1,0:T(8,128)} %copy-done.20), calls=%async_computation.1 | async-start | bytes 2621440 | tf_op jit(solution)/shard_map/all_to_all | solution.py:540
  122.5 1.3 copy-start.22
  123.8 31.0 %copy-start.3 = (f32[40,80,128]{2,1,0:T(8,128)S(1)}, f32[40,80,128]{2,1,0:T(8,128)}, u32[]{:S(2)}) copy-start(f32[40,80,128]{2,1,0:T(8,128)} %copy-done.2) | copy-start | bytes 4915204
  138.8 15.9 %copy-start.8 = (f32[32,80,128]{2,1,0:T(8,128)S(1)}, f32[32,80,128]{2,1,0:T(8,128)}, u32[]{:S(2)}) copy-start(f32[32,80,128]{2,1,0:T(8,128)} %copy-done.6) | copy-start | bytes 3932164
  138.9 15.9 %copy-start.1 = (f32[40,80,128]{2,1,0:T(8,128)S(1)}, f32[40,80,128]{2,1,0:T(8,128)}, u32[]{:S(2)}) copy-start(f32[40,80,128]{2,1,0:T(8,128)} %copy-done) | copy-start | bytes 4915204
  138.9 3.9 %collective-permute-start.6 = (f32[4,80,128]{2,1,0:T(8,128)S(1)}, f32[4,80,128]{2,1,0:T(8,128)S(1)}, u32[]{:S(2)}, u32[]{:S(2)}) collective-permute-start(f32[4,80,128]{2,1,0:T(8,128)S(1)} %get-tuple-element.44), channel_id=1, source_target_pairs={{0,1},{1,0},{2,3},{3,2},{4,5},{5,4},{6,7},{7,6},{8,9},{9,8},{10,11... | collective-permute-start | bytes 491528 | tf_op jit(solution)/shard_map/ppermute | solution.py:555
  139.2 7.1 %collective-permute-start.7 = (f32[4,80,128]{2,1,0:T(8,128)S(1)}, f32[4,80,128]{2,1,0:T(8,128)S(1)}, u32[]{:S(2)}, u32[]{:S(2)}) collective-permute-start(f32[4,80,128]{2,1,0:T(8,128)S(1)} %get-tuple-element.43), channel_id=1, source_target_pairs={{1,2},{2,1},{5,6},{6,5},{9,10},{10,9},{13,14},{14,13},{17,18},{18,... | collective-permute-start | bytes 491528 | tf_op jit(solution)/shard_map/ppermute | solution.py:556
  148.5 6.3 %collective-permute-start.8 = (f32[2,10,8,128]{3,2,1,0:T(8,128)S(1)}, f32[2,10,8,128]{3,2,1,0:T(8,128)S(1)}, u32[]{:S(2)}, u32[]{:S(2)}) collective-permute-start(f32[2,10,8,128]{3,2,1,0:T(8,128)S(1)} %get-tuple-element.36), channel_id=1, source_target_pairs={{0,4},{4,8},{8,12},{12,16},{16,20},{20,24},{24,28},{28,0},{1,5},{5... | collective-permute-start | bytes 245768 | tf_op jit(solution)/shard_map/ppermute | solution.py:549
  150.0 4.8 %collective-permute-start.9 = (f32[2,10,8,128]{3,2,1,0:T(8,128)S(1)}, f32[2,10,8,128]{3,2,1,0:T(8,128)S(1)}, u32[]{:S(2)}, u32[]{:S(2)}) collective-permute-start(f32[2,10,8,128]{3,2,1,0:T(8,128)S(1)} %get-tuple-element.37), channel_id=1, source_target_pairs={{4,0},{8,4},{12,8},{16,12},{20,16},{24,20},{28,24},{0,28},{5,1},{9... | collective-permute-start | bytes 245768 | tf_op jit(solution)/shard_map/ppermute | solution.py:549
  154.8 1.3 copy-start.24
  (9 other events, 9.2 us)

commit v2 on v1

--- a/solution.py
+++ b/solution.py
@@ -36,9 +36,10 @@
     return jnp.where(at == 0, low, jnp.where(at == 1, high, 0.0))
 
 
-def gather_kernel(rows, lev, cols, nb, cells_ref, weights_ref, bg_ref, out_ref, bb, t0, t1, rr0, rr1):
+def gather_kernel(rows, lev, cols, nb, margin, cells_ref, weights_ref, bg_ref, rim_ref, out_ref, bb, t0, t1, rr0, rr1):
     for r in range(rows):
-        hi, lo = split2(bg_ref[r])
+        parts = [put_rim(bg_ref[r, 8 * g:8 * g + 8, :], g, lev // 8, margin, lambda slab: rim_ref[slab, r]) for g in range(lev // 8)]
+        hi, lo = split2(jnp.concatenate(parts, 0))
         bb[r * lev:(r + 1) * lev, 0:cols] = hi
         bb[r * lev:(r + 1) * lev, cols:2 * cols] = lo
     blk = 256
@@ -64,16 +65,16 @@
     lax.fori_loop(0, nb // 2, step, 0)
 
 
-def gather(cells, weights, bg, slots):
+def gather(cells, weights, bg, rim, slots, margin):
     rows, lev, cols = bg.shape
     nb = slots // 256
-    return pl.pallas_call(functools.partial(gather_kernel, rows, lev, cols, nb),
+    return pl.pallas_call(functools.partial(gather_kernel, rows, lev, cols, nb, margin),
         out_shape=jax.ShapeDtypeStruct((2 * nb, lev, 128), F32),
-        in_specs=[pl.BlockSpec(memory_space=VMEM)] * 3,
+        in_specs=[pl.BlockSpec(memory_space=VMEM)] * 4,
         out_specs=pl.BlockSpec(memory_space=VMEM), name="gather",
         scratch_shapes=[VMEM((rows * lev, 2 * cols), BF16), VMEM((rows * lev, 256), F32), VMEM((rows * lev, 256), F32), VMEM((rows, 256), F32), VMEM((rows, 256), F32)],
         compiler_params=params(20),
-    )(cells, weights, bg)
+    )(cells, weights, bg, rim)
 
 
 def scatter_kernel(rows, lev, cols, nb, cells_ref, weights_ref, back_ref, out_ref, x, acc):
@@ -363,17 +364,36 @@
     lax.fori_loop(0, rim.shape[0], step, 0)
 
 
-def tile_sweeps(g, groups, rows, margin, states, e_ref, n_ref, rim, write):
-    tall = rows + 2 * margin
-    put = lanes_of(g)
+def put_rim(x, g, groups, margin, rim):
     _, per = slabs_of(groups)
     slab = g // per
+    lane = lax.broadcasted_iota(jnp.int32, x.shape, x.ndim - 1)
+    edge = rim(slab)
     shift = 128 - margin - 4 * margin * (g - slab * per)
-    def finish(at, end, value):
-        lane, _ = place(end - at)
-        edge = pltpu.roll(rim[slab, at - margin:end - margin], shift, 2)
-        write(at - margin, end - margin, jnp.where((lane < margin) | (lane >= 128 - margin), edge, value))
-    all_sweeps(tall, margin, states, lambda a, b: e_ref[a:b, put, :], lambda a, b: n_ref[a:b, put, :], finish)
+    edge = turn(edge, shift) if isinstance(shift, int) else pltpu.roll(edge, shift, edge.ndim - 1)
+    return jnp.where((lane < margin) | (lane >= 128 - margin), edge, x)
+
+
+def tiles_kernel(groups, rows, margin, u_ref, south_in, north_in, e_ref, n_ref, out_ref, state_a, state_b):
+    tall = rows + 2 * margin
+    def step(g, _):
+        put = lanes_of(g)
+        fill(state_a, put, south_in, u_ref, north_in, margin, 0)
+        def write(at, end, value):
+            out_ref[at - margin:end - margin, put, :] = value
+        all_sweeps(tall, margin, (state_a, state_b), lambda a, b: e_ref[a:b, put, :], lambda a, b: n_ref[a:b, put, :], write)
+        return 0
+    lax.fori_loop(0, groups, step, 0)
+
+
+def tiles(groups, rows, margin, u, south_in, north_in, e, n):
+    tall = rows + 2 * margin
+    size = rows * LANES8 * groups * 128
+    return pl.pallas_call(functools.partial(tiles_kernel, groups, rows, margin),
+        out_shape=jax.ShapeDtypeStruct((rows, LANES8 * groups, 128), F32),
+        in_specs=[WHOLE] * 5, out_specs=WHOLE, name="tiles", scratch_shapes=[VMEM((tall, LANES8, 128), F32)] * 2,
+        cost_estimate=pl.CostEstimate(flops=40 * size, bytes_accessed=20 * size, transcendentals=0),
+        compiler_params=params(16))(u, south_in, north_in, e, n)
 
 
 def fill(state, put, low, middle, high, margin, offset):
@@ -383,7 +403,7 @@
     state[margin + rows:2 * margin + rows] = high[offset:offset + margin, put, :]
 
 
-def forward_kernel(groups, rows, margin, u_ref, south_in, north_in, e_ref, n_ref, strip_ref, from_west, from_east, rims_ref, south_corners, north_corners, out_ref, faces_ref, strip_a, strip_b, mask, state_a, state_b, rim):
+def forward_kernel(rows, margin, strip_ref, from_west, from_east, rims_ref, south_corners, north_corners, rim, faces_ref, strip_a, strip_b, mask):
     tall = rows + 2 * margin
     def join(slab, _):
         for side in range(2):
@@ -411,31 +431,16 @@
         return 0
     lax.fori_loop(0, rim.shape[0], join, 0)
     strip_sweeps(rows, margin, (strip_a, strip_b), faces_ref, rim)
-    def step(g, _):
-        put = lanes_of(g)
-        fill(state_a, put, south_in, u_ref, north_in, margin, 0)
-        def write(at, end, value):
-            out_ref[at:end, put, :] = value
-        tile_sweeps(g, groups, rows, margin, (state_a, state_b), e_ref, n_ref, rim, write)
-        return 0
-    lax.fori_loop(0, groups, step, 0)
-
-
-def sweep_scratch(groups, rows, margin):
+
+
+def forward_strips(groups, rows, margin, *args):
     tall = rows + 2 * margin
     slabs, _ = slabs_of(groups)
-    return [VMEM((2, slabs, tall, LANES8, 128), F32)] * 2, [VMEM((tall, LANES8, 128), F32)] * 2 + [VMEM((slabs, rows, LANES8, 128), F32)]
-
-
-def forward(groups, rows, margin, *args):
-    tall = rows + 2 * margin
-    slabs, _ = slabs_of(groups)
-    strips, tiles = sweep_scratch(groups, rows, margin)
-    return pl.pallas_call(functools.partial(forward_kernel, groups, rows, margin),
-        out_shape=[jax.ShapeDtypeStruct((rows, LANES8 * groups, 128), F32), jax.ShapeDtypeStruct((2, 2, slabs, tall, LANES8, 128), F32)],
-        in_specs=[WHOLE] * 11, out_specs=[WHOLE] * 2, name="forward",
-        scratch_shapes=strips + [VMEM((2, tall + 1, LANES8, 128), F32)] + tiles,
-        compiler_params=params(24))(*args)
+    return pl.pallas_call(functools.partial(forward_kernel, rows, margin),
+        out_shape=[jax.ShapeDtypeStruct((slabs, rows, LANES8, 128), F32), jax.ShapeDtypeStruct((2, 2, slabs, tall, LANES8, 128), F32)],
+        in_specs=[WHOLE] * 6, out_specs=[WHOLE] * 2, name="forward_strips",
+        scratch_shapes=[VMEM((2, slabs, tall, LANES8, 128), F32)] * 2 + [VMEM((2, tall + 1, LANES8, 128), F32)],
+        compiler_params=params(16))(*args)
 
 
 def strip_adjoint_kernel(groups, rows, margin, adjoint_ref, south_in, north_in, strip_ref, to_east, to_west):
@@ -468,8 +473,7 @@
         in_specs=[WHOLE] * 3, out_specs=[WHOLE] * 3, name="strip_adjoint", compiler_params=params(12))(adjoint, south_in, north_in)
 
 
-def backward_kernel(groups, levels, rows, margin, adjoint_ref, south_in, north_in, strip_ref, from_west, from_east, e_ref, n_ref, faces_ref, u_ref, mask_ref,
-                    out_ref, strip_a, strip_b, state_a, state_b, rim):
+def finish_kernel(groups, levels, rows, margin, tiles_ref, strip_ref, from_west, from_east, faces_ref, u_ref, mask_ref, out_ref, strip_a, strip_b, rim):
     quarter = (rows + 2 * margin) // 4
     for slab in range(rim.shape[0]):
         for at in range(0, quarter, 2):
@@ -482,22 +486,24 @@
     def step(g, _):
         put = lanes_of(g)
         start = group_start(g, levels)
-        fill(state_a, put, south_in, adjoint_ref, north_in, margin, 0)
-        def write(at, end, value):
-            value = u_ref[at:end, put, :] + mask_ref[at:end, put, :] * value
-            for r in range(at, end):
-                out_ref[pl.ds(start * rows + r, LANES8, stride=rows), :] = value[r - at]
-        tile_sweeps(g, groups, rows, margin, (state_a, state_b), e_ref, n_ref, rim, write)
+        for at in range(0, rows, LANES8):
+            here = slice(at, at + LANES8)
+            value = put_rim(tiles_ref[here, put, :], g, groups, margin, lambda slab: rim[slab, here])
+            value = u_ref[here, put, :] + mask_ref[here, put, :] * value
+            for r in range(LANES8):
+                out_ref[pl.ds(start * rows + at + r, LANES8, stride=rows), :] = value[r]
         return 0
     lax.fori_loop(0, groups, step, 0)
 
 
-def backward(groups, levels, rows, margin, *args):
-    strips, tiles = sweep_scratch(groups, rows, margin)
-    return pl.pallas_call(functools.partial(backward_kernel, groups, levels, rows, margin),
+def finish(groups, levels, rows, margin, *args):
+    tall = rows + 2 * margin
+    slabs, _ = slabs_of(groups)
+    return pl.pallas_call(functools.partial(finish_kernel, groups, levels, rows, margin),
         out_shape=jax.ShapeDtypeStruct((levels * rows, 128), F32),
-        in_specs=[WHOLE] * 11, out_specs=WHOLE, name="backward",
-        scratch_shapes=strips + tiles, compiler_params=params(24))(*args)
+        in_specs=[WHOLE] * 7, out_specs=WHOLE, name="finish",
+        scratch_shapes=[VMEM((2, slabs, tall, LANES8, 128), F32)] * 2 + [VMEM((slabs, rows, LANES8, 128), F32)],
+        compiler_params=params(20))(*args)
 
 
 def departures_kernel(groups, levels, equivalent_ref, obs_ref, out_ref, back_ref):
@@ -587,8 +593,9 @@
     south_corners, north_corners = swap_edges("gy", corners[:, :, rows - margin:], corners[:, :, :margin])
     rims = strip_rims(groups, margin, south_in, north_in)
     e, n = faces(groups, rows, margin, fields, south_in, north_in)
-    background, strip_faces = forward(groups, rows, margin, fields[0], south_in, north_in, e, n, strip, from_west, from_east, rims, south_corners, north_corners)
-    equivalent = gather(corner_cells, corner_weights, background, slots)
+    background = tiles(groups, rows, margin, fields[0], south_in, north_in, e, n)
+    rim, strip_faces = forward_strips(groups, rows, margin, strip, from_west, from_east, rims, south_corners, north_corners)
+    equivalent = gather(corner_cells, corner_weights, background, rim, slots, margin)
     out, back = departures_of(groups, levels, equivalent, obs)
     sent = exchange(out, share)
     adjoint = scatter(corner_cells, corner_weights, back, rows, cols)
@@ -596,7 +603,8 @@
     strip, to_east, to_west = strip_adjoint(groups, rows, margin, adjoint, south_in, north_in)
     from_west, from_east = pass_around("gx", to_east, to_west)
     departures = place_departures(sent)
-    gradient = backward(groups, levels, rows, margin, adjoint, south_in, north_in, strip, from_west, from_east, e, n, strip_faces, fields[0], fields[1])
+    swept = tiles(groups, rows, margin, adjoint, south_in, north_in, e, n)
+    gradient = finish(groups, levels, rows, margin, swept, strip, from_west, from_east, strip_faces, fields[0], fields[1])
     return gradient.reshape(levels, rows, cols), departures
 
 

time: 168 us -> 164 us (0.976)
  local copies, waits for them, and re-layouts: 20.4 us -> 17.4 us
  waiting for transfers between devices: 34.4 us -> 32.6 us
    unnamed x58, local copies, waits for them, and re-layouts: 20.4 us -> 17.4 us
    ppermute x2, waiting for transfers between devices: 28.8 us -> 27 us  [pass_around(): lax.ppermute(forth, axis, up)]
    pallas_call x3 -> x5, Pallas kernels: 32.7 us -> 32.5 us  [the longest x1 13.3 us: gather(): pl.pallas_call(functools.partial(gather_kernel, rows, lev, cols, nb, marg...]
  transfers between devices with their start and end apart: 12 -> 12, of which waited for: 4 -> 3; matrix products, arithmetic and copies ran while one was open for 1% -> 1% of each run, Pallas kernels for 35% -> 36%
where the time goes in v2:
time: 164 us; the launch traced here: 163 us
  Pallas kernels  66.2 us (40%)
  starting transfers between devices  43.5 us (27%)
  waiting for transfers between devices  32.6 us (20%)
  local copies, waits for them, and re-layouts  17.4 us (11%)
  other arithmetic  2.27 us (1%)
    ppermute x2, waiting for transfers between devices, pass_around(): lax.ppermute(forth, axis, up)  27 us
    all_to_all x2, starting transfers between devices, exchange(): values = lax.all_to_all(values, ('gx', 'gy'), 0, 0, tiled=True)  21.6 us
    unnamed x58, local copies, waits for them, and re-layouts  17.4 us
    pallas_call x1, Pallas kernels, scatter(): pl.pallas_call(functools.partial(scatter_kernel, rows, lev, cols, nb), ou...  15 us
    pallas_call x1, Pallas kernels, gather(): pl.pallas_call(functools.partial(gather_kernel, rows, lev, cols, nb, marg...  13.3 us
    pallas_call x2, Pallas kernels, tiles(): pl.pallas_call(functools.partial(tiles_kernel, groups, rows, margin), out...  12 us
    ppermute x3, starting transfers between devices, swap_edges(): outer = lax.ppermute(jnp.where(odd, forth, back), axis, rounds[1])  10.6 us
    pallas_call x1, Pallas kernels, stage(): pl.pallas_call(functools.partial(stage_kernel, groups, levels, margin), g...  6.49 us
  transfers between devices with their start and end apart: 12, of which 3 were waited for; matrix products, arithmetic and copies ran while one was open for 1% of the time, Pallas kernels for 36%

profile of v2, /device:TPU:1, one launch (start us, length us, event | category | flops | bytes accessed | tf_op | source)
XLA Modules:
  0.0 163.0 jit_solution(9995156128677195567)
XLA Ops:
  1.4 1.3 copy-done.14
  2.7 1.3 copy-done.15
  4.0 1.9 %obs_blocks.1 = f32[32,152,128]{2,1,0:T(8,128)} custom-call(f32[75,4096]{1,0:T(8,128)S(1)} %copy-done.14, f32[75,4096]{1,0:T(8,128)S(1)} %copy-done.15, s32[1,4096]{1,0:T(1,128)S(1)} %bitcast.7), custom_call_target="tpu_custom_call" | custom-call | tf_op jit(solution)/shard_map/obs_blocks/pallas_call | solution.py:145
  5.9 4.9 %lon_sends.1 = (f32[2,32,8,128]{3,2,1,0:T(8,128)S(1)}, f32[2,32,8,128]{3,2,1,0:T(8,128)S(1)}) custom-call(f32[75,32,128]{2,1,0:T(8,128)} %control_ref.3, f32[75,32,128]{2,1,0:T(8,128)} %east_ref.3, f32[75,32,128]{2,1,0:T(8,128)} %north_ref.3, s32[75,32,128]{2,1,0:T(8,128)} %mask_ref.3), custom_call_target="tpu_custom_call" | custom-call | tf_op jit(solution)/shard_map/lon_sends/pallas_call | solution.py:273
  10.8 7.1 %all-to-all-start = ((f32[32,152,128]{2,1,0:T(8,128)}), f32[32,152,128]{2,1,0:T(8,128)S(1)}, u32[]{:S(2)}, u32[]{:S(2)}) async-start(f32[32,152,128]{2,1,0:T(8,128)} %obs_blocks.1), calls=%async_computation | async-start | bytes 4980736 | tf_op jit(solution)/shard_map/all_to_all | solution.py:546
  17.9 1.4 collective-permute-start.2
  19.3 2.8 %collective-permute-start.3 = (f32[2,32,8,128]{3,2,1,0:T(8,128)S(1)}, f32[2,32,8,128]{3,2,1,0:T(8,128)S(1)}, u32[]{:S(2)}, u32[]{:S(2)}) collective-permute-start(f32[2,32,8,128]{3,2,1,0:T(8,128)S(1)} %get-tuple-element.31), channel_id=1, source_target_pairs={{4,0},{8,4},{12,8},{16,12},{20,16},{24,20},{28,24},{0,28},{5,1},{9... | collective-permute-start | bytes 786440 | tf_op jit(solution)/shard_map/ppermute | solution.py:555
  22.1 6.5 %stage.1 = (f32[32,80,128]{2,1,0:T(8,128)S(1)}, f32[32,80,128]{2,1,0:T(8,128)S(1)}, f32[32,80,128]{2,1,0:T(8,128)S(1)}, f32[32,80,128]{2,1,0:T(8,128)S(1)}, f32[...) custom-call(f32[75,32,128]{2,1,0:T(8,128)} %control_ref.3, ...), custom_call_target="tpu_custom_call" | custom-call | tf_op jit(solution)/shard_map/stage/pallas_call | solution.py:239
  29.7 1.1 copy-done.7
  30.8 1.4 copy-done.12
  32.2 1.1 copy-done.18
  36.1 1.4 broadcast_select_fusion.2
  38.3 3.3 %collective-permute-start.1 = (f32[16,80,128]{2,1,0:T(8,128)S(1)}, f32[16,80,128]{2,1,0:T(8,128)S(1)}, u32[]{:S(2)}, u32[]{:S(2)}) collective-permute-start(f32[16,80,128]{2,1,0:T(8,128)S(1)} %get-tuple-element.47), channel_id=1, source_target_pairs={{1,2},{2,1},{5,6},{6,5},{9,10},{10,9},{13,14},{14,13},{17,18},{18,... | collective-permute-start | bytes 1966088 | tf_op jit(solution)/shard_map/ppermute | solution.py:562
  41.6 26.9 %collective-permute-done.2.from_west = f32[2,32,8,128]{3,2,1,0:T(8,128)S(1)} collective-permute-done((f32[2,32,8,128]{3,2,1,0:T(8,128)S(1)}, f32[2,32,8,128]{3,2,1,0:T(8,128)S(1)}, u32[]{:S(2)}, u32[]{:S(2)}) %collective-permute-start.2) | collective-permute-done | bytes 262176 | tf_op jit(solution)/shard_map/ppermute | solution.py:555
  69.6 3.8 %collective-permute-start.5 = (f32[2,2,4,8,128]{4,3,2,1,0:T(8,128)S(1)}, f32[2,2,4,8,128]{4,3,2,1,0:T(8,128)S(1)}, u32[]{:S(2)}, u32[]{:S(2)}) collective-permute-start(f32[2,2,4,8,128]{4,3,2,1,0:T(8,128)S(1)} %get-tuple-element.40), channel_id=1, source_target_pairs={{1,2},{2,1},{5,6},{6,5},{9,10},{10,9},{13,14},{14,13},{17,18},{18,... | collective-permute-start | bytes 196616 | tf_op jit(solution)/shard_map/ppermute | solution.py:562
  73.4 2.1 %collective-permute-done.5 = f32[2,2,4,8,128]{4,3,2,1,0:T(8,128)S(1)} collective-permute-done((f32[2,2,4,8,128]{4,3,2,1,0:T(8,128)S(1)}, f32[2,2,4,8,128]{4,3,2,1,0:T(8,128)S(1)}, u32[]{:S(2)}, u32[]{:S(2)}) %collective-permute-start.5) | collective-permute-done | bytes 65568 | tf_op jit(solution)/shard_map/ppermute | solution.py:562
  77.6 1.1 faces.1
  79.2 2.6 %forward_strips.1 = (f32[2,32,8,128]{3,2,1,0:T(8,128)S(1)}, f32[2,2,2,40,8,128]{5,4,3,2,1,0:T(8,128)S(1)}) custom-call(f32[4,2,2,32,8,128]{5,4,3,2,1,0:T(8,128)S(1)} %copy-done.13, f32[2,32,8,128]{3,2,1,0:T(8,128)S(1)} %collective-permute-done.2.from_west, f32[2,32,8,128]{3,2,1,0:T(8,128)S(1)} %collective-permute-done.3.from_east, ...), custom_call_target="tpu_custom_call" | custom-call | tf_op jit(solution)/shard_map/forward_strips/pallas_call | solution.py:439
  82.9 6.0 %tiles.2.bg_ref = f32[32,80,128]{2,1,0:T(8,128)S(1)} custom-call(f32[32,80,128]{2,1,0:T(8,128)S(1)} %copy-done.5, f32[16,80,128]{2,1,0:T(8,128)S(1)} %get-tuple-element.46.south_in, f32[16,80,128]{2,1,0:T(8,128)S(1)} %get-tuple-element.45.north_in, f32[40,80,128]{2,1,0:T(8,128)S(1)} %get-tuple-element.27.e_ref, f32[40,80,128]{2,1,0:T(8,128)S(1)} %get-tuple-element.28.n_ref), custom_call_target="tpu_custom_call" | custom-call | flops 13107200 | bytes 6553600 | tf_op jit(solution)/shard_map/tiles/pallas_call | solution.py:392
  88.9 13.3 %gather.1.equivalent_ref = f32[32,80,128]{2,1,0:T(8,128)S(1)} custom-call(s32[4,4096]{1,0:T(4,128)S(1)} %copy-done.27, f32[4,4096]{1,0:T(4,128)S(1)} %copy-done.28, f32[32,80,128]{2,1,0:T(8,128)S(1)} %tiles.2.bg_ref, f32[2,32,8,128]{3,2,1,0:T(8,128)S(1)} %get-tuple-element.32.rim_ref), custom_call_target="tpu_custom_call" | custom-call | tf_op jit(solution)/shard_map/gather/pallas_call | solution.py:71
  103.3 1.3 copy-done.11
  104.9 1.1 copy-done.22
  107.1 14.5 %all-to-all-start.1 = ((f32[32,75,128]{2,1,0:T(8,128)}), f32[32,75,128]{2,1,0:T(8,128)S(1)}, u32[]{:S(2)}, u32[]{:S(2)}) async-start(f32[32,75,128]{2,1,0:T(8,128)} %copy-done.22), calls=%async_computation.1 | async-start | bytes 2621440 | tf_op jit(solution)/shard_map/all_to_all | solution.py:546
  121.6 15.0 %scatter.1.u_ref.adjoint_ref = f32[32,80,128]{2,1,0:T(8,128)S(1)} custom-call(s32[4,4096]{1,0:T(4,128)S(1)} %copy-done.27, f32[4,4096]{1,0:T(4,128)S(1)} %copy-done.28, f32[32,80,128]{2,1,0:T(8,128)S(1)} %copy-done.24), custom_call_target="tpu_custom_call" | custom-call | tf_op jit(solution)/shard_map/scatter/pallas_call | solution.py:111
  137.0 3.5 %collective-permute-start.7 = (f32[4,80,128]{2,1,0:T(8,128)S(1)}, f32[4,80,128]{2,1,0:T(8,128)S(1)}, u32[]{:S(2)}, u32[]{:S(2)}) collective-permute-start(f32[4,80,128]{2,1,0:T(8,128)S(1)} %get-tuple-element.43), channel_id=1, source_target_pairs={{1,2},{2,1},{5,6},{6,5},{9,10},{10,9},{13,14},{14,13},{17,18},{18,... | collective-permute-start | bytes 491528 | tf_op jit(solution)/shard_map/ppermute | solution.py:562
  140.5 3.6 %collective-permute-done.7 = f32[4,80,128]{2,1,0:T(8,128)S(1)} collective-permute-done((f32[4,80,128]{2,1,0:T(8,128)S(1)}, f32[4,80,128]{2,1,0:T(8,128)S(1)}, u32[]{:S(2)}, u32[]{:S(2)}) %collective-permute-start.7) | collective-permute-done | bytes 163872 | tf_op jit(solution)/shard_map/ppermute | solution.py:562
  144.1 2.2 %strip_adjoint.1 = (f32[2,2,40,8,128]{4,3,2,1,0:T(8,128)S(1)}, f32[2,10,8,128]{3,2,1,0:T(8,128)S(1)}, f32[2,10,8,128]{3,2,1,0:T(8,128)S(1)}) custom-call(f32[32,80,128]{2,1,0:T(8,128)S(1)} %scatter.1.u_ref.adjoint_ref, f32[4,80,128]{2,1,0:T(8,128)S(1)} %get-tuple-element.50.south_in, f32[4,80,128]{2,1,0:T(8,128)S(1)} %get-tuple-element.49.north_in), custom_call_target="tpu_custom_call" | custom-call | tf_op jit(solution)/shard_map/strip_adjoint/pallas_call | solution.py:471
  146.3 1.5 collective-permute-start.8
  147.8 3.4 %collective-permute-start.9 = (f32[2,10,8,128]{3,2,1,0:T(8,128)S(1)}, f32[2,10,8,128]{3,2,1,0:T(8,128)S(1)}, u32[]{:S(2)}, u32[]{:S(2)}) collective-permute-start(f32[2,10,8,128]{3,2,1,0:T(8,128)S(1)} %get-tuple-element.37), channel_id=1, source_target_pairs={{4,0},{8,4},{12,8},{16,12},{20,16},{24,20},{28,24},{0,28},{5,1},{9... | collective-permute-start | bytes 245768 | tf_op jit(solution)/shard_map/ppermute | solution.py:555
  151.2 6.0 %tiles.3.tiles_ref = f32[32,80,128]{2,1,0:T(8,128)S(1)} custom-call(f32[32,80,128]{2,1,0:T(8,128)S(1)} %scatter.1.u_ref.adjoint_ref, f32[4,80,128]{2,1,0:T(8,128)S(1)} %get-tuple-element.50.south_in, f32[4,80,128]{2,1,0:T(8,128)S(1)} %get-tuple-element.49.north_in, f32[40,80,128]{2,1,0:T(8,128)S(1)} %copy-done.1, f32[40,80,128]{2,1,0:T(8,128)S(1)} %copy-done.3), custom_call_target="tpu_custom_call" | custom-call | flops 13107200 | bytes 6553600 | tf_op jit(solution)/shard_map/tiles/pallas_call | solution.py:392
  157.2 4.6 %finish.1 = f32[2400,128]{1,0:T(8,128)} custom-call(f32[32,80,128]{2,1,0:T(8,128)S(1)} %tiles.3.tiles_ref, f32[2,2,40,8,128]{4,3,2,1,0:T(8,128)S(1)} %get-tuple-element.35.strip_ref, f32[2,10,8,128]{3,2,1,0:T(8,128)S(1)} %collective-permute-done.8.from_west, f32[2,10,8,128]{3,2,1,0:T(8,128)S(1)} %collective-permute-done.9.from_east, ...), custom_call_target="tpu_custom_call" | custom-call | tf_op jit(solution)/shard_map/finish/pallas_call | solution.py:502
  161.9 1.2 place_departures.1
  (72 shorter events, 12.9 us)
Async XLA Ops:
  1.4 1.3 copy-start.14
  2.7 1.3 copy-start.15
  10.8 92.5 %all-to-all-start = ((f32[32,152,128]{2,1,0:T(8,128)}), f32[32,152,128]{2,1,0:T(8,128)S(1)}, u32[]{:S(2)}, u32[]{:S(2)}) async-start(f32[32,152,128]{2,1,0:T(8,128)} %obs_blocks.1), calls=%async_computation | async-start | bytes 4980736 | tf_op jit(solution)/shard_map/all_to_all | solution.py:546
  17.9 50.7 %collective-permute-start.2 = (f32[2,32,8,128]{3,2,1,0:T(8,128)S(1)}, f32[2,32,8,128]{3,2,1,0:T(8,128)S(1)}, u32[]{:S(2)}, u32[]{:S(2)}) collective-permute-start(f32[2,32,8,128]{3,2,1,0:T(8,128)S(1)} %get-tuple-element.30), channel_id=1, source_target_pairs={{0,4},{4,8},{8,12},{12,16},{16,20},{20,24},{24,28},{28,0},{1,5},{5... | collective-permute-start | bytes 786440 | tf_op jit(solution)/shard_map/ppermute | solution.py:555
  19.3 49.3 %collective-permute-start.3 = (f32[2,32,8,128]{3,2,1,0:T(8,128)S(1)}, f32[2,32,8,128]{3,2,1,0:T(8,128)S(1)}, u32[]{:S(2)}, u32[]{:S(2)}) collective-permute-start(f32[2,32,8,128]{3,2,1,0:T(8,128)S(1)} %get-tuple-element.31), channel_id=1, source_target_pairs={{4,0},{8,4},{12,8},{16,12},{20,16},{24,20},{28,24},{0,28},{5,1},{9... | collective-permute-start | bytes 786440 | tf_op jit(solution)/shard_map/ppermute | solution.py:555
  29.7 1.1 copy-start.7
  30.8 1.4 copy-start.12
  37.4 38.0 %collective-permute-start = (f32[16,80,128]{2,1,0:T(8,128)S(1)}, f32[16,80,128]{2,1,0:T(8,128)S(1)}, u32[]{:S(2)}, u32[]{:S(2)}) collective-permute-start(f32[16,80,128]{2,1,0:T(8,128)S(1)} %get-tuple-element.48), channel_id=1, source_target_pairs={{0,1},{1,0},{2,3},{3,2},{4,5},{5,4},{6,7},{7,6},{8,9},{9,8},{10,11... | collective-permute-start | bytes 1966088 | tf_op jit(solution)/shard_map/ppermute | solution.py:561
  38.3 37.2 %collective-permute-start.1 = (f32[16,80,128]{2,1,0:T(8,128)S(1)}, f32[16,80,128]{2,1,0:T(8,128)S(1)}, u32[]{:S(2)}, u32[]{:S(2)}) collective-permute-start(f32[16,80,128]{2,1,0:T(8,128)S(1)} %get-tuple-element.47), channel_id=1, source_target_pairs={{1,2},{2,1},{5,6},{6,5},{9,10},{10,9},{13,14},{14,13},{17,18},{18,... | collective-permute-start | bytes 1966088 | tf_op jit(solution)/shard_map/ppermute | solution.py:562
  68.6 4.8 %collective-permute-start.4 = (f32[2,2,4,8,128]{4,3,2,1,0:T(8,128)S(1)}, f32[2,2,4,8,128]{4,3,2,1,0:T(8,128)S(1)}, u32[]{:S(2)}, u32[]{:S(2)}) collective-permute-start(f32[2,2,4,8,128]{4,3,2,1,0:T(8,128)S(1)} %broadcast_select_fusion.9), channel_id=1, source_target_pairs={{0,1},{1,0},{2,3},{3,2},{4,5},{5,4},{6,7},{7,6},{8,9},{9,8},{10,11... | collective-permute-start | bytes 196616 | tf_op jit(solution)/shard_map/ppermute | solution.py:561
  69.6 5.8 %collective-permute-start.5 = (f32[2,2,4,8,128]{4,3,2,1,0:T(8,128)S(1)}, f32[2,2,4,8,128]{4,3,2,1,0:T(8,128)S(1)}, u32[]{:S(2)}, u32[]{:S(2)}) collective-permute-start(f32[2,2,4,8,128]{4,3,2,1,0:T(8,128)S(1)} %get-tuple-element.40), channel_id=1, source_target_pairs={{1,2},{2,1},{5,6},{6,5},{9,10},{10,9},{13,14},{14,13},{17,18},{18,... | collective-permute-start | bytes 196616 | tf_op jit(solution)/shard_map/ppermute | solution.py:562
  75.5 1.3 copy-start.19
  75.5 1.7 %copy-start.21 = (f32[32,80,128]{2,1,0:T(8,128)S(1)}, f32[32,80,128]{2,1,0:T(8,128)}, u32[]{:S(2)}) copy-start(f32[32,80,128]{2,1,0:T(8,128)} %copy-done.20) | copy-start | bytes 3932164
  75.6 2.0 %copy-start.8 = (f32[32,80,128]{2,1,0:T(8,128)S(1)}, f32[32,80,128]{2,1,0:T(8,128)}, u32[]{:S(2)}) copy-start(f32[32,80,128]{2,1,0:T(8,128)} %copy-done.7) | copy-start | bytes 3932164
  77.6 1.6 copy-start.13
  78.7 4.1 %copy-start = (f32[40,80,128]{2,1,0:T(8,128)}, f32[40,80,128]{2,1,0:T(8,128)S(1)}, u32[]{:S(2)}) copy-start(f32[40,80,128]{2,1,0:T(8,128)S(1)} %get-tuple-element.27.e_ref) | copy-start | bytes 4915204
  78.8 4.1 %copy-start.2 = (f32[40,80,128]{2,1,0:T(8,128)}, f32[40,80,128]{2,1,0:T(8,128)S(1)}, u32[]{:S(2)}) copy-start(f32[40,80,128]{2,1,0:T(8,128)S(1)} %get-tuple-element.28.n_ref) | copy-start | bytes 4915204
  79.2 3.7 %copy-start.5 = (f32[32,80,128]{2,1,0:T(8,128)S(1)}, f32[32,80,128]{2,1,0:T(8,128)}, u32[]{:S(2)}) copy-start(f32[32,80,128]{2,1,0:T(8,128)} %copy-done.4) | copy-start | bytes 3932164
  82.9 6.0 %copy-start.27 = (s32[4,4096]{1,0:T(4,128)S(1)}, s32[4,4096]{1,0:T(4,128)}, u32[]{:S(2)}) copy-start(s32[4,4096]{1,0:T(4,128)} %cells_ref.3) | copy-start | bytes 196612
  82.9 6.0 %copy-start.28 = (f32[4,4096]{1,0:T(4,128)S(1)}, f32[4,4096]{1,0:T(4,128)}, u32[]{:S(2)}) copy-start(f32[4,4096]{1,0:T(4,128)} %weights_ref.3) | copy-start | bytes 196612
  103.3 1.3 copy-start.11
  107.1 14.5 %copy-start.24 = (f32[32,80,128]{2,1,0:T(8,128)S(1)}, f32[32,80,128]{2,1,0:T(8,128)}, u32[]{:S(2)}) copy-start(f32[32,80,128]{2,1,0:T(8,128)} %copy-done.23) | copy-start | bytes 3932164
  107.1 54.8 %all-to-all-start.1 = ((f32[32,75,128]{2,1,0:T(8,128)}), f32[32,75,128]{2,1,0:T(8,128)S(1)}, u32[]{:S(2)}, u32[]{:S(2)}) async-start(f32[32,75,128]{2,1,0:T(8,128)} %copy-done.22), calls=%async_computation.1 | async-start | bytes 2621440 | tf_op jit(solution)/shard_map/all_to_all | solution.py:546
  121.6 29.6 %copy-start.3 = (f32[40,80,128]{2,1,0:T(8,128)S(1)}, f32[40,80,128]{2,1,0:T(8,128)}, u32[]{:S(2)}) copy-start(f32[40,80,128]{2,1,0:T(8,128)} %copy-done.2) | copy-start | bytes 4915204
  136.6 14.6 %copy-start.1 = (f32[40,80,128]{2,1,0:T(8,128)S(1)}, f32[40,80,128]{2,1,0:T(8,128)}, u32[]{:S(2)}) copy-start(f32[40,80,128]{2,1,0:T(8,128)} %copy-done) | copy-start | bytes 4915204
  136.7 3.8 %collective-permute-start.6 = (f32[4,80,128]{2,1,0:T(8,128)S(1)}, f32[4,80,128]{2,1,0:T(8,128)S(1)}, u32[]{:S(2)}, u32[]{:S(2)}) collective-permute-start(f32[4,80,128]{2,1,0:T(8,128)S(1)} %get-tuple-element.44), channel_id=1, source_target_pairs={{0,1},{1,0},{2,3},{3,2},{4,5},{5,4},{6,7},{7,6},{8,9},{9,8},{10,11... | collective-permute-start | bytes 491528 | tf_op jit(solution)/shard_map/ppermute | solution.py:561
  137.0 7.1 %collective-permute-start.7 = (f32[4,80,128]{2,1,0:T(8,128)S(1)}, f32[4,80,128]{2,1,0:T(8,128)S(1)}, u32[]{:S(2)}, u32[]{:S(2)}) collective-permute-start(f32[4,80,128]{2,1,0:T(8,128)S(1)} %get-tuple-element.43), channel_id=1, source_target_pairs={{1,2},{2,1},{5,6},{6,5},{9,10},{10,9},{13,14},{14,13},{17,18},{18,... | collective-permute-start | bytes 491528 | tf_op jit(solution)/shard_map/ppermute | solution.py:562
  146.3 10.9 %collective-permute-start.8 = (f32[2,10,8,128]{3,2,1,0:T(8,128)S(1)}, f32[2,10,8,128]{3,2,1,0:T(8,128)S(1)}, u32[]{:S(2)}, u32[]{:S(2)}) collective-permute-start(f32[2,10,8,128]{3,2,1,0:T(8,128)S(1)} %get-tuple-element.36), channel_id=1, source_target_pairs={{0,4},{4,8},{8,12},{12,16},{16,20},{20,24},{24,28},{28,0},{1,5},{5... | collective-permute-start | bytes 245768 | tf_op jit(solution)/shard_map/ppermute | solution.py:555
  147.8 9.4 %copy-start.6 = (f32[32,80,128]{2,1,0:T(8,128)S(1)}, f32[32,80,128]{2,1,0:T(8,128)}, u32[]{:S(2)}) copy-start(f32[32,80,128]{2,1,0:T(8,128)} %copy-done.4) | copy-start | bytes 3932164
  147.8 9.4 %copy-start.9 = (f32[32,80,128]{2,1,0:T(8,128)S(1)}, f32[32,80,128]{2,1,0:T(8,128)}, u32[]{:S(2)}) copy-start(f32[32,80,128]{2,1,0:T(8,128)} %copy-done.7) | copy-start | bytes 3932164
  147.8 9.4 %copy-start.17 = (f32[2,2,2,40,8,128]{5,4,3,2,1,0:T(8,128)S(1)}, f32[2,2,2,40,8,128]{5,4,3,2,1,0:T(8,128)}, u32[]{:S(2)}) copy-start(f32[2,2,2,40,8,128]{5,4,3,2,1,0:T(8,128)} %copy-done.16) | copy-start | bytes 3932164
  147.8 9.4 %collective-permute-start.9 = (f32[2,10,8,128]{3,2,1,0:T(8,128)S(1)}, f32[2,10,8,128]{3,2,1,0:T(8,128)S(1)}, u32[]{:S(2)}, u32[]{:S(2)}) collective-permute-start(f32[2,10,8,128]{3,2,1,0:T(8,128)S(1)} %get-tuple-element.37), channel_id=1, source_target_pairs={{4,0},{8,4},{12,8},{16,12},{20,16},{24,20},{28,24},{0,28},{5,1},{9... | collective-permute-start | bytes 245768 | tf_op jit(solution)/shard_map/ppermute | solution.py:555
  (9 other events, 9.2 us)

commit v3 on v2

--- a/solution.py
+++ b/solution.py
@@ -198,8 +198,7 @@
 def stage_kernel(groups, levels, margin, control_ref, east_ref, north_ref, mask_ref, *outs):
     cols = control_ref.shape[2]
     refs = [ref.reshape(levels * LANES8, cols) for ref in (control_ref, east_ref, north_ref, mask_ref)]
-    block, last = pl.program_id(0), pl.num_programs(0) - 1
-    field_refs, (top_ref, bottom_ref, strip_ref) = outs[:4], outs[4:]
+    *field_refs, strip_ref = outs
     def step(g, _):
         start = group_start(g, levels)
         for r in range(LANES8):
@@ -221,14 +220,6 @@
                 strip_ref[f, 1, slab, pl.ds(at, count)] = east
         return 0
     lax.fori_loop(0, LANES8 // count, pack, 0)
-    @pl.when(block == 0)
-    def _():
-        for f in range(4):
-            bottom_ref[f * margin:(f + 1) * margin] = field_refs[f][0:margin]
-    @pl.when(block == last)
-    def _():
-        for f in range(4):
-            top_ref[f * margin:(f + 1) * margin] = field_refs[f][LANES8 - margin:LANES8]
 
 
 def stage(groups, margin, natural):
@@ -238,15 +229,15 @@
     natural = [pltpu.with_memory_space_constraint(x, pltpu.HBM) for x in natural]
     return pl.pallas_call(functools.partial(stage_kernel, groups, levels, margin),
         grid=(rows // LANES8,), name="stage",
-        out_shape=[jax.ShapeDtypeStruct((rows, depth, cols), F32)] * 4 + [jax.ShapeDtypeStruct((4 * margin, depth, cols), F32)] * 2
+        out_shape=[jax.ShapeDtypeStruct((rows, depth, cols), F32)] * 4
         + [jax.ShapeDtypeStruct((4, 2, slabs, rows, LANES8, 128), F32)],
         in_specs=[pl.BlockSpec((levels, LANES8, cols), lambda i: (0, i, 0))] * 4,
-        out_specs=[pl.BlockSpec((LANES8, depth, cols), lambda i: (i, 0, 0))] * 4 + [pl.BlockSpec((4 * margin, depth, cols), lambda i: (0, 0, 0))] * 2
+        out_specs=[pl.BlockSpec((LANES8, depth, cols), lambda i: (i, 0, 0))] * 4
         + [pl.BlockSpec((4, 2, slabs, LANES8, LANES8, 128), lambda i: (0, 0, 0, i, 0, 0))],
         compiler_params=params(16))(*natural)
 
 
-def sends_kernel(groups, levels, margin, control_ref, east_ref, north_ref, mask_ref, to_east, to_west):
+def sends_kernel(groups, levels, margin, odd_ref, control_ref, east_ref, north_ref, mask_ref, to_east, to_west, inner_ref, outer_ref):
     cols = control_ref.shape[2]
     refs = [ref.reshape(levels * LANES8, cols) for ref in (control_ref, east_ref, north_ref, mask_ref)]
     slabs, per = slabs_of(groups)
@@ -264,17 +255,34 @@
                     west_out = jnp.where(here, turn(x, margin * (4 * g + f)), west_out)
             to_east[slab, r] = east_out
             to_west[slab, r] = west_out
-
-
-def lon_sends(groups, margin, natural):
+    block, last = pl.program_id(0), pl.num_programs(0) - 1
+    odd = odd_ref[0]
+    def edge(out_ref, first):
+        def step(g, _):
+            start = group_start(g, levels)
+            for i in range(margin):
+                where = pl.ds(start * LANES8 + first + i, LANES8, stride=LANES8)
+                control, east, north, mask = (ref[where, :] for ref in refs)
+                mask = mask.astype(F32)
+                for f, x in enumerate((mask * control, mask, east, north)):
+                    out_ref[f * margin + i, lanes_of(g), :] = x
+            return 0
+        lax.fori_loop(0, groups, step, 0)
+    pl.when((block == 0) & (odd == 1))(lambda: edge(inner_ref, 0))
+    pl.when((block == 0) & (odd == 0))(lambda: edge(outer_ref, 0))
+    pl.when((block == last) & (odd == 0))(lambda: edge(inner_ref, LANES8 - margin))
+    pl.when((block == last) & (odd == 1))(lambda: edge(outer_ref, LANES8 - margin))
+
+
+def edge_sends(groups, margin, odd, natural):
     levels, rows, cols = natural[0].shape
     slabs, _ = slabs_of(groups)
     natural = [pltpu.with_memory_space_constraint(x, pltpu.HBM) for x in natural]
-    return pl.pallas_call(functools.partial(sends_kernel, groups, levels, margin), grid=(rows // LANES8,), name="lon_sends",
-        out_shape=[jax.ShapeDtypeStruct((slabs, rows, LANES8, 128), F32)] * 2,
-        in_specs=[pl.BlockSpec((levels, LANES8, cols), lambda i: (0, i, 0))] * 4,
-        out_specs=[pl.BlockSpec((slabs, LANES8, LANES8, 128), lambda i: (0, i, 0, 0))] * 2,
-        compiler_params=params(16))(*natural)
+    return pl.pallas_call(functools.partial(sends_kernel, groups, levels, margin), grid=(rows // LANES8,), name="edge_sends",
+        out_shape=[jax.ShapeDtypeStruct((slabs, rows, LANES8, 128), F32)] * 2 + [jax.ShapeDtypeStruct((4 * margin, LANES8 * groups, cols), F32)] * 2,
+        in_specs=[pl.BlockSpec(memory_space=pltpu.SMEM)] + [pl.BlockSpec((levels, LANES8, cols), lambda i: (0, i, 0))] * 4,
+        out_specs=[pl.BlockSpec((slabs, LANES8, LANES8, 128), lambda i: (0, i, 0, 0))] * 2 + [pl.BlockSpec((4 * margin, LANES8 * groups, cols), lambda i: (0, 0, 0))] * 2,
+        compiler_params=params(60))(odd, *natural)
 
 
 def rim_kernel(groups, margin, south_in, north_in, strip_ref):
@@ -443,34 +451,47 @@
         compiler_params=params(16))(*args)
 
 
-def strip_adjoint_kernel(groups, rows, margin, adjoint_ref, south_in, north_in, strip_ref, to_east, to_west):
+def strip_own_kernel(groups, rows, adjoint_ref, strip_ref):
+    slabs, per = slabs_of(groups)
+    def step(i, _):
+        for slab in range(slabs):
+            west, east = pack_strip(slab_load(adjoint_ref, 2 * i, 2, slab, per), min(per, groups - slab * per), 2, STEPS)
+            strip_ref[0, slab, pl.ds(2 * i, 2)] = west
+            strip_ref[1, slab, pl.ds(2 * i, 2)] = east
+        return 0
+    lax.fori_loop(0, rows // 2, step, 0)
+
+
+def strip_own(groups, rows, adjoint):
+    slabs, _ = slabs_of(groups)
+    return pl.pallas_call(functools.partial(strip_own_kernel, groups, rows), name="strip_own",
+        out_shape=jax.ShapeDtypeStruct((2, slabs, rows, LANES8, 128), F32),
+        in_specs=[WHOLE], out_specs=WHOLE, compiler_params=params(12))(adjoint)
+
+
+def strip_adjoint_kernel(groups, rows, margin, own_ref, south_in, north_in, strip_ref, to_east, to_west):
     quarter = (rows + 2 * margin) // 4
     slabs, per = slabs_of(groups)
-    def build(ref, i, at):
-        for slab in range(slabs):
-            west, east = pack_strip(slab_load(ref, i, 2, slab, per), min(per, groups - slab * per), 2, margin)
-            strip_ref[0, slab, pl.ds(at, 2)] = west
-            strip_ref[1, slab, pl.ds(at, 2)] = east
-    for i in range(0, margin, 2):
-        build(south_in, i, i)
-        build(north_in, i, i + margin + rows)
-    def inside(i, _):
-        build(adjoint_ref, 2 * i, 2 * i + margin)
-        return 0
-    lax.fori_loop(0, rows // 2, inside, 0)
     for slab in range(slabs):
+        for ref, at in ((south_in, 0), (north_in, margin + rows)):
+            west, east = pack_strip(slab_load(ref, 0, margin, slab, per), min(per, groups - slab * per), margin, margin)
+            strip_ref[0, slab, at:at + margin] = west
+            strip_ref[1, slab, at:at + margin] = east
+        for side in range(2):
+            for at in range(0, rows, LANES8):
+                strip_ref[side, slab, margin + at:margin + at + LANES8] = own_ref[side, slab, at:at + LANES8]
         for at in range(0, quarter, 2):
             here = [slice(at + q * quarter, at + q * quarter + 2) for q in range(4)]
             sends = pack_sends([(strip_ref[0, slab, s], strip_ref[1, slab, s]) for s in here], 2, margin)
             to_east[slab, at:at + 2], to_west[slab, at:at + 2] = sends
 
 
-def strip_adjoint(groups, rows, margin, adjoint, south_in, north_in):
+def strip_adjoint(groups, rows, margin, own, south_in, north_in):
     tall = rows + 2 * margin
     slabs, _ = slabs_of(groups)
     return pl.pallas_call(functools.partial(strip_adjoint_kernel, groups, rows, margin),
         out_shape=[jax.ShapeDtypeStruct((2, slabs, tall, LANES8, 128), F32)] + [jax.ShapeDtypeStruct((slabs, tall // 4, LANES8, 128), F32)] * 2,
-        in_specs=[WHOLE] * 3, out_specs=[WHOLE] * 3, name="strip_adjoint", compiler_params=params(12))(adjoint, south_in, north_in)
+        in_specs=[WHOLE] * 3, out_specs=[WHOLE] * 3, name="strip_adjoint", compiler_params=params(12))(own, south_in, north_in)
 
 
 def finish_kernel(groups, levels, rows, margin, tiles_ref, strip_ref, from_west, from_east, faces_ref, u_ref, mask_ref, out_ref, strip_a, strip_b, rim):
@@ -555,12 +576,16 @@
     return lax.ppermute(forth, axis, up), lax.ppermute(back, axis, [(j, i) for i, j in up])
 
 
-def swap_edges(axis, forth, back):
+def swap_rounds(axis, inner, outer):
     size, odd = lax.axis_size(axis), lax.axis_index(axis) % 2 == 1
     rounds = [[pair for i in range(first, size - 1, 2) for pair in ((i, i + 1), (i + 1, i))] for first in range(2)]
-    inner = lax.ppermute(jnp.where(odd, back, forth), axis, rounds[0])
-    outer = lax.ppermute(jnp.where(odd, forth, back), axis, rounds[1])
+    inner, outer = lax.ppermute(inner, axis, rounds[0]), lax.ppermute(outer, axis, rounds[1])
     return jnp.where(odd, inner, outer), jnp.where(odd, outer, inner)
+
+
+def swap_edges(axis, forth, back):
+    odd = lax.axis_index(axis) % 2 == 1
+    return swap_rounds(axis, jnp.where(odd, back, forth), jnp.where(odd, forth, back))
 
 
 def body(
@@ -582,13 +607,14 @@
     live = (slot_counts[0][:, None] > jnp.arange(capacity)[None, :]).astype(jnp.int32).reshape(1, slots)
     groups = -(-levels // 16) * 2
     natural = (control, east_coeff, north_coeff, ocean_mask)
-    to_east, to_west = lon_sends(groups, margin, natural)
+    odd = (lax.axis_index("gy") % 2).astype(jnp.int32).reshape(1)
+    to_east, to_west, inner, outer = edge_sends(groups, margin, odd, natural)
     from_west, from_east = pass_around("gx", to_east, to_west)
+    south_in, north_in = swap_rounds("gy", inner, outer)
     obs = obs_blocks(obs_value, obs_precision, live)
     obs, *_ = lax.optimization_barrier((obs, to_east, to_west))
     obs = exchange(obs, share)
-    *fields, top, bottom, strip = stage(groups, margin, natural)
-    south_in, north_in = swap_edges("gy", top, bottom)
+    *fields, strip = stage(groups, margin, natural)
     corners = jnp.stack([from_west, from_east])
     south_corners, north_corners = swap_edges("gy", corners[:, :, rows - margin:], corners[:, :, :margin])
     rims = strip_rims(groups, margin, south_in, north_in)
@@ -600,7 +626,8 @@
     sent = exchange(out, share)
     adjoint = scatter(corner_cells, corner_weights, back, rows, cols)
     south_in, north_in = swap_edges("gy", adjoint[rows - margin:], adjoint[:margin])
-    strip, to_east, to_west = strip_adjoint(groups, rows, margin, adjoint, south_in, north_in)
+    own = strip_own(groups, rows, adjoint)
+    strip, to_east, to_west = strip_adjoint(groups, rows, margin, own, south_in, north_in)
     from_west, from_east = pass_around("gx", to_east, to_west)
     departures = place_departures(sent)
     swept = tiles(groups, rows, margin, adjoint, south_in, north_in, e, n)

time: 164 us -> 166 us (1.012)
  waiting for transfers between devices: 32.6 us -> 44.1 us
  local copies, waits for them, and re-layouts: 17.4 us -> 7.22 us
    ppermute x2, waiting for transfers between devices: 27 us -> 42.3 us  [pass_around(): lax.ppermute(forth, axis, up)]
    unnamed x58 -> x42, local copies, waits for them, and re-layouts: 17.4 us -> 7.22 us
    ppermute x6, waiting for transfers between devices: 5.66 us -> 1.77 us  [the longest x3 1.76 us: swap_rounds(): lax.ppermute(outer, axis, rounds[1])]
    pallas_call x1 -> x2, Pallas kernels: 4.87 us -> 8.11 us  [the longest x1 6.35 us: edge_sends(): pl.pallas_call(functools.partial(sends_kernel, groups, levels, margin), g...]
    pallas_call x1, Pallas kernels: 2.17 us -> 0.41 us  [strip_adjoint(): pl.pallas_call(functools.partial(strip_adjoint_kernel, groups, rows, marg...]
  transfers between devices with their start and end apart: 12 -> 12, of which waited for: 3 -> 2; matrix products, arithmetic and copies ran while one was open for 1% -> 1% of each run, Pallas kernels for 36% -> 35%
where the time goes in v3:
time: 166 us; the launch traced here: 165 us
  Pallas kernels  67.6 us (41%)
  waiting for transfers between devices  44.1 us (27%)
  starting transfers between devices  42.2 us (25%)
  local copies, waits for them, and re-layouts  7.22 us (4%)
  other arithmetic  3.06 us (2%)
    ppermute x2, waiting for transfers between devices, pass_around(): lax.ppermute(forth, axis, up)  42.3 us
    all_to_all x2, starting transfers between devices, exchange(): values = lax.all_to_all(values, ('gx', 'gy'), 0, 0, tiled=True)  20.2 us
    pallas_call x1, Pallas kernels, scatter(): pl.pallas_call(functools.partial(scatter_kernel, rows, lev, cols, nb), ou...  15 us
    pallas_call x1, Pallas kernels, gather(): pl.pallas_call(functools.partial(gather_kernel, rows, lev, cols, nb, marg...  13.3 us
    pallas_call x2, Pallas kernels, tiles(): pl.pallas_call(functools.partial(tiles_kernel, groups, rows, margin), out...  12 us
    ppermute x3, starting transfers between devices, swap_rounds(): lax.ppermute(outer, axis, rounds[1])  10.7 us
    unnamed x42, local copies, waits for them, and re-layouts  7.22 us
    pallas_call x1, Pallas kernels, stage(): pl.pallas_call(functools.partial(stage_kernel, groups, levels, margin), g...  6.39 us
  transfers between devices with their start and end apart: 12, of which 2 were waited for; matrix products, arithmetic and copies ran while one was open for 1% of the time, Pallas kernels for 35%

profile of v3, /device:TPU:1, one launch (start us, length us, event | category | flops | bytes accessed | tf_op | source)
XLA Modules:
  0.0 165.3 jit_solution(15839090869756412769)
XLA Ops:
  1.4 1.3 copy-done.10
  2.7 1.3 copy-done.11
  4.0 1.9 %obs_blocks.1 = f32[32,152,128]{2,1,0:T(8,128)} custom-call(f32[75,4096]{1,0:T(8,128)S(1)} %copy-done.10, f32[75,4096]{1,0:T(8,128)S(1)} %copy-done.11, s32[1,4096]{1,0:T(1,128)S(1)} %bitcast.8), custom_call_target="tpu_custom_call" | custom-call | tf_op jit(solution)/shard_map/obs_blocks/pallas_call | solution.py:145
  5.9 6.3 %edge_sends.1 = (f32[2,32,8,128]{3,2,1,0:T(8,128)}, f32[2,32,8,128]{3,2,1,0:T(8,128)}, f32[16,80,128]{2,1,0:T(8,128)}, f32[16,80,128]{2,1,0:T(8,128)}) custom-call(s32[1]{0:T(128)} %bitcast.odd_ref, f32[75,32,128]{2,1,0:T(8,128)} %control_ref.3, f32[75,32,128]{2,1,0:T(8,128)} %east_ref.3, f32[75,32,128]{2,1,0:T(8,128)} %north_ref.3, s32[75,32,128]{2,1,0:T(8,128)} %mask_ref.3), custom_call_target="tpu_custom_call" | custom-call | tf_op jit(solution)/shard_map/edge_sends/pallas_call | solution.py:281
  12.3 7.1 %all-to-all-start = ((f32[32,152,128]{2,1,0:T(8,128)}), f32[32,152,128]{2,1,0:T(8,128)S(1)}, u32[]{:S(2)}, u32[]{:S(2)}) async-start(f32[32,152,128]{2,1,0:T(8,128)} %obs_blocks.1), calls=%async_computation | async-start | bytes 4980736 | tf_op jit(solution)/shard_map/all_to_all | solution.py:567
  19.4 1.4 collective-permute-start.2
  20.8 2.8 %collective-permute-start.3 = (f32[2,32,8,128]{3,2,1,0:T(8,128)S(1)}, f32[2,32,8,128]{3,2,1,0:T(8,128)S(1)}, u32[]{:S(2)}, u32[]{:S(2)}) collective-permute-start(f32[2,32,8,128]{3,2,1,0:T(8,128)S(1)} %copy-done.19), channel_id=1, source_target_pairs={{4,0},{8,4},{12,8},{16,12},{20,16},{24,20},{28,24},{0,28},{5,1},{9... | collective-permute-start | bytes 786440 | tf_op jit(solution)/shard_map/ppermute | solution.py:576
  23.6 0.8 collective-permute-start
  24.4 3.3 %collective-permute-start.1 = (f32[16,80,128]{2,1,0:T(8,128)}, f32[16,80,128]{2,1,0:T(8,128)}, u32[]{:S(2)}, u32[]{:S(2)}) collective-permute-start(f32[16,80,128]{2,1,0:T(8,128)} %get-tuple-element.23), channel_id=1, source_target_pairs={{1,2},{2,1},{5,6},{6,5},{9,10},{10,9},{13,14},{14,13},{17,18},{18,... | collective-permute-start | bytes 1966088 | tf_op jit(solution)/shard_map/ppermute | solution.py:582
  27.7 42.3 %collective-permute-done.2.from_west = f32[2,32,8,128]{3,2,1,0:T(8,128)S(1)} collective-permute-done((f32[2,32,8,128]{3,2,1,0:T(8,128)S(1)}, f32[2,32,8,128]{3,2,1,0:T(8,128)S(1)}, u32[]{:S(2)}, u32[]{:S(2)}) %collective-permute-start.2) | collective-permute-done | bytes 262176 | tf_op jit(solution)/shard_map/ppermute | solution.py:576
  70.1 1.0 collective-permute-start.4
  71.1 3.8 %collective-permute-start.5 = (f32[2,2,4,8,128]{4,3,2,1,0:T(8,128)S(1)}, f32[2,2,4,8,128]{4,3,2,1,0:T(8,128)S(1)}, u32[]{:S(2)}, u32[]{:S(2)}) collective-permute-start(f32[2,2,4,8,128]{4,3,2,1,0:T(8,128)S(1)} %get-tuple-element.40), channel_id=1, source_target_pairs={{1,2},{2,1},{5,6},{6,5},{9,10},{10,9},{13,14},{14,13},{17,18},{18,... | collective-permute-start | bytes 196616 | tf_op jit(solution)/shard_map/ppermute | solution.py:582
  75.0 6.4 %stage.1 = (f32[32,80,128]{2,1,0:T(8,128)S(1)}, f32[32,80,128]{2,1,0:T(8,128)S(1)}, f32[32,80,128]{2,1,0:T(8,128)S(1)}, f32[32,80,128]{2,1,0:T(8,128)S(1)}, f32[4,2,2,32,8,128]{5,4,3,2,1,0:T(8,128)S(1)}) custom-call(f32[75,32,128]{2,1,0:T(8,128)} %control_ref.3, f32[75,32,128]{2,1,0:T(8,128)} %east_ref.3, f32[75,32,128]{2,1,0:T(8,128)} %north_ref.3, ...), custom_call_target="tpu_custom_call" | custom-call | tf_op jit(solution)/shard_map/stage/pallas_call | solution.py:230
  81.4 2.2 %broadcast_select_fusion = (f32[16,80,128]{2,1,0:T(8,128)S(1)}, f32[16,80,128]{2,1,0:T(8,128)S(1)}) fusion(f32[16,80,128]{2,1,0:T(8,128)} %collective-permute-done.1, f32[16,80,128]{2,1,0:T(8,128)} %collective-permute-done, pred[]{:T(512)S(6)} %eq.14), kind=kLoop, calls=%fused_computation | loop fusion | flops 327680 | bytes 2621441 | tf_op jit(solution)/shard_map/jit(_where)/select_n | solution.py:583
  84.5 1.1 faces.1
  85.6 2.6 %forward_strips.1 = (f32[2,32,8,128]{3,2,1,0:T(8,128)S(1)}, f32[2,2,2,40,8,128]{5,4,3,2,1,0:T(8,128)S(1)}) custom-call(f32[4,2,2,32,8,128]{5,4,3,2,1,0:T(8,128)S(1)} %get-tuple-element.29.strip_ref, f32[2,32,8,128]{3,2,1,0:T(8,128)S(1)} %collective-permute-done.2.from_west, f32[2,32,8,128]{3,2,1,0:T(8,128)S(1)} %collective-permute-done.3.from_east, ...), custom_call_target="tpu_custom_call" | custom-call | tf_op jit(solution)/shard_map/forward_strips/pallas_call | solution.py:447
  88.3 6.0 %tiles.2.bg_ref = f32[32,80,128]{2,1,0:T(8,128)S(1)} custom-call(f32[32,80,128]{2,1,0:T(8,128)S(1)} %get-tuple-element.21.u_ref, f32[16,80,128]{2,1,0:T(8,128)S(1)} %get-tuple-element.46.south_in, f32[16,80,128]{2,1,0:T(8,128)S(1)} %get-tuple-element.45.north_in, f32[40,80,128]{2,1,0:T(8,128)S(1)} %get-tuple-element.27.e_ref, ...), custom_call_target="tpu_custom_call" | custom-call | flops 13107200 | bytes 6553600 | tf_op jit(solution)/shard_map/tiles/pallas_call | solution.py:400
  94.3 13.3 %gather.1.equivalent_ref = f32[32,80,128]{2,1,0:T(8,128)S(1)} custom-call(s32[4,4096]{1,0:T(4,128)S(1)} %copy-done.17, f32[4,4096]{1,0:T(4,128)S(1)} %copy-done.18, f32[32,80,128]{2,1,0:T(8,128)S(1)} %tiles.2.bg_ref, f32[2,32,8,128]{3,2,1,0:T(8,128)S(1)} %get-tuple-element.32.rim_ref), custom_call_target="tpu_custom_call" | custom-call | tf_op jit(solution)/shard_map/gather/pallas_call | solution.py:71
  107.6 1.0 copy-done.8
  108.7 1.3 copy-done.9
  110.3 1.1 copy-done.14
  111.4 1.1 copy-done.15
  112.4 13.1 %all-to-all-start.1 = ((f32[32,75,128]{2,1,0:T(8,128)}), f32[32,75,128]{2,1,0:T(8,128)S(1)}, u32[]{:S(2)}, u32[]{:S(2)}) async-start(f32[32,75,128]{2,1,0:T(8,128)} %copy-done.14), calls=%async_computation.1 | async-start | bytes 2621440 | tf_op jit(solution)/shard_map/all_to_all | solution.py:567
  125.6 15.0 %scatter.1.u_ref.adjoint_ref = f32[32,80,128]{2,1,0:T(8,128)S(1)} custom-call(s32[4,4096]{1,0:T(4,128)S(1)} %copy-done.17, f32[4,4096]{1,0:T(4,128)S(1)} %copy-done.18, f32[32,80,128]{2,1,0:T(8,128)S(1)} %copy-done.16), custom_call_target="tpu_custom_call" | custom-call | tf_op jit(solution)/shard_map/scatter/pallas_call | solution.py:111
  141.0 3.6 %collective-permute-start.7 = (f32[4,80,128]{2,1,0:T(8,128)S(1)}, f32[4,80,128]{2,1,0:T(8,128)S(1)}, u32[]{:S(2)}, u32[]{:S(2)}) collective-permute-start(f32[4,80,128]{2,1,0:T(8,128)S(1)} %get-tuple-element.43), channel_id=1, source_target_pairs={{1,2},{2,1},{5,6},{6,5},{9,10},{10,9},{13,14},{14,13},{17,18},{18,... | collective-permute-start | bytes 491528 | tf_op jit(solution)/shard_map/ppermute | solution.py:582
  144.6 1.8 %strip_own.1.own_ref = f32[2,2,32,8,128]{4,3,2,1,0:T(8,128)S(1)} custom-call(f32[32,80,128]{2,1,0:T(8,128)S(1)} %scatter.1.u_ref.adjoint_ref), custom_call_target="tpu_custom_call" | custom-call | tf_op jit(solution)/shard_map/strip_own/pallas_call | solution.py:467
  146.4 1.8 %collective-permute-done.7 = f32[4,80,128]{2,1,0:T(8,128)S(1)} collective-permute-done((f32[4,80,128]{2,1,0:T(8,128)S(1)}, f32[4,80,128]{2,1,0:T(8,128)S(1)}, u32[]{:S(2)}, u32[]{:S(2)}) %collective-permute-start.7) | collective-permute-done | bytes 163872 | tf_op jit(solution)/shard_map/ppermute | solution.py:582
  148.6 1.5 collective-permute-start.8
  150.1 3.3 %collective-permute-start.9 = (f32[2,10,8,128]{3,2,1,0:T(8,128)S(1)}, f32[2,10,8,128]{3,2,1,0:T(8,128)S(1)}, u32[]{:S(2)}, u32[]{:S(2)}) collective-permute-start(f32[2,10,8,128]{3,2,1,0:T(8,128)S(1)} %get-tuple-element.37), channel_id=1, source_target_pairs={{4,0},{8,4},{12,8},{16,12},{20,16},{24,20},{28,24},{0,28},{5,1},{9... | collective-permute-start | bytes 245768 | tf_op jit(solution)/shard_map/ppermute | solution.py:576
  153.4 6.0 %tiles.3.tiles_ref = f32[32,80,128]{2,1,0:T(8,128)S(1)} custom-call(f32[32,80,128]{2,1,0:T(8,128)S(1)} %scatter.1.u_ref.adjoint_ref, f32[4,80,128]{2,1,0:T(8,128)S(1)} %get-tuple-element.48.south_in, f32[4,80,128]{2,1,0:T(8,128)S(1)} %get-tuple-element.47.north_in, f32[40,80,128]{2,1,0:T(8,128)S(1)} %copy-done.1, f32[40,80,128]{2,1,0:T(8,128)S(1)} %copy-done.3), custom_call_target="tpu_custom_call" | custom-call | flops 13107200 | bytes 6553600 | tf_op jit(solution)/shard_map/tiles/pallas_call | solution.py:400
  159.5 4.6 %finish.1 = f32[2400,128]{1,0:T(8,128)} custom-call(f32[32,80,128]{2,1,0:T(8,128)S(1)} %tiles.3.tiles_ref, f32[2,2,40,8,128]{4,3,2,1,0:T(8,128)S(1)} %get-tuple-element.35.strip_ref, f32[2,10,8,128]{3,2,1,0:T(8,128)S(1)} %collective-permute-done.8.from_west, f32[2,10,8,128]{3,2,1,0:T(8,128)S(1)} %collective-permute-done.9.from_east, ...), custom_call_target="tpu_custom_call" | custom-call | tf_op jit(solution)/shard_map/finish/pallas_call | solution.py:523
  164.1 1.2 place_departures.1
  (56 shorter events, 2.7 us)
Async XLA Ops:
  1.4 1.3 copy-start.10
  2.7 1.3 copy-start.11
  12.3 7.1 %copy-start.20 = (f32[2,32,8,128]{3,2,1,0:T(8,128)S(1)}, f32[2,32,8,128]{3,2,1,0:T(8,128)}, u32[]{:S(2)}) copy-start(f32[2,32,8,128]{3,2,1,0:T(8,128)} %get-tuple-element.30) | copy-start | bytes 786436
  12.3 8.5 %copy-start.19 = (f32[2,32,8,128]{3,2,1,0:T(8,128)S(1)}, f32[2,32,8,128]{3,2,1,0:T(8,128)}, u32[]{:S(2)}) copy-start(f32[2,32,8,128]{3,2,1,0:T(8,128)} %get-tuple-element.31) | copy-start | bytes 786436
  12.3 96.4 %all-to-all-start = ((f32[32,152,128]{2,1,0:T(8,128)}), f32[32,152,128]{2,1,0:T(8,128)S(1)}, u32[]{:S(2)}, u32[]{:S(2)}) async-start(f32[32,152,128]{2,1,0:T(8,128)} %obs_blocks.1), calls=%async_computation | async-start | bytes 4980736 | tf_op jit(solution)/shard_map/all_to_all | solution.py:567
  19.4 50.7 %collective-permute-start.2 = (f32[2,32,8,128]{3,2,1,0:T(8,128)S(1)}, f32[2,32,8,128]{3,2,1,0:T(8,128)S(1)}, u32[]{:S(2)}, u32[]{:S(2)}) collective-permute-start(f32[2,32,8,128]{3,2,1,0:T(8,128)S(1)} %copy-done.20), channel_id=1, source_target_pairs={{0,4},{4,8},{8,12},{12,16},{16,20},{20,24},{24,28},{28,0},{1,5},{5... | collective-permute-start | bytes 786440 | tf_op jit(solution)/shard_map/ppermute | solution.py:576
  20.8 49.3 %collective-permute-start.3 = (f32[2,32,8,128]{3,2,1,0:T(8,128)S(1)}, f32[2,32,8,128]{3,2,1,0:T(8,128)S(1)}, u32[]{:S(2)}, u32[]{:S(2)}) collective-permute-start(f32[2,32,8,128]{3,2,1,0:T(8,128)S(1)} %copy-done.19), channel_id=1, source_target_pairs={{4,0},{8,4},{12,8},{16,12},{20,16},{24,20},{28,24},{0,28},{5,1},{9... | collective-permute-start | bytes 786440 | tf_op jit(solution)/shard_map/ppermute | solution.py:576
  23.6 57.8 %collective-permute-start = (f32[16,80,128]{2,1,0:T(8,128)}, f32[16,80,128]{2,1,0:T(8,128)}, u32[]{:S(2)}, u32[]{:S(2)}) collective-permute-start(f32[16,80,128]{2,1,0:T(8,128)} %get-tuple-element.22), channel_id=1, source_target_pairs={{0,1},{1,0},{2,3},{3,2},{4,5},{5,4},{6,7},{7,6},{8,9},{9,8},{10,11... | collective-permute-start | bytes 1966088 | tf_op jit(solution)/shard_map/ppermute | solution.py:582
  24.4 57.0 %collective-permute-start.1 = (f32[16,80,128]{2,1,0:T(8,128)}, f32[16,80,128]{2,1,0:T(8,128)}, u32[]{:S(2)}, u32[]{:S(2)}) collective-permute-start(f32[16,80,128]{2,1,0:T(8,128)} %get-tuple-element.23), channel_id=1, source_target_pairs={{1,2},{2,1},{5,6},{6,5},{9,10},{10,9},{13,14},{14,13},{17,18},{18,... | collective-permute-start | bytes 1966088 | tf_op jit(solution)/shard_map/ppermute | solution.py:582
  70.1 11.3 %collective-permute-start.4 = (f32[2,2,4,8,128]{4,3,2,1,0:T(8,128)S(1)}, f32[2,2,4,8,128]{4,3,2,1,0:T(8,128)S(1)}, u32[]{:S(2)}, u32[]{:S(2)}) collective-permute-start(f32[2,2,4,8,128]{4,3,2,1,0:T(8,128)S(1)} %broadcast_select_fusion.7), channel_id=1, source_target_pairs={{0,1},{1,0},{2,3},{3,2},{4,5},{5,4},{6,7},{7,6},{8,9},{9,8},{10,11... | collective-permute-start | bytes 196616 | tf_op jit(solution)/shard_map/ppermute | solution.py:582
  71.1 10.3 %collective-permute-start.5 = (f32[2,2,4,8,128]{4,3,2,1,0:T(8,128)S(1)}, f32[2,2,4,8,128]{4,3,2,1,0:T(8,128)S(1)}, u32[]{:S(2)}, u32[]{:S(2)}) collective-permute-start(f32[2,2,4,8,128]{4,3,2,1,0:T(8,128)S(1)} %get-tuple-element.40), channel_id=1, source_target_pairs={{1,2},{2,1},{5,6},{6,5},{9,10},{10,9},{13,14},{14,13},{17,18},{18,... | collective-permute-start | bytes 196616 | tf_op jit(solution)/shard_map/ppermute | solution.py:582
  81.4 3.1 %copy-start.6 = (f32[32,80,128]{2,1,0:T(8,128)}, f32[32,80,128]{2,1,0:T(8,128)S(1)}, u32[]{:S(2)}) copy-start(f32[32,80,128]{2,1,0:T(8,128)S(1)} %get-tuple-element.24.mask_ref) | copy-start | bytes 3932164
  81.4 6.8 %copy-start.4 = (f32[32,80,128]{2,1,0:T(8,128)}, f32[32,80,128]{2,1,0:T(8,128)S(1)}, u32[]{:S(2)}) copy-start(f32[32,80,128]{2,1,0:T(8,128)S(1)} %get-tuple-element.21.u_ref) | copy-start | bytes 3932164
  85.6 2.6 %copy-start = (f32[40,80,128]{2,1,0:T(8,128)}, f32[40,80,128]{2,1,0:T(8,128)S(1)}, u32[]{:S(2)}) copy-start(f32[40,80,128]{2,1,0:T(8,128)S(1)} %get-tuple-element.27.e_ref) | copy-start | bytes 4915204
  85.6 2.6 %copy-start.2 = (f32[40,80,128]{2,1,0:T(8,128)}, f32[40,80,128]{2,1,0:T(8,128)S(1)}, u32[]{:S(2)}) copy-start(f32[40,80,128]{2,1,0:T(8,128)S(1)} %get-tuple-element.28.n_ref) | copy-start | bytes 4915204
  88.2 6.1 %copy-start.12 = (f32[2,2,2,40,8,128]{5,4,3,2,1,0:T(8,128)}, f32[2,2,2,40,8,128]{5,4,3,2,1,0:T(8,128)S(1)}, u32[]{:S(2)}) copy-start(f32[2,2,2,40,8,128]{5,4,3,2,1,0:T(8,128)S(1)} %get-tuple-element.38.faces_ref) | copy-start | bytes 3932164
  88.2 6.0 %copy-start.17 = (s32[4,4096]{1,0:T(4,128)S(1)}, s32[4,4096]{1,0:T(4,128)}, u32[]{:S(2)}) copy-start(s32[4,4096]{1,0:T(4,128)} %cells_ref.3) | copy-start | bytes 196612
  88.2 6.0 %copy-start.18 = (f32[4,4096]{1,0:T(4,128)S(1)}, f32[4,4096]{1,0:T(4,128)}, u32[]{:S(2)}) copy-start(f32[4,4096]{1,0:T(4,128)} %weights_ref.3) | copy-start | bytes 196612
  107.6 1.1 copy-start.8
  108.7 1.3 copy-start.9
  110.3 1.1 copy-start.14
  112.4 13.2 %copy-start.16 = (f32[32,80,128]{2,1,0:T(8,128)S(1)}, f32[32,80,128]{2,1,0:T(8,128)}, u32[]{:S(2)}) copy-start(f32[32,80,128]{2,1,0:T(8,128)} %copy-done.15) | copy-start | bytes 3932164
  112.4 51.7 %all-to-all-start.1 = ((f32[32,75,128]{2,1,0:T(8,128)}), f32[32,75,128]{2,1,0:T(8,128)S(1)}, u32[]{:S(2)}, u32[]{:S(2)}) async-start(f32[32,75,128]{2,1,0:T(8,128)} %copy-done.14), calls=%async_computation.1 | async-start | bytes 2621440 | tf_op jit(solution)/shard_map/all_to_all | solution.py:567
  140.6 5.7 %collective-permute-start.6 = (f32[4,80,128]{2,1,0:T(8,128)S(1)}, f32[4,80,128]{2,1,0:T(8,128)S(1)}, u32[]{:S(2)}, u32[]{:S(2)}) collective-permute-start(f32[4,80,128]{2,1,0:T(8,128)S(1)} %get-tuple-element.44), channel_id=1, source_target_pairs={{0,1},{1,0},{2,3},{3,2},{4,5},{5,4},{6,7},{7,6},{8,9},{9,8},{10,11... | collective-permute-start | bytes 491528 | tf_op jit(solution)/shard_map/ppermute | solution.py:582
  141.0 12.5 %copy-start.1 = (f32[40,80,128]{2,1,0:T(8,128)S(1)}, f32[40,80,128]{2,1,0:T(8,128)}, u32[]{:S(2)}) copy-start(f32[40,80,128]{2,1,0:T(8,128)} %copy-done) | copy-start | bytes 4915204
  141.0 12.5 %copy-start.3 = (f32[40,80,128]{2,1,0:T(8,128)S(1)}, f32[40,80,128]{2,1,0:T(8,128)}, u32[]{:S(2)}) copy-start(f32[40,80,128]{2,1,0:T(8,128)} %copy-done.2) | copy-start | bytes 4915204
  141.0 7.2 %collective-permute-start.7 = (f32[4,80,128]{2,1,0:T(8,128)S(1)}, f32[4,80,128]{2,1,0:T(8,128)S(1)}, u32[]{:S(2)}, u32[]{:S(2)}) collective-permute-start(f32[4,80,128]{2,1,0:T(8,128)S(1)} %get-tuple-element.43), channel_id=1, source_target_pairs={{1,2},{2,1},{5,6},{6,5},{9,10},{10,9},{13,14},{14,13},{17,18},{18,... | collective-permute-start | bytes 491528 | tf_op jit(solution)/shard_map/ppermute | solution.py:582
  148.6 10.8 %collective-permute-start.8 = (f32[2,10,8,128]{3,2,1,0:T(8,128)S(1)}, f32[2,10,8,128]{3,2,1,0:T(8,128)S(1)}, u32[]{:S(2)}, u32[]{:S(2)}) collective-permute-start(f32[2,10,8,128]{3,2,1,0:T(8,128)S(1)} %get-tuple-element.36), channel_id=1, source_target_pairs={{0,4},{4,8},{8,12},{12,16},{16,20},{20,24},{24,28},{28,0},{1,5},{5... | collective-permute-start | bytes 245768 | tf_op jit(solution)/shard_map/ppermute | solution.py:576
  150.1 9.3 %copy-start.5 = (f32[32,80,128]{2,1,0:T(8,128)S(1)}, f32[32,80,128]{2,1,0:T(8,128)}, u32[]{:S(2)}) copy-start(f32[32,80,128]{2,1,0:T(8,128)} %copy-done.4) | copy-start | bytes 3932164
  150.1 9.3 %copy-start.7 = (f32[32,80,128]{2,1,0:T(8,128)S(1)}, f32[32,80,128]{2,1,0:T(8,128)}, u32[]{:S(2)}) copy-start(f32[32,80,128]{2,1,0:T(8,128)} %copy-done.6) | copy-start | bytes 3932164
  150.1 9.3 %copy-start.13 = (f32[2,2,2,40,8,128]{5,4,3,2,1,0:T(8,128)S(1)}, f32[2,2,2,40,8,128]{5,4,3,2,1,0:T(8,128)}, u32[]{:S(2)}) copy-start(f32[2,2,2,40,8,128]{5,4,3,2,1,0:T(8,128)} %copy-done.12) | copy-start | bytes 3932164
  150.1 9.3 %collective-permute-start.9 = (f32[2,10,8,128]{3,2,1,0:T(8,128)S(1)}, f32[2,10,8,128]{3,2,1,0:T(8,128)S(1)}, u32[]{:S(2)}, u32[]{:S(2)}) collective-permute-start(f32[2,10,8,128]{3,2,1,0:T(8,128)S(1)} %get-tuple-element.37), channel_id=1, source_target_pairs={{4,0},{8,4},{12,8},{16,12},{20,16},{24,20},{28,24},{0,28},{5,1},{9... | collective-permute-start | bytes 245768 | tf_op jit(solution)/shard_map/ppermute | solution.py:576
  (1 other events, 1.1 us)

commit v4 on v3

--- a/solution.py
+++ b/solution.py
@@ -9,6 +9,7 @@
 
 
 F32, BF16 = jnp.float32, jnp.bfloat16
+TOGETHER = 2
 VMEM = pltpu.VMEM
 STEPS = 4
 LANES8 = 8
@@ -77,43 +78,52 @@
     )(cells, weights, bg, rim)
 
 
+def spread_levels(x, lev):
+    levels = x.shape[0]
+    full = levels // 8 * 8
+    parts = [x[:full]] + ([x[levels - 8:]] if levels > full else [])
+    short = lev - sum(p.shape[0] for p in parts)
+    return jnp.concatenate(parts + ([jnp.zeros((short, x.shape[1]), x.dtype)] if short else []), 0)
+
+
 def scatter_kernel(rows, lev, cols, nb, cells_ref, weights_ref, back_ref, out_ref, x, acc):
     blk = 256
     acc[...] = jnp.zeros_like(acc)
-    def step(jb, _):
+    def prepare(jb, column):
         r, s, east, west, north, south = hats(cells_ref, weights_ref, pl.multiple_of(jb * blk, blk), blk, cols)
         hi, lo = split2(hat(s, west, east, cols))
         right = jnp.concatenate([hi, lo], 0)
-        back = jnp.concatenate([back_ref[2 * jb], back_ref[2 * jb + 1]], 1)
+        back = jnp.concatenate([spread_levels(back_ref[2 * jb], lev), spread_levels(back_ref[2 * jb + 1], lev)], 1)
         u_hi, u_lo = split2(back * south)
         v_hi, v_lo = split2(back * north)
         one = hat(r, 1.0, 0.0, rows + 1).astype(BF16)
         for q in range(rows):
             at = jnp.broadcast_to(one[q:q + 1, :], (lev, blk))
+            high, low = u_hi * at, u_lo * at
             if q:
                 below = jnp.broadcast_to(one[q - 1:q, :], (lev, blk))
-                x[q * lev:(q + 1) * lev, 0:blk] = u_hi * at + v_hi * below
-                x[q * lev:(q + 1) * lev, blk:] = u_lo * at + v_lo * below
-            else:
-                x[0:lev, 0:blk] = u_hi * at
-                x[0:lev, blk:] = u_lo * at
-        acc[...] += lax.dot_general(x[...], jnp.concatenate([right, right], 1), (((1,), (1,)), ((), ())), preferred_element_type=F32)
-        return 0
-    lax.fori_loop(0, nb, step, 0)
+                high, low = high + v_hi * below, low + v_lo * below
+            x[q * lev:(q + 1) * lev, column:column + blk] = high
+            x[q * lev:(q + 1) * lev, column + blk:column + 2 * blk] = low
+        return jnp.concatenate([right, right], 1)
+    def step(i, _):
+        right = jnp.concatenate([prepare(TOGETHER * i + t, 512 * t) for t in range(TOGETHER)], 1)
+        acc[...] += lax.dot_general(x[...], right, (((1,), (1,)), ((), ())), preferred_element_type=F32)
+        return 0
+    lax.fori_loop(0, nb // TOGETHER, step, 0)
     for r in range(rows):
         a = acc[r * lev:(r + 1) * lev, :]
         out_ref[r] = a[:, 0:cols] + a[:, cols:]
 
 
-def scatter(cells, weights, back, rows, cols):
-    n2, lev, _ = back.shape
-    nb = n2 // 2
+def scatter(cells, weights, back, rows, cols, lev):
+    nb = back.shape[0] // 2
     return pl.pallas_call(functools.partial(scatter_kernel, rows, lev, cols, nb),
         out_shape=jax.ShapeDtypeStruct((rows, lev, cols), F32),
         in_specs=[pl.BlockSpec(memory_space=VMEM)] * 3,
         out_specs=pl.BlockSpec(memory_space=VMEM), name="scatter",
-        scratch_shapes=[VMEM((rows * lev, 512), BF16), VMEM((rows * lev, 256), F32)],
-        compiler_params=params(20),
+        scratch_shapes=[VMEM((rows * lev, 512 * TOGETHER), BF16), VMEM((rows * lev, 256), F32)],
+        compiler_params=params(24),
     )(cells, weights, back)
 
 
@@ -494,7 +504,7 @@
         in_specs=[WHOLE] * 3, out_specs=[WHOLE] * 3, name="strip_adjoint", compiler_params=params(12))(own, south_in, north_in)
 
 
-def finish_kernel(groups, levels, rows, margin, tiles_ref, strip_ref, from_west, from_east, faces_ref, u_ref, mask_ref, out_ref, strip_a, strip_b, rim):
+def finish_kernel(groups, levels, rows, margin, tiles_ref, strip_ref, from_west, from_east, faces_ref, u_ref, mask_ref, out_ref, strip_a, strip_b, rim, result, sems):
     quarter = (rows + 2 * margin) // 4
     for slab in range(rim.shape[0]):
         for at in range(0, quarter, 2):
@@ -504,17 +514,22 @@
                 for side in range(2):
                     strip_a[side, slab, here] = pair[side]
     strip_sweeps(rows, margin, (strip_a, strip_b), faces_ref, rim)
-    def step(g, _):
-        put = lanes_of(g)
-        start = group_start(g, levels)
+    def send(g):
+        fresh = LANES8 * g - group_start(g, levels)
+        source = result.at[g, fresh * rows:LANES8 * rows]
+        return pltpu.make_async_copy(source, out_ref.at[LANES8 * g * rows:min(LANES8 * (g + 1), levels) * rows], sems.at[g])
+    live = -(-levels // LANES8)
+    for g in range(live):
+        put = slice(LANES8 * g, LANES8 * (g + 1))
         for at in range(0, rows, LANES8):
             here = slice(at, at + LANES8)
             value = put_rim(tiles_ref[here, put, :], g, groups, margin, lambda slab: rim[slab, here])
             value = u_ref[here, put, :] + mask_ref[here, put, :] * value
             for r in range(LANES8):
-                out_ref[pl.ds(start * rows + at + r, LANES8, stride=rows), :] = value[r]
-        return 0
-    lax.fori_loop(0, groups, step, 0)
+                result[g, pl.ds(at + r, LANES8, stride=rows), :] = value[r]
+        send(g).start()
+    for g in range(live):
+        send(g).wait()
 
 
 def finish(groups, levels, rows, margin, *args):
@@ -522,27 +537,25 @@
     slabs, _ = slabs_of(groups)
     return pl.pallas_call(functools.partial(finish_kernel, groups, levels, rows, margin),
         out_shape=jax.ShapeDtypeStruct((levels * rows, 128), F32),
-        in_specs=[WHOLE] * 7, out_specs=WHOLE, name="finish",
-        scratch_shapes=[VMEM((2, slabs, tall, LANES8, 128), F32)] * 2 + [VMEM((slabs, rows, LANES8, 128), F32)],
+        in_specs=[WHOLE] * 7, out_specs=pl.BlockSpec(memory_space=pltpu.HBM), name="finish",
+        scratch_shapes=[VMEM((2, slabs, tall, LANES8, 128), F32)] * 2 + [VMEM((slabs, rows, LANES8, 128), F32), VMEM((groups, LANES8 * rows, 128), F32), pltpu.SemaphoreType.DMA((groups,))],
         compiler_params=params(20))(*args)
 
 
-def departures_kernel(groups, levels, equivalent_ref, obs_ref, out_ref, back_ref):
+def departures_kernel(levels, equivalent_ref, obs_ref, out_ref):
     def step(p, _):
-        for g in range(groups):
+        for g in range(-(-levels // LANES8)):
             start = group_start(g, levels)
             here = slice(LANES8 * g, LANES8 * (g + 1))
-            gap = obs_ref[p, levels + start:levels + start + LANES8, :] * (equivalent_ref[p, here, :] - obs_ref[p, start:start + LANES8, :])
-            back_ref[p, here, :] = gap
-            out_ref[p, start:start + LANES8, :] = gap
+            out_ref[p, start:start + LANES8, :] = obs_ref[p, levels + start:levels + start + LANES8, :] * (equivalent_ref[p, here, :] - obs_ref[p, start:start + LANES8, :])
         return 0
     lax.fori_loop(0, out_ref.shape[0], step, 0, unroll=2)
 
 
-def departures_of(groups, levels, equivalent, obs):
-    return pl.pallas_call(functools.partial(departures_kernel, groups, levels),
-        out_shape=[jax.ShapeDtypeStruct((equivalent.shape[0], levels, 128), F32), jax.ShapeDtypeStruct(equivalent.shape, F32)],
-        in_specs=[WHOLE] * 2, out_specs=[WHOLE] * 2, name="departures", compiler_params=params(16))(equivalent, obs)
+def departures_of(levels, equivalent, obs):
+    return pl.pallas_call(functools.partial(departures_kernel, levels),
+        out_shape=jax.ShapeDtypeStruct((equivalent.shape[0], levels, 128), F32),
+        in_specs=[WHOLE] * 2, out_specs=WHOLE, name="departures", compiler_params=params(16))(equivalent, obs)
 
 
 def place_kernel(part_ref, out_ref):
@@ -622,9 +635,9 @@
     background = tiles(groups, rows, margin, fields[0], south_in, north_in, e, n)
     rim, strip_faces = forward_strips(groups, rows, margin, strip, from_west, from_east, rims, south_corners, north_corners)
     equivalent = gather(corner_cells, corner_weights, background, rim, slots, margin)
-    out, back = departures_of(groups, levels, equivalent, obs)
+    out = departures_of(levels, equivalent, obs)
     sent = exchange(out, share)
-    adjoint = scatter(corner_cells, corner_weights, back, rows, cols)
+    adjoint = scatter(corner_cells, corner_weights, out, rows, cols, LANES8 * groups)
     south_in, north_in = swap_edges("gy", adjoint[rows - margin:], adjoint[:margin])
     own = strip_own(groups, rows, adjoint)
     strip, to_east, to_west = strip_adjoint(groups, rows, margin, own, south_in, north_in)

time: 166 us -> 164 us (0.988)
  local copies, waits for them, and re-layouts: 7.22 us -> 5.06 us
    unnamed x42 -> x36, local copies, waits for them, and re-layouts: 7.22 us -> 5.06 us
where the time goes in v4:
time: 164 us; the launch traced here: 163 us
  Pallas kernels  67.6 us (41%)
  waiting for transfers between devices  44.2 us (27%)
  starting transfers between devices  42.2 us (26%)
  local copies, waits for them, and re-layouts  5.06 us (3%)
  other arithmetic  3.06 us (2%)
    ppermute x2, waiting for transfers between devices, pass_around(): lax.ppermute(forth, axis, up)  42.3 us
    all_to_all x2, starting transfers between devices, exchange(): values = lax.all_to_all(values, ('gx', 'gy'), 0, 0, tiled=True)  20.2 us
    pallas_call x1, Pallas kernels, scatter(): pl.pallas_call(functools.partial(scatter_kernel, rows, lev, cols, nb), ou...  14.9 us
    pallas_call x1, Pallas kernels, gather(): pl.pallas_call(functools.partial(gather_kernel, rows, lev, cols, nb, marg...  13.3 us
    pallas_call x2, Pallas kernels, tiles(): pl.pallas_call(functools.partial(tiles_kernel, groups, rows, margin), out...  12 us
    ppermute x3, starting transfers between devices, swap_rounds(): lax.ppermute(outer, axis, rounds[1])  10.8 us
    pallas_call x1, Pallas kernels, stage(): pl.pallas_call(functools.partial(stage_kernel, groups, levels, margin), g...  6.39 us
    pallas_call x1, Pallas kernels, edge_sends(): pl.pallas_call(functools.partial(sends_kernel, groups, levels, margin), g...  6.35 us
  transfers between devices with their start and end apart: 12, of which 2 were waited for; matrix products, arithmetic and copies ran while one was open for 1% of the time, Pallas kernels for 35%

profile of v4, /device:TPU:1, one launch (start us, length us, event | category | flops | bytes accessed | tf_op | source)
XLA Modules:
  0.0 163.2 jit_solution(13575352109019203416)
XLA Ops:
  1.4 1.3 copy-done.10
  2.7 1.3 copy-done.11
  4.0 1.9 %obs_blocks.1 = f32[32,152,128]{2,1,0:T(8,128)} custom-call(f32[75,4096]{1,0:T(8,128)S(1)} %copy-done.10, f32[75,4096]{1,0:T(8,128)S(1)} %copy-done.11, s32[1,4096]{1,0:T(1,128)S(1)} %bitcast.8), custom_call_target="tpu_custom_call" | custom-call | tf_op jit(solution)/shard_map/obs_blocks/pallas_call | solution.py:155
  5.9 6.3 %edge_sends.1 = (f32[2,32,8,128]{3,2,1,0:T(8,128)}, f32[2,32,8,128]{3,2,1,0:T(8,128)}, f32[16,80,128]{2,1,0:T(8,128)}, f32[16,80,128]{2,1,0:T(8,128)}) custom-call(s32[1]{0:T(128)} %bitcast.odd_ref, f32[75,32,128]{2,1,0:T(8,128)} %control_ref.3, f32[75,32,128]{2,1,0:T(8,128)} %east_ref.3, f32[75,32,128]{2,1,0:T(8,128)} %north_ref.3, s32[75,32,128]{2,1,0:T(8,128)} %mask_ref.3), custom_call_target="tpu_custom_call" | custom-call | tf_op jit(solution)/shard_map/edge_sends/pallas_call | solution.py:291
  12.3 7.1 %all-to-all-start = ((f32[32,152,128]{2,1,0:T(8,128)}), f32[32,152,128]{2,1,0:T(8,128)S(1)}, u32[]{:S(2)}, u32[]{:S(2)}) async-start(f32[32,152,128]{2,1,0:T(8,128)} %obs_blocks.1), calls=%async_computation | async-start | bytes 4980736 | tf_op jit(solution)/shard_map/all_to_all | solution.py:580
  19.4 1.4 collective-permute-start.2
  20.8 2.8 %collective-permute-start.3 = (f32[2,32,8,128]{3,2,1,0:T(8,128)S(1)}, f32[2,32,8,128]{3,2,1,0:T(8,128)S(1)}, u32[]{:S(2)}, u32[]{:S(2)}) collective-permute-start(f32[2,32,8,128]{3,2,1,0:T(8,128)S(1)} %copy-done.16), channel_id=1, source_target_pairs={{4,0},{8,4},{12,8},{16,12},{20,16},{24,20},{28,24},{0,28},{5,1},{9... | collective-permute-start | bytes 786440 | tf_op jit(solution)/shard_map/ppermute | solution.py:589
  23.6 0.8 collective-permute-start
  24.4 3.3 %collective-permute-start.1 = (f32[16,80,128]{2,1,0:T(8,128)}, f32[16,80,128]{2,1,0:T(8,128)}, u32[]{:S(2)}, u32[]{:S(2)}) collective-permute-start(f32[16,80,128]{2,1,0:T(8,128)} %get-tuple-element.21), channel_id=1, source_target_pairs={{1,2},{2,1},{5,6},{6,5},{9,10},{10,9},{13,14},{14,13},{17,18},{18,... | collective-permute-start | bytes 1966088 | tf_op jit(solution)/shard_map/ppermute | solution.py:595
  27.7 42.3 %collective-permute-done.2.from_west = f32[2,32,8,128]{3,2,1,0:T(8,128)S(1)} collective-permute-done((f32[2,32,8,128]{3,2,1,0:T(8,128)S(1)}, f32[2,32,8,128]{3,2,1,0:T(8,128)S(1)}, u32[]{:S(2)}, u32[]{:S(2)}) %collective-permute-start.2) | collective-permute-done | bytes 262176 | tf_op jit(solution)/shard_map/ppermute | solution.py:589
  70.1 1.0 collective-permute-start.4
  71.1 3.8 %collective-permute-start.5 = (f32[2,2,4,8,128]{4,3,2,1,0:T(8,128)S(1)}, f32[2,2,4,8,128]{4,3,2,1,0:T(8,128)S(1)}, u32[]{:S(2)}, u32[]{:S(2)}) collective-permute-start(f32[2,2,4,8,128]{4,3,2,1,0:T(8,128)S(1)} %get-tuple-element.36), channel_id=1, source_target_pairs={{1,2},{2,1},{5,6},{6,5},{9,10},{10,9},{13,14},{14,13},{17,18},{18,... | collective-permute-start | bytes 196616 | tf_op jit(solution)/shard_map/ppermute | solution.py:595
  75.0 6.4 %stage.1 = (f32[32,80,128]{2,1,0:T(8,128)S(1)}, f32[32,80,128]{2,1,0:T(8,128)S(1)}, f32[32,80,128]{2,1,0:T(8,128)S(1)}, f32[32,80,128]{2,1,0:T(8,128)S(1)}, f32[4,2,2,32,8,128]{5,4,3,2,1,0:T(8,128)S(1)}) custom-call(f32[75,32,128]{2,1,0:T(8,128)} %control_ref.3, f32[75,32,128]{2,1,0:T(8,128)} %east_ref.3, f32[75,32,128]{2,1,0:T(8,128)} %north_ref.3, ...), custom_call_target="tpu_custom_call" | custom-call | tf_op jit(solution)/shard_map/stage/pallas_call | solution.py:240
  81.4 2.2 %broadcast_select_fusion = (f32[16,80,128]{2,1,0:T(8,128)S(1)}, f32[16,80,128]{2,1,0:T(8,128)S(1)}) fusion(f32[16,80,128]{2,1,0:T(8,128)} %collective-permute-done.1, f32[16,80,128]{2,1,0:T(8,128)} %collective-permute-done, pred[]{:T(512)S(6)} %eq.14), kind=kLoop, calls=%fused_computation | loop fusion | flops 327680 | bytes 2621441 | tf_op jit(solution)/shard_map/jit(_where)/select_n | solution.py:596
  83.7 0.7 strip_rims.1.rims_ref
  84.5 1.1 faces.1
  85.6 2.6 %forward_strips.1 = (f32[2,32,8,128]{3,2,1,0:T(8,128)S(1)}, f32[2,2,2,40,8,128]{5,4,3,2,1,0:T(8,128)S(1)}) custom-call(f32[4,2,2,32,8,128]{5,4,3,2,1,0:T(8,128)S(1)} %get-tuple-element.27.strip_ref, f32[2,32,8,128]{3,2,1,0:T(8,128)S(1)} %collective-permute-done.2.from_west, f32[2,32,8,128]{3,2,1,0:T(8,128)S(1)} %collective-permute-done.3.from_east, ...), custom_call_target="tpu_custom_call" | custom-call | tf_op jit(solution)/shard_map/forward_strips/pallas_call | solution.py:457
  88.3 6.0 %tiles.2.bg_ref = f32[32,80,128]{2,1,0:T(8,128)S(1)} custom-call(f32[32,80,128]{2,1,0:T(8,128)S(1)} %get-tuple-element.19.u_ref, f32[16,80,128]{2,1,0:T(8,128)S(1)} %get-tuple-element.42.south_in, f32[16,80,128]{2,1,0:T(8,128)S(1)} %get-tuple-element.41.north_in, f32[40,80,128]{2,1,0:T(8,128)S(1)} %get-tuple-element.25.e_ref, ...), custom_call_target="tpu_custom_call" | custom-call | flops 13107200 | bytes 6553600 | tf_op jit(solution)/shard_map/tiles/pallas_call | solution.py:410
  94.3 13.3 %gather.1.equivalent_ref = f32[32,80,128]{2,1,0:T(8,128)S(1)} custom-call(s32[4,4096]{1,0:T(4,128)S(1)} %copy-done.14, f32[4,4096]{1,0:T(4,128)S(1)} %copy-done.15, f32[32,80,128]{2,1,0:T(8,128)S(1)} %tiles.2.bg_ref, f32[2,32,8,128]{3,2,1,0:T(8,128)S(1)} %get-tuple-element.30.rim_ref), custom_call_target="tpu_custom_call" | custom-call | tf_op jit(solution)/shard_map/gather/pallas_call | solution.py:72
  107.6 1.0 copy-done.8
  108.7 1.3 copy-done.9
  110.0 1.3 departures.1.back_ref
  111.3 13.1 %all-to-all-start.1 = ((f32[32,75,128]{2,1,0:T(8,128)}), f32[32,75,128]{2,1,0:T(8,128)S(1)}, u32[]{:S(2)}, u32[]{:S(2)}) async-start(f32[32,75,128]{2,1,0:T(8,128)} %departures.1.back_ref), calls=%async_computation.1 | async-start | bytes 2621440 | tf_op jit(solution)/shard_map/all_to_all | solution.py:580
  124.5 14.9 %scatter.1.u_ref.adjoint_ref = f32[32,80,128]{2,1,0:T(8,128)S(1)} custom-call(s32[4,4096]{1,0:T(4,128)S(1)} %copy-done.14, f32[4,4096]{1,0:T(4,128)S(1)} %copy-done.15, f32[32,75,128]{2,1,0:T(8,128)} %departures.1.back_ref), custom_call_target="tpu_custom_call" | custom-call | tf_op jit(solution)/shard_map/scatter/pallas_call | solution.py:121
  139.7 3.6 %collective-permute-start.7 = (f32[4,80,128]{2,1,0:T(8,128)S(1)}, f32[4,80,128]{2,1,0:T(8,128)S(1)}, u32[]{:S(2)}, u32[]{:S(2)}) collective-permute-start(f32[4,80,128]{2,1,0:T(8,128)S(1)} %get-tuple-element.39), channel_id=1, source_target_pairs={{1,2},{2,1},{5,6},{6,5},{9,10},{10,9},{13,14},{14,13},{17,18},{18,... | collective-permute-start | bytes 491528 | tf_op jit(solution)/shard_map/ppermute | solution.py:595
  143.4 1.8 %strip_own.1.own_ref = f32[2,2,32,8,128]{4,3,2,1,0:T(8,128)S(1)} custom-call(f32[32,80,128]{2,1,0:T(8,128)S(1)} %scatter.1.u_ref.adjoint_ref), custom_call_target="tpu_custom_call" | custom-call | tf_op jit(solution)/shard_map/strip_own/pallas_call | solution.py:477
  145.2 1.8 %collective-permute-done.7 = f32[4,80,128]{2,1,0:T(8,128)S(1)} collective-permute-done((f32[4,80,128]{2,1,0:T(8,128)S(1)}, f32[4,80,128]{2,1,0:T(8,128)S(1)}, u32[]{:S(2)}, u32[]{:S(2)}) %collective-permute-start.7) | collective-permute-done | bytes 163872 | tf_op jit(solution)/shard_map/ppermute | solution.py:595
  147.4 1.5 collective-permute-start.8
  148.9 3.4 %collective-permute-start.9 = (f32[2,10,8,128]{3,2,1,0:T(8,128)S(1)}, f32[2,10,8,128]{3,2,1,0:T(8,128)S(1)}, u32[]{:S(2)}, u32[]{:S(2)}) collective-permute-start(f32[2,10,8,128]{3,2,1,0:T(8,128)S(1)} %get-tuple-element.34), channel_id=1, source_target_pairs={{4,0},{8,4},{12,8},{16,12},{20,16},{24,20},{28,24},{0,28},{5,1},{9... | collective-permute-start | bytes 245768 | tf_op jit(solution)/shard_map/ppermute | solution.py:589
  152.3 6.0 %tiles.3.tiles_ref = f32[32,80,128]{2,1,0:T(8,128)S(1)} custom-call(f32[32,80,128]{2,1,0:T(8,128)S(1)} %scatter.1.u_ref.adjoint_ref, f32[4,80,128]{2,1,0:T(8,128)S(1)} %get-tuple-element.44.south_in, f32[4,80,128]{2,1,0:T(8,128)S(1)} %get-tuple-element.43.north_in, f32[40,80,128]{2,1,0:T(8,128)S(1)} %copy-done.1, f32[40,80,128]{2,1,0:T(8,128)S(1)} %copy-done.3), custom_call_target="tpu_custom_call" | custom-call | flops 13107200 | bytes 6553600 | tf_op jit(solution)/shard_map/tiles/pallas_call | solution.py:410
  158.3 3.6 %finish.1 = f32[2400,128]{1,0:T(8,128)} custom-call(f32[32,80,128]{2,1,0:T(8,128)S(1)} %tiles.3.tiles_ref, f32[2,2,40,8,128]{4,3,2,1,0:T(8,128)S(1)} %get-tuple-element.32.strip_ref, f32[2,10,8,128]{3,2,1,0:T(8,128)S(1)} %collective-permute-done.8.from_west, f32[2,10,8,128]{3,2,1,0:T(8,128)S(1)} %collective-permute-done.9.from_east, ...), custom_call_target="tpu_custom_call" | custom-call | tf_op jit(solution)/shard_map/finish/pallas_call | solution.py:538
  162.0 1.2 place_departures.1
  (50 shorter events, 1.6 us)
Async XLA Ops:
  1.4 1.3 copy-start.10
  2.7 1.3 copy-start.11
  12.3 7.1 %copy-start.17 = (f32[2,32,8,128]{3,2,1,0:T(8,128)S(1)}, f32[2,32,8,128]{3,2,1,0:T(8,128)}, u32[]{:S(2)}) copy-start(f32[2,32,8,128]{3,2,1,0:T(8,128)} %get-tuple-element.28) | copy-start | bytes 786436
  12.3 8.5 %copy-start.16 = (f32[2,32,8,128]{3,2,1,0:T(8,128)S(1)}, f32[2,32,8,128]{3,2,1,0:T(8,128)}, u32[]{:S(2)}) copy-start(f32[2,32,8,128]{3,2,1,0:T(8,128)} %get-tuple-element.29) | copy-start | bytes 786436
  12.3 96.4 %all-to-all-start = ((f32[32,152,128]{2,1,0:T(8,128)}), f32[32,152,128]{2,1,0:T(8,128)S(1)}, u32[]{:S(2)}, u32[]{:S(2)}) async-start(f32[32,152,128]{2,1,0:T(8,128)} %obs_blocks.1), calls=%async_computation | async-start | bytes 4980736 | tf_op jit(solution)/shard_map/all_to_all | solution.py:580
  19.4 50.7 %collective-permute-start.2 = (f32[2,32,8,128]{3,2,1,0:T(8,128)S(1)}, f32[2,32,8,128]{3,2,1,0:T(8,128)S(1)}, u32[]{:S(2)}, u32[]{:S(2)}) collective-permute-start(f32[2,32,8,128]{3,2,1,0:T(8,128)S(1)} %copy-done.17), channel_id=1, source_target_pairs={{0,4},{4,8},{8,12},{12,16},{16,20},{20,24},{24,28},{28,0},{1,5},{5... | collective-permute-start | bytes 786440 | tf_op jit(solution)/shard_map/ppermute | solution.py:589
  20.8 49.3 %collective-permute-start.3 = (f32[2,32,8,128]{3,2,1,0:T(8,128)S(1)}, f32[2,32,8,128]{3,2,1,0:T(8,128)S(1)}, u32[]{:S(2)}, u32[]{:S(2)}) collective-permute-start(f32[2,32,8,128]{3,2,1,0:T(8,128)S(1)} %copy-done.16), channel_id=1, source_target_pairs={{4,0},{8,4},{12,8},{16,12},{20,16},{24,20},{28,24},{0,28},{5,1},{9... | collective-permute-start | bytes 786440 | tf_op jit(solution)/shard_map/ppermute | solution.py:589
  23.6 57.8 %collective-permute-start = (f32[16,80,128]{2,1,0:T(8,128)}, f32[16,80,128]{2,1,0:T(8,128)}, u32[]{:S(2)}, u32[]{:S(2)}) collective-permute-start(f32[16,80,128]{2,1,0:T(8,128)} %get-tuple-element.20), channel_id=1, source_target_pairs={{0,1},{1,0},{2,3},{3,2},{4,5},{5,4},{6,7},{7,6},{8,9},{9,8},{10,11... | collective-permute-start | bytes 1966088 | tf_op jit(solution)/shard_map/ppermute | solution.py:595
  24.4 57.0 %collective-permute-start.1 = (f32[16,80,128]{2,1,0:T(8,128)}, f32[16,80,128]{2,1,0:T(8,128)}, u32[]{:S(2)}, u32[]{:S(2)}) collective-permute-start(f32[16,80,128]{2,1,0:T(8,128)} %get-tuple-element.21), channel_id=1, source_target_pairs={{1,2},{2,1},{5,6},{6,5},{9,10},{10,9},{13,14},{14,13},{17,18},{18,... | collective-permute-start | bytes 1966088 | tf_op jit(solution)/shard_map/ppermute | solution.py:595
  70.1 11.3 %collective-permute-start.4 = (f32[2,2,4,8,128]{4,3,2,1,0:T(8,128)S(1)}, f32[2,2,4,8,128]{4,3,2,1,0:T(8,128)S(1)}, u32[]{:S(2)}, u32[]{:S(2)}) collective-permute-start(f32[2,2,4,8,128]{4,3,2,1,0:T(8,128)S(1)} %broadcast_select_fusion.7), channel_id=1, source_target_pairs={{0,1},{1,0},{2,3},{3,2},{4,5},{5,4},{6,7},{7,6},{8,9},{9,8},{10,11... | collective-permute-start | bytes 196616 | tf_op jit(solution)/shard_map/ppermute | solution.py:595
  71.1 10.3 %collective-permute-start.5 = (f32[2,2,4,8,128]{4,3,2,1,0:T(8,128)S(1)}, f32[2,2,4,8,128]{4,3,2,1,0:T(8,128)S(1)}, u32[]{:S(2)}, u32[]{:S(2)}) collective-permute-start(f32[2,2,4,8,128]{4,3,2,1,0:T(8,128)S(1)} %get-tuple-element.36), channel_id=1, source_target_pairs={{1,2},{2,1},{5,6},{6,5},{9,10},{10,9},{13,14},{14,13},{17,18},{18,... | collective-permute-start | bytes 196616 | tf_op jit(solution)/shard_map/ppermute | solution.py:595
  81.4 3.1 %copy-start.6 = (f32[32,80,128]{2,1,0:T(8,128)}, f32[32,80,128]{2,1,0:T(8,128)S(1)}, u32[]{:S(2)}) copy-start(f32[32,80,128]{2,1,0:T(8,128)S(1)} %get-tuple-element.22.mask_ref) | copy-start | bytes 3932164
  81.4 6.8 %copy-start.4 = (f32[32,80,128]{2,1,0:T(8,128)}, f32[32,80,128]{2,1,0:T(8,128)S(1)}, u32[]{:S(2)}) copy-start(f32[32,80,128]{2,1,0:T(8,128)S(1)} %get-tuple-element.19.u_ref) | copy-start | bytes 3932164
  85.6 2.6 %copy-start = (f32[40,80,128]{2,1,0:T(8,128)}, f32[40,80,128]{2,1,0:T(8,128)S(1)}, u32[]{:S(2)}) copy-start(f32[40,80,128]{2,1,0:T(8,128)S(1)} %get-tuple-element.25.e_ref) | copy-start | bytes 4915204
  85.6 2.6 %copy-start.2 = (f32[40,80,128]{2,1,0:T(8,128)}, f32[40,80,128]{2,1,0:T(8,128)S(1)}, u32[]{:S(2)}) copy-start(f32[40,80,128]{2,1,0:T(8,128)S(1)} %get-tuple-element.26.n_ref) | copy-start | bytes 4915204
  88.2 6.1 %copy-start.12 = (f32[2,2,2,40,8,128]{5,4,3,2,1,0:T(8,128)}, f32[2,2,2,40,8,128]{5,4,3,2,1,0:T(8,128)S(1)}, u32[]{:S(2)}) copy-start(f32[2,2,2,40,8,128]{5,4,3,2,1,0:T(8,128)S(1)} %get-tuple-element.35.faces_ref) | copy-start | bytes 3932164
  88.2 6.0 %copy-start.14 = (s32[4,4096]{1,0:T(4,128)S(1)}, s32[4,4096]{1,0:T(4,128)}, u32[]{:S(2)}) copy-start(s32[4,4096]{1,0:T(4,128)} %cells_ref.3) | copy-start | bytes 196612
  88.2 6.0 %copy-start.15 = (f32[4,4096]{1,0:T(4,128)S(1)}, f32[4,4096]{1,0:T(4,128)}, u32[]{:S(2)}) copy-start(f32[4,4096]{1,0:T(4,128)} %weights_ref.3) | copy-start | bytes 196612
  107.6 1.1 copy-start.8
  108.7 1.3 copy-start.9
  111.3 50.7 %all-to-all-start.1 = ((f32[32,75,128]{2,1,0:T(8,128)}), f32[32,75,128]{2,1,0:T(8,128)S(1)}, u32[]{:S(2)}, u32[]{:S(2)}) async-start(f32[32,75,128]{2,1,0:T(8,128)} %departures.1.back_ref), calls=%async_computation.1 | async-start | bytes 2621440 | tf_op jit(solution)/shard_map/all_to_all | solution.py:580
  139.4 5.8 %collective-permute-start.6 = (f32[4,80,128]{2,1,0:T(8,128)S(1)}, f32[4,80,128]{2,1,0:T(8,128)S(1)}, u32[]{:S(2)}, u32[]{:S(2)}) collective-permute-start(f32[4,80,128]{2,1,0:T(8,128)S(1)} %get-tuple-element.40), channel_id=1, source_target_pairs={{0,1},{1,0},{2,3},{3,2},{4,5},{5,4},{6,7},{7,6},{8,9},{9,8},{10,11... | collective-permute-start | bytes 491528 | tf_op jit(solution)/shard_map/ppermute | solution.py:595
  139.7 12.6 %copy-start.1 = (f32[40,80,128]{2,1,0:T(8,128)S(1)}, f32[40,80,128]{2,1,0:T(8,128)}, u32[]{:S(2)}) copy-start(f32[40,80,128]{2,1,0:T(8,128)} %copy-done) | copy-start | bytes 4915204
  139.7 12.6 %copy-start.3 = (f32[40,80,128]{2,1,0:T(8,128)S(1)}, f32[40,80,128]{2,1,0:T(8,128)}, u32[]{:S(2)}) copy-start(f32[40,80,128]{2,1,0:T(8,128)} %copy-done.2) | copy-start | bytes 4915204
  139.7 7.2 %collective-permute-start.7 = (f32[4,80,128]{2,1,0:T(8,128)S(1)}, f32[4,80,128]{2,1,0:T(8,128)S(1)}, u32[]{:S(2)}, u32[]{:S(2)}) collective-permute-start(f32[4,80,128]{2,1,0:T(8,128)S(1)} %get-tuple-element.39), channel_id=1, source_target_pairs={{1,2},{2,1},{5,6},{6,5},{9,10},{10,9},{13,14},{14,13},{17,18},{18,... | collective-permute-start | bytes 491528 | tf_op jit(solution)/shard_map/ppermute | solution.py:595
  147.4 10.9 %collective-permute-start.8 = (f32[2,10,8,128]{3,2,1,0:T(8,128)S(1)}, f32[2,10,8,128]{3,2,1,0:T(8,128)S(1)}, u32[]{:S(2)}, u32[]{:S(2)}) collective-permute-start(f32[2,10,8,128]{3,2,1,0:T(8,128)S(1)} %get-tuple-element.33), channel_id=1, source_target_pairs={{0,4},{4,8},{8,12},{12,16},{16,20},{20,24},{24,28},{28,0},{1,5},{5... | collective-permute-start | bytes 245768 | tf_op jit(solution)/shard_map/ppermute | solution.py:589
  148.9 9.4 %copy-start.5 = (f32[32,80,128]{2,1,0:T(8,128)S(1)}, f32[32,80,128]{2,1,0:T(8,128)}, u32[]{:S(2)}) copy-start(f32[32,80,128]{2,1,0:T(8,128)} %copy-done.4) | copy-start | bytes 3932164
  148.9 9.4 %copy-start.7 = (f32[32,80,128]{2,1,0:T(8,128)S(1)}, f32[32,80,128]{2,1,0:T(8,128)}, u32[]{:S(2)}) copy-start(f32[32,80,128]{2,1,0:T(8,128)} %copy-done.6) | copy-start | bytes 3932164
  148.9 9.4 %copy-start.13 = (f32[2,2,2,40,8,128]{5,4,3,2,1,0:T(8,128)S(1)}, f32[2,2,2,40,8,128]{5,4,3,2,1,0:T(8,128)}, u32[]{:S(2)}) copy-start(f32[2,2,2,40,8,128]{5,4,3,2,1,0:T(8,128)} %copy-done.12) | copy-start | bytes 3932164
  148.9 9.4 %collective-permute-start.9 = (f32[2,10,8,128]{3,2,1,0:T(8,128)S(1)}, f32[2,10,8,128]{3,2,1,0:T(8,128)S(1)}, u32[]{:S(2)}, u32[]{:S(2)}) collective-permute-start(f32[2,10,8,128]{3,2,1,0:T(8,128)S(1)} %get-tuple-element.34), channel_id=1, source_target_pairs={{4,0},{8,4},{12,8},{16,12},{20,16},{24,20},{28,24},{0,28},{5,1},{9... | collective-permute-start | bytes 245768 | tf_op jit(solution)/shard_map/ppermute | solution.py:589
